TPU v7x, 32 devices: a whole 2x2x4 slice. The times are simulated.
32 devices in a mesh: expert: 4 (over y, core), replica: 2 (over x), seq: 4 (over z).
Axes of the slice: x: 2, y: 2, z: 4, core: 2. Of those that a mesh axis runs over, the one named last changes fastest.
Arguments:
- tokens: bfloat16 [1536, 3584], P(('expert', 'replica'), 'seq'), may hold values from -6 to 6
- cotangent: bfloat16 [1536, 3584], P(('expert', 'replica'), 'seq'), may hold values from -6 to 6
- route_weight: float32 [1536], P(('expert', 'replica')), may hold values from 0.1 to 1
- expert_ids: int32 [1536, 1], P(('expert', 'replica')), may hold values from 0 to 3; in each aligned block of 192 rows (0 to 191, 192 to 383, ...) at most 72 rows name the same one
- gate_weight: bfloat16 [4, 3584, 1024], P('expert', 'seq', 'replica'), may hold values from -0.09375 to 0.09375
- up_weight: bfloat16 [4, 3584, 1024], P('expert', 'seq', 'replica'), may hold values from -0.09375 to 0.09375
- down_weight: bfloat16 [4, 1024, 3584], P('expert', 'replica', 'seq'), may hold values from -0.1875 to 0.1875
Outputs:
- token_grad: bfloat16 [1536, 3584], P(('expert', 'replica'), 'seq')
- gate_grad: bfloat16 [4, 3584, 1024], P('expert', 'seq', 'replica')
- up_grad: bfloat16 [4, 3584, 1024], P('expert', 'seq', 'replica')
- down_grad: bfloat16 [4, 1024, 3584], P('expert', 'replica', 'seq')
Inputs may be any that keep to these rules, and one draw needn't show every extreme that they name: `expert_ids`: among the 192 tokens of one block (the tokens of one device) no expert is named more than 72 times, a bound that some block reaches.
All inputs are finite; a program needn't handle non-finite values.
Results may differ from a plain program's by a relative error of at most 0.02.
Values may be sent and summed in bfloat16 or wider, within the bound.
No kernel may reach another device: no remote copies, remote signals or barrier semaphores. Data moves between devices by JAX's collectives and lax.ppermute only.
A program may use at most 64 MiB of HBM per device.

v0:
```python
import jax
import jax.numpy as jnp
from jax import lax
from jax.sharding import PartitionSpec as P


def matmul_last(left, right):
    return lax.dot_general(
        left, right, (((1,), (1,)), ((), ())), preferred_element_type=jnp.float32
    )


def matmul_first(left, right):
    return lax.dot_general(
        left, right, (((0,), (0,)), ((), ())), preferred_element_type=jnp.float32
    )


def local(tokens, cotangent, route_weight, expert_ids, gate_weight, up_weight, down_weight):
    n_expert = lax.axis_size("expert")
    count = tokens.shape[0]
    quarter = tokens.shape[1]
    capacity = 3 * count // (2 * n_expert)
    chosen = expert_ids[:, 0]
    onehot = (chosen[:, None] == jnp.arange(n_expert, dtype=jnp.int32)[None, :]).astype(jnp.int32)
    before = jnp.cumsum(onehot, axis=0) - onehot
    within = jnp.sum(before * onehot, axis=1)
    target = chosen * capacity + within
    table = (
        jnp.full((n_expert * capacity,), count, jnp.int32)
        .at[target]
        .set(jnp.arange(count, dtype=jnp.int32))
    )
    blank = jnp.zeros((1, quarter), jnp.bfloat16)
    padded_x = jnp.concatenate([tokens, blank], axis=0)
    scaled = (route_weight[:, None] * cotangent.astype(jnp.float32)).astype(jnp.bfloat16)
    padded_g = jnp.concatenate([scaled, blank], axis=0)
    send_x = padded_x[table].reshape(n_expert, capacity, quarter)
    send_g = padded_g[table].reshape(n_expert, capacity, quarter)
    recv_x = lax.all_to_all(send_x, "expert", split_axis=0, concat_axis=0, tiled=True)
    rows_x = recv_x.reshape(-1, quarter)
    full_gate, full_up, full_down = (
        lax.all_gather(gate_weight, "replica", axis=2, tiled=True),
        lax.all_gather(up_weight, "replica", axis=2, tiled=True),
        lax.all_gather(down_weight, "replica", axis=1, tiled=True),
    )
    w_gate = full_gate[0]
    w_up = full_up[0]
    w_down = full_down[0]
    part_gate = jnp.dot(rows_x, w_gate, preferred_element_type=jnp.float32)
    part_up = jnp.dot(rows_x, w_up, preferred_element_type=jnp.float32)
    gate, upper = (
        lax.psum(part_gate.astype(jnp.bfloat16), "seq").astype(jnp.float32),
        lax.psum(part_up.astype(jnp.bfloat16), "seq").astype(jnp.float32),
    )
    sigma = jax.nn.sigmoid(gate)
    active = gate * sigma
    hidden = (active * upper).astype(jnp.bfloat16)
    recv_g = lax.all_to_all(send_g, "expert", split_axis=0, concat_axis=0, tiled=True)
    rows_g = recv_g.reshape(-1, quarter)
    part_dh = matmul_last(rows_g, w_down)
    hgrad = lax.psum(part_dh.astype(jnp.bfloat16), "seq").astype(jnp.float32)
    gate_delta = (hgrad * upper * sigma * (1.0 + gate * (1.0 - sigma))).astype(jnp.bfloat16)
    up_delta = (hgrad * active).astype(jnp.bfloat16)
    out_rows = (matmul_last(gate_delta, w_gate) + matmul_last(up_delta, w_up)).astype(jnp.bfloat16)
    returned = lax.all_to_all(
        out_rows.reshape(n_expert, capacity, quarter),
        "expert",
        split_axis=0,
        concat_axis=0,
        tiled=True,
    )
    returned = returned.reshape(-1, quarter)
    token_grad = (route_weight[:, None] * returned[target].astype(jnp.float32)).astype(jnp.bfloat16)
    grad_gate = matmul_first(rows_x, gate_delta).astype(jnp.bfloat16)[None]
    grad_up = matmul_first(rows_x, up_delta).astype(jnp.bfloat16)[None]
    grad_down = matmul_first(hidden, rows_g).astype(jnp.bfloat16)[None]
    pieces_gate, pieces_up = (
        lax.all_to_all(grad_gate, "replica", split_axis=2, concat_axis=0, tiled=True),
        lax.all_to_all(grad_up, "replica", split_axis=2, concat_axis=0, tiled=True),
    )
    pieces_down = lax.all_to_all(grad_down, "replica", split_axis=1, concat_axis=0, tiled=True)
    gate_grad = jnp.sum(pieces_gate.astype(jnp.float32), axis=0, keepdims=True).astype(jnp.bfloat16)
    up_grad = jnp.sum(pieces_up.astype(jnp.float32), axis=0, keepdims=True).astype(jnp.bfloat16)
    down_grad = jnp.sum(pieces_down.astype(jnp.float32), axis=0, keepdims=True).astype(jnp.bfloat16)
    return (token_grad, gate_grad, up_grad, down_grad)


def solution(mesh):
    placed = (
        P(("expert", "replica"), "seq"),
        P(("expert", "replica"), "seq"),
        P(("expert", "replica")),
        P(("expert", "replica"), None),
        P("expert", "seq", "replica"),
        P("expert", "seq", "replica"),
        P("expert", "replica", "seq"),
    )
    return jax.shard_map(
        local,
        mesh=mesh,
        in_specs=placed,
        out_specs=(
            P(("expert", "replica"), "seq"),
            P("expert", "seq", "replica"),
            P("expert", "seq", "replica"),
            P("expert", "replica", "seq"),
        ),
        check_vma=False,
    )
```

profile of v0, /device:TPU:0, one launch (start us, length us, event | category | flops | bytes accessed | tf_op | source)
XLA Modules:
  0.0 313.1 jit_solution(9565606176509443783)
XLA Ops:
  7.2 0.7 all-gather.6.cloned.1.call-update
  8.0 0.7 all-gather.8.cloned.1.call-update
  9.5 1.2 reduce-window.6
  11.2 1.2 scatter_custom_fusion
  12.4 2.6 gather_fusion.1
  15.0 4.4 %all-to-all-start.1 = ((bf16[4,72,896]{2,1,0:T(8,128)(2,1)}), bf16[4,72,896]{2,1,0:T(8,128)(2,1)S(1)}, u32[]{:S(2)}, u32[]{:S(2)}) async-start(bf16[4,72,896]{2,1,0:T(8,128)(2,1)} %bitcast.8), calls=%async_computation.1 | async-start | bytes 1032192 | tf_op jit(solution)/shard_map/all_to_all | solution.py:40
  19.6 2.6 gather_fusion
  22.2 6.0 %all-to-all-done.1 = bf16[4,72,896]{2,1,0:T(8,128)(2,1)S(1)} async-done(((bf16[4,72,896]{2,1,0:T(8,128)(2,1)}), bf16[4,72,896]{2,1,0:T(8,128)(2,1)S(1)}, u32[]{:S(2)}, u32[]{:S(2)}) %all-to-all-start.1) | async-done | bytes 516128 | tf_op jit(solution)/shard_map/all_to_all | solution.py:40
  28.1 3.5 %all-to-all-start = ((bf16[4,72,896]{2,1,0:T(8,128)(2,1)}), bf16[4,72,896]{2,1,0:T(8,128)(2,1)S(1)}, u32[]{:S(2)}, u32[]{:S(2)}) async-start(bf16[4,72,896]{2,1,0:T(8,128)(2,1)} %bitcast.5), calls=%async_computation | async-start | bytes 1032192 | tf_op jit(solution)/shard_map/all_to_all | solution.py:59
  31.7 10.8 %all-gather.6.cloned.1.call-done = bf16[1,896,1024]{2,1,0:T(8,128)(2,1)} async-done(((bf16[1,896,512]{2,1,0:T(8,128)(2,1)}), bf16[1,896,1024]{2,1,0:T(8,128)(2,1)}) %all-gather.6.cloned.1.call-update) | async-done | bytes 1835024 | tf_op jit(solution)/shard_map/all_gather | solution.py:44
  42.4 3.1 fusion.16
  45.5 28.6 %all-gather.8.cloned.1.call-done = bf16[1,896,1024]{2,1,0:T(8,128)(2,1)} async-done(((bf16[1,896,512]{2,1,0:T(8,128)(2,1)}), bf16[1,896,1024]{2,1,0:T(8,128)(2,1)}) %all-gather.8.cloned.1.call-update) | async-done | bytes 1835024 | tf_op jit(solution)/shard_map/all_gather | solution.py:43
  74.1 3.1 fusion.19
  77.2 28.6 %all-gather.4.cloned.1.call-done = bf16[1,1024,896]{2,1,0:T(8,128)(2,1)} async-done(((bf16[1,512,896]{2,1,0:T(8,128)(2,1)}), bf16[1,1024,896]{2,1,0:T(8,128)(2,1)}) %all-gather.4.cloned.1.call-update) | async-done | bytes 1835024 | tf_op jit(solution)/shard_map/all_gather | solution.py:45
  105.9 3.3 %fusion.13 = bf16[288,1024]{1,0:T(8,128)(2,1)} fusion(bf16[288,896]{1,0:T(8,128)(2,1)S(1)} %bitcast.80, bf16[1,1024,896]{2,1,0:T(8,128)(2,1)} %all-gather.4.cloned.1.call-done), kind=kOutput, calls=%fused_computation.24 | convolution fusion | flops 528777216 | bytes 2940928 | tf_op jit(solution)/shard_map/dot_general | solution.py:8
  109.2 75.7 %all-reduce.6.cloned.1.call-done = (bf16[288,1024]{1,0:T(8,128)(2,1)}, bf16[288,1024]{1,0:T(8,128)(2,1)}, bf16[288,1024]{1,0:T(8,128)(2,1)}) async-done(((bf16[288,1024]{1,0:T(8,128)(2,1)}, bf16[288,1024]{1,0:T(8,128)(2,1)}, bf16[288,1024]{1,0:T(8,128)(2,1)}), (bf16[288,1024]{1,0:T(8,128)(2,1)}, bf16[288,1024]{1,0:T(8,128)(2,1)}, bf16[288,1024]{1,0:T(8,128)(2,1)})) %all-reduce.6.cloned.1.call-update) | async-done | bytes 1769488 | tf_op jit(solution)/shard_map/psum | solution.py:54
  184.9 2.6 fusion
  187.6 1.7 fusion.22
  189.3 3.5 %all-to-all-start.2 = ((bf16[4,72,896]{2,1,0:T(8,128)(2,1)}), bf16[4,72,896]{2,1,0:T(8,128)(2,1)S(1)}, u32[]{:S(2)}, u32[]{:S(2)}) async-start(bf16[4,72,896]{2,1,0:T(8,128)(2,1)} %bitcast.12), calls=%async_computation.2 | async-start | bytes 1032192 | tf_op jit(solution)/shard_map/all_to_all | solution.py:66
  192.8 2.8 convert_bitcast_fusion.2
  195.5 6.6 %copy.25 = bf16[1,896,1024]{1,0,2:T(2,128)(2,1)} copy(bf16[1,896,1024]{2,1,0:T(8,128)(2,1)S(1)} %convert_bitcast_fusion.2) | data formatting | bytes 3670016 | tf_op jit(solution)/shard_map/broadcast_in_dim | solution.py:75
  202.7 12.1 %reduce.9 = bf16[1024,896]{1,0:T(8,128)(2,1)S(1)} reduce(bf16[1024,1,896]{2,1,0:T(2,128)(2,1)} %bitcast.68, bf16[]{:T(256)} %broadcast.68), dimensions={1}, to_apply=%bitcast.51.reduce_sub_computation | reduce | bytes 3670018
  214.8 1.5 reshape.120
  216.3 4.9 %all-to-all-start.3 = ((bf16[2,2,229376]{2,1,0:T(2,128)(2,1)}), bf16[2,2,229376]{2,1,0:T(2,128)(2,1)}, u32[]{:S(2)}, u32[]{:S(2)}) async-start(bf16[2,2,229376]{2,1,0:T(2,128)(2,1)} %reshape.120), calls=%async_computation.3 | async-start | bytes 3670016 | tf_op jit(solution)/shard_map/all_to_all | solution.py:79
  221.2 2.5 convert_bitcast_fusion.1
  223.7 6.6 %copy.26 = bf16[1,896,1024]{1,0,2:T(2,128)(2,1)} copy(bf16[1,896,1024]{2,1,0:T(8,128)(2,1)S(1)} %convert_bitcast_fusion.1) | data formatting | bytes 3670016 | tf_op jit(solution)/shard_map/broadcast_in_dim | solution.py:76
  230.4 12.1 %reduce.10 = bf16[1024,896]{1,0:T(8,128)(2,1)S(1)} reduce(bf16[1024,1,896]{2,1,0:T(2,128)(2,1)} %bitcast.70, bf16[]{:T(256)} %broadcast.68), dimensions={1}, to_apply=%bitcast.53.reduce_sub_computation | reduce | bytes 3670018
  242.5 1.5 reshape.122
  244.0 4.8 %all-to-all-start.4 = ((bf16[2,2,229376]{2,1,0:T(2,128)(2,1)}), bf16[2,2,229376]{2,1,0:T(2,128)(2,1)}, u32[]{:S(2)}, u32[]{:S(2)}) async-start(bf16[2,2,229376]{2,1,0:T(2,128)(2,1)} %reshape.122), calls=%async_computation.4 | async-start | bytes 3670016 | tf_op jit(solution)/shard_map/all_to_all | solution.py:80
  248.9 1.4 convert_bitcast_fusion
  250.3 4.6 %copy.37 = bf16[1,1024,896]{2,0,1:T(2,128)(2,1)} copy(bf16[1,1024,896]{2,1,0:T(8,128)(2,1)S(1)} %convert_bitcast_fusion) | data formatting | bytes 3670016 | tf_op jit(solution)/shard_map/broadcast_in_dim | solution.py:77
  254.9 12.1 %reduce.11 = bf16[1024,896]{1,0:T(8,128)(2,1)S(1)} reduce(bf16[1024,1,896]{2,1,0:T(2,128)(2,1)} %bitcast.69, bf16[]{:T(256)} %broadcast.68), dimensions={1}, to_apply=%bitcast.66.reduce_sub_computation | reduce | bytes 3670018
  267.0 1.6 reshape.124
  268.6 3.3 %all-to-all-done.4 = bf16[2,2,229376]{2,1,0:T(2,128)(2,1)} async-done(((bf16[2,2,229376]{2,1,0:T(2,128)(2,1)}), bf16[2,2,229376]{2,1,0:T(2,128)(2,1)}, u32[]{:S(2)}, u32[]{:S(2)}) %all-to-all-start.4) | async-done | bytes 1835040 | tf_op jit(solution)/shard_map/all_to_all | solution.py:80
  271.8 3.9 %all-to-all-start.5 = ((bf16[2,2,229376]{2,1,0:T(2,128)(2,1)}), bf16[2,2,229376]{2,1,0:T(2,128)(2,1)S(1)}, u32[]{:S(2)}, u32[]{:S(2)}) async-start(bf16[2,2,229376]{2,1,0:T(2,128)(2,1)} %reshape.124), calls=%async_computation.5 | async-start | bytes 3670016 | tf_op jit(solution)/shard_map/all_to_all | solution.py:82
  275.8 1.0 gather_fusion.2
  276.8 0.9 multiply_convert_fusion
  277.7 4.0 %reshape.121 = bf16[1024,1,896]{2,1,0:T(2,128)(2,1)} reshape(bf16[2,2,229376]{2,1,0:T(2,128)(2,1)} %all-to-all-done.3) | data formatting | bytes 3670016
  281.7 3.6 %copy.30 = bf16[1,896,1024]{1,2,0:T(8,128)(2,1)} copy(bf16[1,896,1024]{1,0,2:T(2,128)(2,1)} %bitcast.71) | data formatting | bytes 3670016
  285.2 2.3 reduce_sum.46
  287.5 1.3 copy.28
  288.8 4.0 %reshape.123 = bf16[1024,1,896]{2,1,0:T(2,128)(2,1)} reshape(bf16[2,2,229376]{2,1,0:T(2,128)(2,1)} %all-to-all-done.4) | data formatting | bytes 3670016
  292.8 3.6 %copy.31 = bf16[1,896,1024]{1,2,0:T(8,128)(2,1)} copy(bf16[1,896,1024]{1,0,2:T(2,128)(2,1)} %bitcast.72) | data formatting | bytes 3670016
  296.3 2.3 reduce_sum.47
  298.7 1.3 copy.29
  300.0 2.8 reshape.125
  302.7 2.3 copy.32
  305.1 1.5 reduce.8
  (50 shorter events, 2.1 us)
Async XLA Ops:
  7.2 2.2 copy-start.2
  7.2 35.2 %all-gather.6.cloned.1.call-start = ((), (), s32[]{:S(2)}) async-start(), calls=%async_computation.7 | async-start | bytes 2752512 | tf_op jit(solution)/shard_map/all_gather | solution.py:44
  7.9 3.2 %copy-start = (bf16[192,896]{1,0:T(8,128)(2,1)S(1)}, bf16[192,896]{1,0:T(8,128)(2,1)}, u32[]{:S(2)}) copy-start(bf16[192,896]{1,0:T(8,128)(2,1)} %param.7) | copy-start | bytes 1032196
  7.9 66.2 %all-gather.8.cloned.1.call-start = ((), (), s32[]{:S(2)}) async-start(), calls=%async_computation.8 | async-start | bytes 2752512 | tf_op jit(solution)/shard_map/all_gather | solution.py:43
  8.7 97.2 %all-gather.4.cloned.1.call-start = ((), (), s32[]{:S(2)}) async-start(), calls=%async_computation.6 | async-start | bytes 2752512 | tf_op jit(solution)/shard_map/all_gather | solution.py:45
  12.4 7.0 %copy-start.3 = (f32[192]{0:T(256)S(1)}, f32[192]{0:T(256)}, u32[]{:S(2)}) copy-start(f32[192]{0:T(256)} %param.9) | copy-start | bytes 2308
  15.0 4.4 %copy-start.1 = (bf16[192,896]{1,0:T(8,128)(2,1)S(1)}, bf16[192,896]{1,0:T(8,128)(2,1)}, u32[]{:S(2)}) copy-start(bf16[192,896]{1,0:T(8,128)(2,1)} %param.8) | copy-start | bytes 1032196
  15.0 13.1 %all-to-all-start.1 = ((bf16[4,72,896]{2,1,0:T(8,128)(2,1)}), bf16[4,72,896]{2,1,0:T(8,128)(2,1)S(1)}, u32[]{:S(2)}, u32[]{:S(2)}) async-start(bf16[4,72,896]{2,1,0:T(8,128)(2,1)} %bitcast.8), calls=%async_computation.1 | async-start | bytes 1032192 | tf_op jit(solution)/shard_map/all_to_all | solution.py:40
  28.1 49.1 %all-to-all-start = ((bf16[4,72,896]{2,1,0:T(8,128)(2,1)}), bf16[4,72,896]{2,1,0:T(8,128)(2,1)S(1)}, u32[]{:S(2)}, u32[]{:S(2)}) async-start(bf16[4,72,896]{2,1,0:T(8,128)(2,1)} %bitcast.5), calls=%async_computation | async-start | bytes 1032192 | tf_op jit(solution)/shard_map/all_to_all | solution.py:59
  31.6 153.3 %all-reduce.6.cloned.1.call-start = ((), (), s32[]{:S(2)}) async-start(), calls=%async_computation.9 | async-start | bytes 3538944 | tf_op jit(solution)/shard_map/psum | solution.py:54
  105.9 79.0 %copy-start.5 = (bf16[1,896,1024]{2,1,0:T(8,128)(2,1)S(1)}, bf16[1,896,1024]{2,1,0:T(8,128)(2,1)}, u32[]{:S(2)}) copy-start(bf16[1,896,1024]{2,1,0:T(8,128)(2,1)} %all-gather.8.cloned.1.call-done) | copy-start | bytes 5505028
  184.9 2.7 copy-start.4
  184.9 2.7 copy-start.7
  184.9 2.7 copy-start.9
  189.3 27.0 %all-to-all-start.2 = ((bf16[4,72,896]{2,1,0:T(8,128)(2,1)}), bf16[4,72,896]{2,1,0:T(8,128)(2,1)S(1)}, u32[]{:S(2)}, u32[]{:S(2)}) async-start(bf16[4,72,896]{2,1,0:T(8,128)(2,1)} %bitcast.12), calls=%async_computation.2 | async-start | bytes 1032192 | tf_op jit(solution)/shard_map/all_to_all | solution.py:66
  216.3 27.7 %all-to-all-start.3 = ((bf16[2,2,229376]{2,1,0:T(2,128)(2,1)}), bf16[2,2,229376]{2,1,0:T(2,128)(2,1)}, u32[]{:S(2)}, u32[]{:S(2)}) async-start(bf16[2,2,229376]{2,1,0:T(2,128)(2,1)} %reshape.120), calls=%async_computation.3 | async-start | bytes 3670016 | tf_op jit(solution)/shard_map/all_to_all | solution.py:79
  244.0 4.9 %copy-start.6 = (bf16[288,1024]{1,0:T(8,128)(2,1)S(1)}, bf16[288,1024]{1,0:T(8,128)(2,1)}, u32[]{:S(2)}) copy-start(bf16[288,1024]{1,0:T(8,128)(2,1)} %get-tuple-element.8) | copy-start | bytes 1769476
  244.0 4.9 %copy-start.8 = (bf16[288,1024]{1,0:T(8,128)(2,1)S(1)}, bf16[288,1024]{1,0:T(8,128)(2,1)}, u32[]{:S(2)}) copy-start(bf16[288,1024]{1,0:T(8,128)(2,1)} %get-tuple-element.10) | copy-start | bytes 1769476
  244.0 27.8 %all-to-all-start.4 = ((bf16[2,2,229376]{2,1,0:T(2,128)(2,1)}), bf16[2,2,229376]{2,1,0:T(2,128)(2,1)}, u32[]{:S(2)}, u32[]{:S(2)}) async-start(bf16[2,2,229376]{2,1,0:T(2,128)(2,1)} %reshape.122), calls=%async_computation.4 | async-start | bytes 3670016 | tf_op jit(solution)/shard_map/all_to_all | solution.py:80
  271.8 28.1 %all-to-all-start.5 = ((bf16[2,2,229376]{2,1,0:T(2,128)(2,1)}), bf16[2,2,229376]{2,1,0:T(2,128)(2,1)S(1)}, u32[]{:S(2)}, u32[]{:S(2)}) async-start(bf16[2,2,229376]{2,1,0:T(2,128)(2,1)} %reshape.124), calls=%async_computation.5 | async-start | bytes 3670016 | tf_op jit(solution)/shard_map/all_to_all | solution.py:82
Sparse Core Ops, SparseCore 0:
  9.5 32.8 all-gather.5
  44.0 30.1 all-gather.7
  75.7 30.1 all-gather.3
  109.3 75.5 all-reduce.5
where the time goes:
time: 314 us; the launch traced here: 313 us
  waiting for transfers between devices  155 us (49%)
  local copies, waits for them, and re-layouts  53.5 us (17%)
  other arithmetic  44.8 us (14%)
  starting transfers between devices  25.1 us (8%)
  matrix products  20.5 us (7%)
  between operations  14 us (4%)
    psum x1, waiting for transfers between devices, local(): lax.psum(part_up.astype(jnp.bfloat16), 'seq').astype(jnp.float32)  75.7 us
    unnamed x4, other arithmetic  36.3 us
    all_gather x1, waiting for transfers between devices, local(): lax.all_gather(down_weight, 'replica', axis=1, tiled=True)  28.6 us
    all_gather x1, waiting for transfers between devices, local(): lax.all_gather(gate_weight, 'replica', axis=2, tiled=True)  28.6 us
    unnamed x33, local copies, waits for them, and re-layouts  27.9 us
    all_gather x1, waiting for transfers between devices, local(): lax.all_gather(up_weight, 'replica', axis=2, tiled=True)  10.8 us
    dot_general x3, matrix products, matmul_last(): lax.dot_general(left, right, (((1,), (1,)), ((), ())), preferred_element_...  7.66 us
    broadcast_in_dim x1, local copies, waits for them, and re-layouts, local(): grad_up = matmul_first(rows_x, up_delta).astype(jnp.bfloat16)[None]  6.63 us
  transfers between devices with their start and end apart: 10, of which 7 were waited for; matrix products, arithmetic and copies ran while one was open for 33% of the time, Pallas kernels for 0%

commit v1 on v0

v1 whole, which is shorter than its diff:
```python
import functools

import jax
import jax.numpy as jnp
from jax import lax
from jax.experimental import pallas as pl
from jax.experimental.pallas import tpu as pltpu
from jax.sharding import PartitionSpec as P

F32 = jnp.float32
BF16 = jnp.bfloat16
VMEM = pltpu.VMEM
SMEM = pltpu.SMEM


def mm(left, right, dims):
    return lax.dot_general(left, right, (dims, ((), ())), preferred_element_type=F32)


NN = ((1,), (0,))
NT = ((1,), (1,))
TN = ((0,), (0,))


def call(body, out_shape, n_smem, n_vmem, name, scratch=()):
    outs = out_shape if isinstance(out_shape, (list, tuple)) else [out_shape]
    return pl.pallas_call(
        body,
        out_shape=out_shape,
        in_specs=[pl.BlockSpec(memory_space=SMEM)] * n_smem + [pl.BlockSpec(memory_space=VMEM)] * n_vmem,
        out_specs=jax.tree.map(lambda _: pl.BlockSpec(memory_space=VMEM), out_shape),
        scratch_shapes=list(scratch),
        name=name,
    )


def column(row):
    count = row.shape[1]
    eye = lax.broadcasted_iota(jnp.int32, (count, count), 0) == lax.broadcasted_iota(jnp.int32, (count, count), 1)
    return jnp.sum(jnp.where(eye, row, jnp.zeros_like(row)), axis=1, keepdims=True)


def slots(ids, rank, owner, cap):
    places = lax.broadcasted_iota(jnp.int32, (ids.shape[0], cap), 1)
    return jnp.where((ids == owner) & (rank == places), 1.0, 0.0).astype(BF16)


def prep_body(n_expert, cap, ids_ref, tokens_ref, cot_ref, rw_ref, sx_ref, sg_ref, rank_ref):
    ids = ids_ref[...]
    count = ids.shape[0]
    lanes = lax.broadcasted_iota(jnp.int32, (count, 128), 1)
    onehot = jnp.where(ids == lanes, 1.0, 0.0)
    lower = jnp.where(
        lax.broadcasted_iota(jnp.int32, (count, count), 0) > lax.broadcasted_iota(jnp.int32, (count, count), 1), 1.0, 0.0
    )
    before = mm(lower.astype(BF16), onehot.astype(BF16), NN)
    rank = jnp.sum(before * onehot, axis=1, keepdims=True).astype(jnp.int32)
    rank_ref[...] = rank
    tokens = tokens_ref[...]
    scaled = (column(rw_ref[...]) * cot_ref[...].astype(F32)).astype(BF16)
    for j in range(n_expert):
        pick = slots(ids, rank, j, cap)
        sx_ref[j] = mm(pick, tokens, TN).astype(BF16)
        sg_ref[j] = mm(pick, scaled, TN).astype(BF16)


def part_body(half, waves, x_ref, g_ref, wg_ref, wu_ref, wd_ref, *outs):
    x = x_ref[...]
    g = g_ref[...]
    pg = mm(x, wg_ref[...], NN).astype(BF16)
    pu = mm(x, wu_ref[...], NN).astype(BF16)
    pd = mm(g, wd_ref[...], NT).astype(BF16)
    rows = x.shape[0] // waves
    for i in range(waves):
        outs[i][:, :half] = pg[i * rows:(i + 1) * rows]
        outs[i][:, half:2 * half] = pu[i * rows:(i + 1) * rows]
        outs[i][:, 2 * half:] = pd[i * rows:(i + 1) * rows]


def act_body(half, s_ref, m_ref, o_ref):
    gate = s_ref[:, :half].astype(F32) + m_ref[:, :half].astype(F32)
    upper = s_ref[:, half:2 * half].astype(F32) + m_ref[:, half:2 * half].astype(F32)
    hgrad = s_ref[:, 2 * half:].astype(F32) + m_ref[:, 2 * half:].astype(F32)
    sigma = jax.nn.sigmoid(gate)
    active = gate * sigma
    o_ref[:, :half] = (hgrad * upper * sigma * (1.0 + gate * (1.0 - sigma))).astype(BF16)
    o_ref[:, half:2 * half] = (hgrad * active).astype(BF16)
    o_ref[:, 2 * half:] = (active * upper).astype(BF16)


def out_body(half, edge_ref, t_ref, r_ref, wg_ref, wu_ref, a_ref, o_ref):
    @pl.when(edge_ref[0] == 1)
    def _():
        a_ref[...] = r_ref[...]

    @pl.when(edge_ref[0] == 0)
    def _():
        a_ref[...] = t_ref[...]

    o_ref[...] = (
        mm(a_ref[:, :half], wg_ref[...], NT) + mm(a_ref[:, half:2 * half], wu_ref[...], NT)
    ).astype(BF16)


def wgrad_body(half, n_x, n_a, *refs):
    xs, gs, acts = refs[:n_x], refs[n_x:2 * n_x], refs[2 * n_x:2 * n_x + n_a]
    gg_ref, gu_ref, gd_ref = refs[2 * n_x + n_a:]
    x = jnp.concatenate([r[...] for r in xs], axis=0)
    g = jnp.concatenate([r[...] for r in gs], axis=0)
    a = jnp.concatenate([r[...] for r in acts], axis=0)
    gg_ref[0] = mm(x, a[:, :half], TN).astype(BF16)
    gu_ref[0] = mm(x, a[:, half:2 * half], TN).astype(BF16)
    gd_ref[0] = mm(a[:, 2 * half:], g, TN).astype(BF16)


def final_body(n_expert, cap, ids_ref, rank_ref, rw_ref, ret_ref, o_ref):
    ids = ids_ref[...]
    rank = rank_ref[...]
    total = None
    for j in range(n_expert):
        term = mm(slots(ids, rank, j, cap), ret_ref[j], NN)
        total = term if total is None else total + term
    o_ref[...] = (column(rw_ref[...]) * total).astype(BF16)


def local(tokens, cotangent, route_weight, expert_ids, gate_weight, up_weight, down_weight):
    n_expert = lax.axis_size("expert")
    n_rep = lax.axis_size("replica")
    n_seq = lax.axis_size("seq")
    assert n_seq == 4 and n_rep & (n_rep - 1) == 0
    count, quarter = tokens.shape
    half = gate_weight.shape[2]
    cap = -(-(3 * count // (2 * n_expert)) // 8) * 8
    rows = n_expert * cap
    waves = 2
    wrows = rows // waves
    sds = jax.ShapeDtypeStruct
    z = lax.axis_index("seq")
    is_edge = (z == 0) | (z == n_seq - 1)
    edge = is_edge.astype(jnp.int32).reshape(1)
    w_gate, w_up, w_down = gate_weight[0], up_weight[0], down_weight[0]
    rw = route_weight.reshape(1, count)

    send_x, send_g, rank = call(
        functools.partial(prep_body, n_expert, cap),
        [sds((n_expert, cap, quarter), BF16), sds((n_expert, cap, quarter), BF16), sds((count, 1), jnp.int32)],
        0, 4, "prep",
    )(expert_ids, tokens, cotangent, rw)
    own_x = lax.all_to_all(send_x, "expert", 0, 0, tiled=True).reshape(rows, quarter)
    own_g = lax.all_to_all(send_g, "expert", 0, 0, tiled=True).reshape(rows, quarter)
    xs, gs = [own_x], [own_g]
    for k in range(1, n_rep):
        pairs = [(i, i ^ k) for i in range(n_rep)]
        xs.append(lax.ppermute(own_x, "replica", pairs))
        gs.append(lax.ppermute(own_g, "replica", pairs))
    parts = []
    for k in range(n_rep):
        parts += call(
            functools.partial(part_body, half, waves), [sds((wrows, 3 * half), BF16)] * waves, 0, 5, f"part{k}"
        )(xs[k], gs[k], w_gate, w_up, w_down)

    n_wave = len(parts)
    lag = 3
    sums, acts, outs = {}, {}, {}
    full = []
    inward, outward, middle = [(0, 1), (3, 2)], [(1, 0), (2, 3)], [(1, 2), (2, 1)]
    act = call(functools.partial(act_body, half), sds((wrows, 3 * half), BF16), 0, 2, "act")
    out = call(
        functools.partial(out_body, half), [sds((wrows, 3 * half), BF16), sds((wrows, quarter), BF16)], 1, 4, "out"
    )
    for i in range(n_wave + lag):
        back = i - lag
        if back < 0:
            got = lax.ppermute(parts[i], "seq", inward)
        elif i < n_wave:
            got = lax.ppermute(jnp.where(is_edge, parts[i], acts[back]), "seq", inward + outward)
        else:
            got = lax.ppermute(acts[back], "seq", outward)
        if i < n_wave:
            sums[i] = (parts[i].astype(F32) + got.astype(F32)).astype(BF16)
            acts[i] = act(sums[i], lax.ppermute(sums[i], "seq", middle))
        if back >= 0:
            a, o = out(edge, acts[back], got, w_gate, w_up)
            full.append(a)
            outs[back] = o

    total = [outs[i].astype(F32) for i in range(waves)]
    for k in range(1, n_rep):
        pairs = [(i, i ^ k) for i in range(n_rep)]
        for i in range(waves):
            total[i] = total[i] + lax.ppermute(outs[k * waves + i], "replica", pairs).astype(F32)
    back_rows = jnp.concatenate([t.astype(BF16) for t in total], axis=0).reshape(n_expert, cap, quarter)
    returned = lax.all_to_all(back_rows, "expert", 0, 0, tiled=True)
    gate_grad, up_grad, down_grad = call(
        functools.partial(wgrad_body, half, n_rep, n_wave),
        [sds((1, quarter, half), BF16), sds((1, quarter, half), BF16), sds((1, half, quarter), BF16)],
        0, 2 * n_rep + n_wave, "wgrad",
    )(*xs, *gs, *full)
    token_grad = call(
        functools.partial(final_body, n_expert, cap), sds((count, quarter), BF16), 0, 4, "final"
    )(expert_ids, rank, rw, returned)
    return (token_grad, gate_grad, up_grad, down_grad)


def solution(mesh):
    placed = (
        P(("expert", "replica"), "seq"),
        P(("expert", "replica"), "seq"),
        P(("expert", "replica")),
        P(("expert", "replica"), None),
        P("expert", "seq", "replica"),
        P("expert", "seq", "replica"),
        P("expert", "replica", "seq"),
    )
    return jax.shard_map(
        local,
        mesh=mesh,
        in_specs=placed,
        out_specs=(
            P(("expert", "replica"), "seq"),
            P("expert", "seq", "replica"),
            P("expert", "seq", "replica"),
            P("expert", "replica", "seq"),
        ),
        check_vma=False,
    )
```

time: 314 us -> 153 us (0.49)
  waiting for transfers between devices: 155 us -> 44.5 us
  local copies, waits for them, and re-layouts: 53.5 us -> 9.16 us
  other arithmetic: 44.8 us -> 2.47 us
  Pallas kernels: 0 us -> 40.3 us
  blocking collectives: 0 us -> 25.6 us
  matrix products: 20.5 us -> 0 us
  between operations: 14 us -> 0.93 us
  starting transfers between devices: 25.1 us -> 28.8 us
    psum x1 -> x0, waiting for transfers between devices: 75.7 us -> none  [local(): lax.psum(part_up.astype(jnp.bfloat16), 'seq').astype(jnp.float32)]
    all_gather x3 -> x0, waiting for transfers between devices: 68 us -> none  [the longest x1 28.6 us: local(): lax.all_gather(down_weight, 'replica', axis=1, tiled=True)]
    ppermute x0 -> x15, waiting for transfers between devices: none -> 41.2 us  [the longest x3 15.4 us: local(): got = lax.ppermute(parts[i], 'seq', inward)]
    pallas_call x0 -> x13, Pallas kernels: none -> 40.3 us  [the longest x4 12.7 us: local(): a, o = out(edge, acts[back], got, w_gate, w_up)]
    unnamed x4 -> x0, other arithmetic: 36.3 us -> none
    all_to_all x0 -> x2, blocking collectives: none -> 25.6 us  [the longest x1 13.8 us: local(): lax.all_to_all(send_x, 'expert', 0, 0, tiled=True).reshape(rows, quarter)]
    ppermute x0 -> x15, starting transfers between devices: none -> 25.4 us  [the longest x3 12.5 us: local(): got = lax.ppermute(parts[i], 'seq', inward)]
    all_to_all x6 -> x1, starting transfers between devices: 25 us -> 3.47 us  [local(): returned = lax.all_to_all(back_rows, 'expert', 0, 0, tiled=True)]
  transfers between devices with their start and end apart: 10 -> 16, of which waited for: 7 -> 7; matrix products, arithmetic and copies ran while one was open for 33% -> 1% of each run, Pallas kernels for 0% -> 20%
where the time goes in v1:
time: 153 us; the launch traced here: 152 us
  waiting for transfers between devices  44.5 us (29%)
  Pallas kernels  40.3 us (26%)
  starting transfers between devices  28.8 us (19%)
  blocking collectives  25.6 us (17%)
  local copies, waits for them, and re-layouts  9.16 us (6%)
  other arithmetic  2.47 us (2%)
    ppermute x3, waiting for transfers between devices, local(): got = lax.ppermute(parts[i], 'seq', inward)  15.4 us
    ppermute x3, waiting for transfers between devices, local(): got = lax.ppermute(acts[back], 'seq', outward)  13.8 us
    all_to_all x1, blocking collectives, local(): lax.all_to_all(send_x, 'expert', 0, 0, tiled=True).reshape(rows, quarter)  13.8 us
    pallas_call x4, Pallas kernels, local(): a, o = out(edge, acts[back], got, w_gate, w_up)  12.7 us
    ppermute x3, starting transfers between devices, local(): got = lax.ppermute(parts[i], 'seq', inward)  12.5 us
    all_to_all x1, blocking collectives, local(): lax.all_to_all(send_g, 'expert', 0, 0, tiled=True).reshape(rows, quarter)  11.8 us
    unnamed x45, local copies, waits for them, and re-layouts  9.16 us
    pallas_call x4, Pallas kernels, local(): acts[i] = act(sums[i], lax.ppermute(sums[i], 'seq', middle))  8.55 us
  transfers between devices with their start and end apart: 16, of which 7 were waited for; matrix products, arithmetic and copies ran while one was open for 1% of the time, Pallas kernels for 20%

profile of v1, /device:TPU:0, one launch (start us, length us, event | category | flops | bytes accessed | tf_op | source)
XLA Modules:
  0.0 151.7 jit_solution(4284998117198806149)
XLA Ops:
  0.6 1.4 copy.12.ids_ref
  2.1 3.1 %prep.1 = (bf16[4,72,896]{2,1,0:T(8,128)(2,1)}, bf16[4,72,896]{2,1,0:T(8,128)(2,1)}, s32[192,1]{1,0:T(8,128)}) custom-call(s32[192,1]{1,0:T(8,128)} %copy.12.ids_ref, bf16[192,896]{1,0:T(8,128)(2,1)} %tokens_ref.1, bf16[192,896]{1,0:T(8,128)(2,1)} %cot_ref.1, f32[1,192]{1,0:T(1,128)} %bitcast.28), custom_call_target="tpu_custom_call" | custom-call | tf_op jit(solution)/shard_map/prep/pallas_call | solution.py:144
  5.2 13.8 %all_to_all.15 = bf16[4,72,896]{2,1,0:T(8,128)(2,1)} all-to-all(bf16[4,72,896]{2,1,0:T(8,128)(2,1)} %get-tuple-element.23), channel_id=1, replica_groups=mesh['expert'=4,'replica'=2,'seq'=4] {'expert'}, dimensions={0} | all-to-all | bytes 1032192 | tf_op jit(solution)/shard_map/all_to_all | solution.py:149
  18.9 11.8 %all_to_all.16 = bf16[4,72,896]{2,1,0:T(8,128)(2,1)} all-to-all(bf16[4,72,896]{2,1,0:T(8,128)(2,1)S(1)} %copy-done.11), channel_id=1, replica_groups=mesh['expert'=4,'replica'=2,'seq'=4] {'expert'}, dimensions={0} | all-to-all | bytes 1032192 | tf_op jit(solution)/shard_map/all_to_all | solution.py:150
  30.7 4.1 %part0.1 = (bf16[144,1536]{1,0:T(8,128)(2,1)}, bf16[144,1536]{1,0:T(8,128)(2,1)}) custom-call(bf16[288,896]{1,0:T(8,128)(2,1)} %bitcast.20, bf16[288,896]{1,0:T(8,128)(2,1)} %bitcast.23, bf16[896,512]{1,0:T(8,128)(2,1)} %bitcast.8, bf16[896,512]{1,0:T(8,128)(2,1)} %bitcast.14, bf16[512,896]{1,0:T(8,128)(2,1)} %bitcast.26), custom_call_target="tpu_custom_call" | custom-call | tf_op jit(solution)/shard_map/part0/pallas_call | solution.py:158
  34.8 4.4 %collective-permute-start = (bf16[144,1536]{1,0:T(8,128)(2,1)}, bf16[144,1536]{1,0:T(8,128)(2,1)S(1)}, u32[]{:S(2)}, u32[]{:S(2)}) collective-permute-start(bf16[144,1536]{1,0:T(8,128)(2,1)} %get-tuple-element.25), channel_id=1, source_target_pairs={{0,1},{3,2},{4,5},{7,6},{8,9},{11,10},{12,13},{15,14},{16,17},{19,... | collective-permute-start | bytes 1327112 | tf_op jit(solution)/shard_map/ppermute | solution.py:174
  39.2 1.6 %collective-permute-start.2 = (bf16[288,896]{1,0:T(8,128)(2,1)S(1)}, bf16[288,896]{1,0:T(8,128)(2,1)S(1)}, u32[]{:S(2)}, u32[]{:S(2)}) collective-permute-start(bf16[288,896]{1,0:T(8,128)(2,1)S(1)} %bitcast.22), channel_id=1, source_target_pairs={{0,4},{4,0},{1,5},{5,1},{2,6},{6,2},{3,7},{7,3},{8,12},{12,8},{9,1... | collective-permute-start | bytes 1548296 | tf_op jit(solution)/shard_map/ppermute | solution.py:154
  41.3 7.2 %collective-permute-done = bf16[144,1536]{1,0:T(8,128)(2,1)S(1)} collective-permute-done((bf16[144,1536]{1,0:T(8,128)(2,1)}, bf16[144,1536]{1,0:T(8,128)(2,1)S(1)}, u32[]{:S(2)}, u32[]{:S(2)}) %collective-permute-start) | collective-permute-done | bytes 442400 | tf_op jit(solution)/shard_map/ppermute | solution.py:174
  48.6 1.1 add_convert_fusion.3.s_ref
  49.7 1.4 collective-permute-start.1
  51.2 6.4 %collective-permute-start.9 = (bf16[144,1536]{1,0:T(8,128)(2,1)S(1)}, bf16[144,1536]{1,0:T(8,128)(2,1)S(1)}, u32[]{:S(2)}, u32[]{:S(2)}) collective-permute-start(bf16[144,1536]{1,0:T(8,128)(2,1)S(1)} %copy-done.12), channel_id=1, source_target_pairs={{0,1},{3,2},{4,5},{7,6},{8,9},{11,10},{12,13},{15,14},{16,17},{19,... | collective-permute-start | bytes 1327112 | tf_op jit(solution)/shard_map/ppermute | solution.py:174
  57.6 5.7 %collective-permute-done.3.g_ref.refs_3_ = bf16[288,896]{1,0:T(8,128)(2,1)S(1)} collective-permute-done((bf16[288,896]{1,0:T(8,128)(2,1)S(1)}, bf16[288,896]{1,0:T(8,128)(2,1)S(1)}, u32[]{:S(2)}, u32[]{:S(2)}) %collective-permute-start.3) | collective-permute-done | bytes 516128 | tf_op jit(solution)/shard_map/ppermute | solution.py:155
  63.2 0.8 copy-done.4
  64.0 4.0 %part1.1 = (bf16[144,1536]{1,0:T(8,128)(2,1)}, bf16[144,1536]{1,0:T(8,128)(2,1)}) custom-call(bf16[288,896]{1,0:T(8,128)(2,1)} %copy-done.3, bf16[288,896]{1,0:T(8,128)(2,1)} %copy-done.4, bf16[896,512]{1,0:T(8,128)(2,1)} %bitcast.9, bf16[896,512]{1,0:T(8,128)(2,1)} %bitcast.15, bf16[512,896]{1,0:T(8,128)(2,1)} %bitcast.27), custom_call_target="tpu_custom_call" | custom-call | tf_op jit(solution)/shard_map/part1/pallas_call | solution.py:158
  68.0 1.7 %collective-permute-start.5 = (bf16[144,1536]{1,0:T(8,128)(2,1)}, bf16[144,1536]{1,0:T(8,128)(2,1)S(1)}, u32[]{:S(2)}, u32[]{:S(2)}) collective-permute-start(bf16[144,1536]{1,0:T(8,128)(2,1)} %get-tuple-element.28), channel_id=1, source_target_pairs={{0,1},{3,2},{4,5},{7,6},{8,9},{11,10},{12,13},{15,14},{16,17},{19,... | collective-permute-start | bytes 1327112 | tf_op jit(solution)/shard_map/ppermute | solution.py:174
  69.7 2.2 %act.4.t_ref = bf16[144,1536]{1,0:T(8,128)(2,1)} custom-call(bf16[144,1536]{1,0:T(8,128)(2,1)} %copy-done.6, bf16[144,1536]{1,0:T(8,128)(2,1)} %collective-permute-done.1.m_ref), custom_call_target="tpu_custom_call" | custom-call | tf_op jit(solution)/shard_map/act/pallas_call | solution.py:181
  72.4 8.1 %collective-permute-done.5 = bf16[144,1536]{1,0:T(8,128)(2,1)S(1)} collective-permute-done((bf16[144,1536]{1,0:T(8,128)(2,1)}, bf16[144,1536]{1,0:T(8,128)(2,1)S(1)}, u32[]{:S(2)}, u32[]{:S(2)}) %collective-permute-start.5) | collective-permute-done | bytes 442400 | tf_op jit(solution)/shard_map/ppermute | solution.py:174
  80.7 0.7 collective-permute-start.6
  81.4 6.3 %collective-permute-done.4.r_ref = bf16[144,1536]{1,0:T(8,128)(2,1)S(1)} collective-permute-done((bf16[144,1536]{1,0:T(8,128)(2,1)S(1)}, bf16[144,1536]{1,0:T(8,128)(2,1)S(1)}, u32[]{:S(2)}, u32[]{:S(2)}) %collective-permute-start.4) | collective-permute-done | bytes 442400 | tf_op jit(solution)/shard_map/ppermute | solution.py:176
  88.5 0.7 collective-permute-start.12
  89.3 0.7 collective-permute-start.10
  90.0 0.8 copy-done.13
  90.8 2.1 %act.5.t_ref = bf16[144,1536]{1,0:T(8,128)(2,1)} custom-call(bf16[144,1536]{1,0:T(8,128)(2,1)} %copy-done.7, bf16[144,1536]{1,0:T(8,128)(2,1)} %copy-done.13), custom_call_target="tpu_custom_call" | custom-call | tf_op jit(solution)/shard_map/act/pallas_call | solution.py:181
  92.9 1.3 collective-permute-start.7
  94.2 0.8 copy-done.14
  95.0 2.1 %act.7.t_ref = bf16[144,1536]{1,0:T(8,128)(2,1)} custom-call(bf16[144,1536]{1,0:T(8,128)(2,1)} %copy-done.9, bf16[144,1536]{1,0:T(8,128)(2,1)} %copy-done.14), custom_call_target="tpu_custom_call" | custom-call | tf_op jit(solution)/shard_map/act/pallas_call | solution.py:181
  97.1 1.3 collective-permute-start.13
  98.4 0.8 copy-done.15
  99.2 2.1 %act.6.t_ref = bf16[144,1536]{1,0:T(8,128)(2,1)} custom-call(bf16[144,1536]{1,0:T(8,128)(2,1)} %copy-done.8, bf16[144,1536]{1,0:T(8,128)(2,1)} %copy-done.15), custom_call_target="tpu_custom_call" | custom-call | tf_op jit(solution)/shard_map/act/pallas_call | solution.py:181
  101.3 1.3 collective-permute-start.11
  102.6 9.7 %collective-permute-done.7.r_ref = bf16[144,1536]{1,0:T(8,128)(2,1)S(1)} collective-permute-done((bf16[144,1536]{1,0:T(8,128)(2,1)}, bf16[144,1536]{1,0:T(8,128)(2,1)S(1)}, u32[]{:S(2)}, u32[]{:S(2)}) %collective-permute-start.7) | collective-permute-done | bytes 442400 | tf_op jit(solution)/shard_map/ppermute | solution.py:178
  112.4 0.8 copy-done.19
  113.1 3.2 %out.5 = (bf16[144,1536]{1,0:T(8,128)(2,1)}, bf16[144,896]{1,0:T(8,128)(2,1)}) custom-call(s32[1]{0:T(128)} %bitcast.1.edge_ref, bf16[144,1536]{1,0:T(8,128)(2,1)} %act.5.t_ref, bf16[144,1536]{1,0:T(8,128)(2,1)} %copy-done.19, bf16[896,512]{1,0:T(8,128)(2,1)} %bitcast.10, bf16[896,512]{1,0:T(8,128)(2,1)} %bitcast.16), custom_call_target="tpu_custom_call" | custom-call | tf_op jit(solution)/shard_map/out/pallas_call | solution.py:183
  116.3 1.5 collective-permute-start.8
  117.8 4.0 %collective-permute-done.13.r_ref = bf16[144,1536]{1,0:T(8,128)(2,1)S(1)} collective-permute-done((bf16[144,1536]{1,0:T(8,128)(2,1)}, bf16[144,1536]{1,0:T(8,128)(2,1)S(1)}, u32[]{:S(2)}, u32[]{:S(2)}) %collective-permute-start.13) | collective-permute-done | bytes 442400 | tf_op jit(solution)/shard_map/ppermute | solution.py:178
  121.8 0.8 copy-done.18
  122.6 3.2 %out.7 = (bf16[144,1536]{1,0:T(8,128)(2,1)}, bf16[144,896]{1,0:T(8,128)(2,1)}) custom-call(s32[1]{0:T(128)} %bitcast.1.edge_ref, bf16[144,1536]{1,0:T(8,128)(2,1)} %act.7.t_ref, bf16[144,1536]{1,0:T(8,128)(2,1)} %copy-done.18, bf16[896,512]{1,0:T(8,128)(2,1)} %bitcast.11, bf16[896,512]{1,0:T(8,128)(2,1)} %bitcast.17), custom_call_target="tpu_custom_call" | custom-call | tf_op jit(solution)/shard_map/out/pallas_call | solution.py:183
  125.8 1.5 collective-permute-start.14
  127.3 3.2 %out.4 = (bf16[144,1536]{1,0:T(8,128)(2,1)}, bf16[144,896]{1,0:T(8,128)(2,1)}) custom-call(s32[1]{0:T(128)} %bitcast.1.edge_ref, bf16[144,1536]{1,0:T(8,128)(2,1)} %act.4.t_ref, bf16[144,1536]{1,0:T(8,128)(2,1)} %copy-done.10, bf16[896,512]{1,0:T(8,128)(2,1)} %bitcast.12, bf16[896,512]{1,0:T(8,128)(2,1)} %bitcast.18), custom_call_target="tpu_custom_call" | custom-call | tf_op jit(solution)/shard_map/out/pallas_call | solution.py:183
  130.5 0.8 copy-done.17
  131.3 3.2 %out.6 = (bf16[144,1536]{1,0:T(8,128)(2,1)}, bf16[144,896]{1,0:T(8,128)(2,1)}) custom-call(s32[1]{0:T(128)} %bitcast.1.edge_ref, bf16[144,1536]{1,0:T(8,128)(2,1)} %act.6.t_ref, bf16[144,1536]{1,0:T(8,128)(2,1)} %copy-done.17, bf16[896,512]{1,0:T(8,128)(2,1)} %bitcast.13, bf16[896,512]{1,0:T(8,128)(2,1)} %bitcast.19), custom_call_target="tpu_custom_call" | custom-call | tf_op jit(solution)/shard_map/out/pallas_call | solution.py:183
  134.5 0.9 copy-done.21
  135.5 0.8 pad_maximum_fusion
  136.3 3.5 %all-to-all-start.2 = ((bf16[4,72,896]{2,1,0:T(8,128)(2,1)}), bf16[4,72,896]{2,1,0:T(8,128)(2,1)S(1)}, u32[]{:S(2)}, u32[]{:S(2)}) async-start(bf16[4,72,896]{2,1,0:T(8,128)(2,1)} %bitcast.7), calls=%async_computation.2 | async-start | bytes 1032192 | tf_op jit(solution)/shard_map/all_to_all | solution.py:193
  139.8 5.4 %wgrad.1 = (bf16[1,896,512]{2,1,0:T(8,128)(2,1)}, bf16[1,896,512]{2,1,0:T(8,128)(2,1)}, bf16[1,512,896]{2,1,0:T(8,128)(2,1)}) custom-call(bf16[288,896]{1,0:T(8,128)(2,1)} %bitcast.21, bf16[288,896]{1,0:T(8,128)(2,1)} %copy-done.3, bf16[288,896]{1,0:T(8,128)(2,1)} %bitcast.24, bf16[288,896]{1,0:T(8,128)(2,1)} %copy-done.4, ...), custom_call_target="tpu_custom_call" | custom-call | tf_op jit(solution)/shard_map/wgrad/pallas_call | solution.py:194
  145.2 3.3 %all-to-all-done.2.ret_ref = bf16[4,72,896]{2,1,0:T(8,128)(2,1)S(1)} async-done(((bf16[4,72,896]{2,1,0:T(8,128)(2,1)}), bf16[4,72,896]{2,1,0:T(8,128)(2,1)S(1)}, u32[]{:S(2)}, u32[]{:S(2)}) %all-to-all-start.2) | async-done | bytes 516128 | tf_op jit(solution)/shard_map/all_to_all | solution.py:193
  148.5 0.8 copy-done.2
  149.3 2.5 %final.1 = bf16[192,896]{1,0:T(8,128)(2,1)} custom-call(s32[192,1]{1,0:T(8,128)} %copy.12.ids_ref, s32[192,1]{1,0:T(8,128)} %get-tuple-element.22.rank_ref, f32[1,192]{1,0:T(1,128)} %bitcast.29, bf16[4,72,896]{2,1,0:T(8,128)(2,1)} %copy-done.2), custom_call_target="tpu_custom_call" | custom-call | tf_op jit(solution)/shard_map/final/pallas_call | solution.py:199
  (52 shorter events, 2.3 us)
Async XLA Ops:
  5.2 13.8 %copy-start.11 = (bf16[4,72,896]{2,1,0:T(8,128)(2,1)S(1)}, bf16[4,72,896]{2,1,0:T(8,128)(2,1)}, u32[]{:S(2)}) copy-start(bf16[4,72,896]{2,1,0:T(8,128)(2,1)} %get-tuple-element.24) | copy-start | bytes 1548292
  30.7 8.5 %copy-start = (bf16[4,72,896]{2,1,0:T(8,128)(2,1)S(1)}, bf16[4,72,896]{2,1,0:T(8,128)(2,1)}, u32[]{:S(2)}) copy-start(bf16[4,72,896]{2,1,0:T(8,128)(2,1)} %all_to_all.15) | copy-start | bytes 1548292
  30.7 10.1 %copy-start.1 = (bf16[4,72,896]{2,1,0:T(8,128)(2,1)S(1)}, bf16[4,72,896]{2,1,0:T(8,128)(2,1)}, u32[]{:S(2)}) copy-start(bf16[4,72,896]{2,1,0:T(8,128)(2,1)} %all_to_all.16) | copy-start | bytes 1548292
  34.8 16.3 %copy-start.12 = (bf16[144,1536]{1,0:T(8,128)(2,1)S(1)}, bf16[144,1536]{1,0:T(8,128)(2,1)}, u32[]{:S(2)}) copy-start(bf16[144,1536]{1,0:T(8,128)(2,1)} %get-tuple-element.30) | copy-start | bytes 1327108
  34.8 13.8 %collective-permute-start = (bf16[144,1536]{1,0:T(8,128)(2,1)}, bf16[144,1536]{1,0:T(8,128)(2,1)S(1)}, u32[]{:S(2)}, u32[]{:S(2)}) collective-permute-start(bf16[144,1536]{1,0:T(8,128)(2,1)} %get-tuple-element.25), channel_id=1, source_target_pairs={{0,1},{3,2},{4,5},{7,6},{8,9},{11,10},{12,13},{15,14},{16,17},{19,... | collective-permute-start | bytes 1327112 | tf_op jit(solution)/shard_map/ppermute | solution.py:174
  39.2 18.3 %collective-permute-start.2 = (bf16[288,896]{1,0:T(8,128)(2,1)S(1)}, bf16[288,896]{1,0:T(8,128)(2,1)S(1)}, u32[]{:S(2)}, u32[]{:S(2)}) collective-permute-start(bf16[288,896]{1,0:T(8,128)(2,1)S(1)} %bitcast.22), channel_id=1, source_target_pairs={{0,4},{4,0},{1,5},{5,1},{2,6},{6,2},{3,7},{7,3},{8,12},{12,8},{9,1... | collective-permute-start | bytes 1548296 | tf_op jit(solution)/shard_map/ppermute | solution.py:154
  40.8 22.4 %collective-permute-start.3 = (bf16[288,896]{1,0:T(8,128)(2,1)S(1)}, bf16[288,896]{1,0:T(8,128)(2,1)S(1)}, u32[]{:S(2)}, u32[]{:S(2)}) collective-permute-start(bf16[288,896]{1,0:T(8,128)(2,1)S(1)} %bitcast.25), channel_id=1, source_target_pairs={{0,4},{4,0},{1,5},{5,1},{2,6},{6,2},{3,7},{7,3},{8,12},{12,8},{9,1... | collective-permute-start | bytes 1548296 | tf_op jit(solution)/shard_map/ppermute | solution.py:155
  49.7 18.3 %copy-start.6 = (bf16[144,1536]{1,0:T(8,128)(2,1)}, bf16[144,1536]{1,0:T(8,128)(2,1)S(1)}, u32[]{:S(2)}) copy-start(bf16[144,1536]{1,0:T(8,128)(2,1)S(1)} %add_convert_fusion.3.s_ref) | copy-start | bytes 1327108
  49.7 20.0 %collective-permute-start.1 = (bf16[144,1536]{1,0:T(8,128)(2,1)S(1)}, bf16[144,1536]{1,0:T(8,128)(2,1)}, u32[]{:S(2)}, u32[]{:S(2)}) collective-permute-start(bf16[144,1536]{1,0:T(8,128)(2,1)S(1)} %add_convert_fusion.3.s_ref), channel_id=1, source_target_pairs={{1,2},{2,1},{5,6},{6,5},{9,10},{10,9},{13,14},{14,13},{17,18},{18,... | collective-permute-start | bytes 1327112 | tf_op jit(solution)/shard_map/ppermute | solution.py:181
  51.2 38.0 %collective-permute-start.9 = (bf16[144,1536]{1,0:T(8,128)(2,1)S(1)}, bf16[144,1536]{1,0:T(8,128)(2,1)S(1)}, u32[]{:S(2)}, u32[]{:S(2)}) collective-permute-start(bf16[144,1536]{1,0:T(8,128)(2,1)S(1)} %copy-done.12), channel_id=1, source_target_pairs={{0,1},{3,2},{4,5},{7,6},{8,9},{11,10},{12,13},{15,14},{16,17},{19,... | collective-permute-start | bytes 1327112 | tf_op jit(solution)/shard_map/ppermute | solution.py:174
  57.6 5.7 %copy-start.3 = (bf16[288,896]{1,0:T(8,128)(2,1)}, bf16[288,896]{1,0:T(8,128)(2,1)S(1)}, u32[]{:S(2)}) copy-start(bf16[288,896]{1,0:T(8,128)(2,1)S(1)} %collective-permute-done.2.x_ref.refs_1_) | copy-start | bytes 1548292
  63.2 0.8 copy-start.4
  68.0 3.9 %copy-start.5 = (bf16[144,1536]{1,0:T(8,128)(2,1)S(1)}, bf16[144,1536]{1,0:T(8,128)(2,1)}, u32[]{:S(2)}) copy-start(bf16[144,1536]{1,0:T(8,128)(2,1)} %get-tuple-element.26) | copy-start | bytes 1327108
  68.0 12.5 %collective-permute-start.5 = (bf16[144,1536]{1,0:T(8,128)(2,1)}, bf16[144,1536]{1,0:T(8,128)(2,1)S(1)}, u32[]{:S(2)}, u32[]{:S(2)}) collective-permute-start(bf16[144,1536]{1,0:T(8,128)(2,1)} %get-tuple-element.28), channel_id=1, source_target_pairs={{0,1},{3,2},{4,5},{7,6},{8,9},{11,10},{12,13},{15,14},{16,17},{19,... | collective-permute-start | bytes 1327112 | tf_op jit(solution)/shard_map/ppermute | solution.py:174
  71.9 8.7 %copy-start.16 = (bf16[144,1536]{1,0:T(8,128)(2,1)S(1)}, bf16[144,1536]{1,0:T(8,128)(2,1)}, u32[]{:S(2)}) copy-start(bf16[144,1536]{1,0:T(8,128)(2,1)} %get-tuple-element.28) | copy-start | bytes 1327108
  72.0 15.8 %collective-permute-start.4 = (bf16[144,1536]{1,0:T(8,128)(2,1)S(1)}, bf16[144,1536]{1,0:T(8,128)(2,1)S(1)}, u32[]{:S(2)}, u32[]{:S(2)}) collective-permute-start(bf16[144,1536]{1,0:T(8,128)(2,1)S(1)} %broadcast_select_fusion), channel_id=1, source_target_pairs={{0,1},{3,2},{1,0},{2,3},{4,5},{7,6},{5,4},{6,7},{8,9},{11,10},{9,8... | collective-permute-start | bytes 1327112 | tf_op jit(solution)/shard_map/ppermute | solution.py:176
  80.7 7.1 %copy-start.7 = (bf16[144,1536]{1,0:T(8,128)(2,1)}, bf16[144,1536]{1,0:T(8,128)(2,1)S(1)}, u32[]{:S(2)}) copy-start(bf16[144,1536]{1,0:T(8,128)(2,1)S(1)} %add_convert_fusion.2.s_ref) | copy-start | bytes 1327108
  80.7 9.3 %collective-permute-start.6 = (bf16[144,1536]{1,0:T(8,128)(2,1)S(1)}, bf16[144,1536]{1,0:T(8,128)(2,1)S(1)}, u32[]{:S(2)}, u32[]{:S(2)}) collective-permute-start(bf16[144,1536]{1,0:T(8,128)(2,1)S(1)} %add_convert_fusion.2.s_ref), channel_id=1, source_target_pairs={{1,2},{2,1},{5,6},{6,5},{9,10},{10,9},{13,14},{14,13},{17,18},{18,... | collective-permute-start | bytes 1327112 | tf_op jit(solution)/shard_map/ppermute | solution.py:181
  87.7 0.8 copy-start.10
  88.5 0.8 copy-start.9
  88.5 5.7 %collective-permute-start.12 = (bf16[144,1536]{1,0:T(8,128)(2,1)S(1)}, bf16[144,1536]{1,0:T(8,128)(2,1)S(1)}, u32[]{:S(2)}, u32[]{:S(2)}) collective-permute-start(bf16[144,1536]{1,0:T(8,128)(2,1)S(1)} %add_convert_fusion.s_ref), channel_id=1, source_target_pairs={{1,2},{2,1},{5,6},{6,5},{9,10},{10,9},{13,14},{14,13},{17,18},{18,... | collective-permute-start | bytes 1327112 | tf_op jit(solution)/shard_map/ppermute | solution.py:181
  89.3 3.6 %copy-start.8 = (bf16[144,1536]{1,0:T(8,128)(2,1)}, bf16[144,1536]{1,0:T(8,128)(2,1)S(1)}, u32[]{:S(2)}) copy-start(bf16[144,1536]{1,0:T(8,128)(2,1)S(1)} %add_convert_fusion.1.s_ref) | copy-start | bytes 1327108
  89.3 9.1 %collective-permute-start.10 = (bf16[144,1536]{1,0:T(8,128)(2,1)S(1)}, bf16[144,1536]{1,0:T(8,128)(2,1)S(1)}, u32[]{:S(2)}, u32[]{:S(2)}) collective-permute-start(bf16[144,1536]{1,0:T(8,128)(2,1)S(1)} %add_convert_fusion.1.s_ref), channel_id=1, source_target_pairs={{1,2},{2,1},{5,6},{6,5},{9,10},{10,9},{13,14},{14,13},{17,18},{18,... | collective-permute-start | bytes 1327112 | tf_op jit(solution)/shard_map/ppermute | solution.py:181
  90.0 0.8 copy-start.13
  92.9 19.4 %collective-permute-start.7 = (bf16[144,1536]{1,0:T(8,128)(2,1)}, bf16[144,1536]{1,0:T(8,128)(2,1)S(1)}, u32[]{:S(2)}, u32[]{:S(2)}) collective-permute-start(bf16[144,1536]{1,0:T(8,128)(2,1)} %act.5.t_ref), channel_id=1, source_target_pairs={{1,0},{2,3},{5,4},{6,7},{9,8},{10,11},{13,12},{14,15},{17,16},{18,... | collective-permute-start | bytes 1327112 | tf_op jit(solution)/shard_map/ppermute | solution.py:178
  94.2 0.8 copy-start.14
  97.1 24.7 %collective-permute-start.13 = (bf16[144,1536]{1,0:T(8,128)(2,1)}, bf16[144,1536]{1,0:T(8,128)(2,1)S(1)}, u32[]{:S(2)}, u32[]{:S(2)}) collective-permute-start(bf16[144,1536]{1,0:T(8,128)(2,1)} %act.7.t_ref), channel_id=1, source_target_pairs={{1,0},{2,3},{5,4},{6,7},{9,8},{10,11},{13,12},{14,15},{17,16},{18,... | collective-permute-start | bytes 1327112 | tf_op jit(solution)/shard_map/ppermute | solution.py:178
  98.4 0.8 copy-start.15
  101.3 29.2 %collective-permute-start.11 = (bf16[144,1536]{1,0:T(8,128)(2,1)}, bf16[144,1536]{1,0:T(8,128)(2,1)S(1)}, u32[]{:S(2)}, u32[]{:S(2)}) collective-permute-start(bf16[144,1536]{1,0:T(8,128)(2,1)} %act.6.t_ref), channel_id=1, source_target_pairs={{1,0},{2,3},{5,4},{6,7},{9,8},{10,11},{13,12},{14,15},{17,16},{18,... | collective-permute-start | bytes 1327112 | tf_op jit(solution)/shard_map/ppermute | solution.py:178
  112.4 0.8 copy-start.19
  116.3 18.1 %collective-permute-start.8 = (bf16[144,896]{1,0:T(8,128)(2,1)}, bf16[144,896]{1,0:T(8,128)(2,1)S(1)}, u32[]{:S(2)}, u32[]{:S(2)}) collective-permute-start(bf16[144,896]{1,0:T(8,128)(2,1)} %get-tuple-element.29), channel_id=1, source_target_pairs={{0,4},{4,0},{1,5},{5,1},{2,6},{6,2},{3,7},{7,3},{8,12},{12,8},{9,1... | collective-permute-start | bytes 774152 | tf_op jit(solution)/shard_map/ppermute | solution.py:191
  121.8 0.8 copy-start.18
  125.8 8.7 %collective-permute-start.14 = (bf16[144,896]{1,0:T(8,128)(2,1)}, bf16[144,896]{1,0:T(8,128)(2,1)S(1)}, u32[]{:S(2)}, u32[]{:S(2)}) collective-permute-start(bf16[144,896]{1,0:T(8,128)(2,1)} %get-tuple-element.32), channel_id=1, source_target_pairs={{0,4},{4,0},{1,5},{5,1},{2,6},{6,2},{3,7},{7,3},{8,12},{12,8},{9,1... | collective-permute-start | bytes 774152 | tf_op jit(solution)/shard_map/ppermute | solution.py:191
  130.5 3.9 %copy-start.20 = (bf16[144,896]{1,0:T(8,128)(2,1)S(1)}, bf16[144,896]{1,0:T(8,128)(2,1)}, u32[]{:S(2)}) copy-start(bf16[144,896]{1,0:T(8,128)(2,1)} %get-tuple-element.27) | copy-start | bytes 774148
  130.5 0.8 copy-start.17
  134.4 0.9 copy-start.21
  136.3 12.2 %all-to-all-start.2 = ((bf16[4,72,896]{2,1,0:T(8,128)(2,1)}), bf16[4,72,896]{2,1,0:T(8,128)(2,1)S(1)}, u32[]{:S(2)}, u32[]{:S(2)}) async-start(bf16[4,72,896]{2,1,0:T(8,128)(2,1)} %bitcast.7), calls=%async_computation.2 | async-start | bytes 1032192 | tf_op jit(solution)/shard_map/all_to_all | solution.py:193
  148.5 0.8 copy-start.2

commit v2 on v1

v2 whole, which is shorter than its diff:
```python
import functools

import jax
import jax.numpy as jnp
from jax import lax
from jax.experimental import pallas as pl
from jax.experimental.pallas import tpu as pltpu
from jax.sharding import PartitionSpec as P


F32 = jnp.float32
BF16 = jnp.bfloat16
VMEM = pltpu.VMEM
SMEM = pltpu.SMEM


def mm(left, right, dims):
    return lax.dot_general(left, right, (dims, ((), ())), preferred_element_type=F32)


NN = ((1,), (0,))
NT = ((1,), (1,))
TN = ((0,), (0,))


def vm(x):
    return pltpu.with_memory_space_constraint(x, pltpu.VMEM)


def call(body, outs, n_smem, args, raw=()):
    return pl.pallas_call(
        body,
        out_shape=outs,
        in_specs=[pl.BlockSpec(memory_space=SMEM)] * n_smem + [pl.BlockSpec(memory_space=VMEM)] * (len(args) - n_smem),
        out_specs=jax.tree.map(lambda _: pl.BlockSpec(memory_space=VMEM), outs),
        compiler_params=pltpu.CompilerParams(vmem_limit_bytes=16 << 20),
    )(*args[:n_smem], *[a if i in raw else vm(a) for i, a in enumerate(args) if i >= n_smem])


def column(row):
    count = row.shape[1]
    eye = lax.broadcasted_iota(jnp.int32, (count, count), 0) == lax.broadcasted_iota(jnp.int32, (count, count), 1)
    return jnp.sum(jnp.where(eye, row, jnp.zeros_like(row)), axis=1, keepdims=True)


def ranks(ids):
    count = ids.shape[0]
    lanes = lax.broadcasted_iota(jnp.int32, (count, 128), 1)
    onehot = jnp.where(ids == lanes, 1.0, 0.0)
    lower = jnp.where(
        lax.broadcasted_iota(jnp.int32, (count, count), 0) > lax.broadcasted_iota(jnp.int32, (count, count), 1), 1.0, 0.0
    )
    before = mm(lower.astype(BF16), onehot.astype(BF16), NN)
    return jnp.sum(before * onehot, axis=1, keepdims=True).astype(jnp.int32)


def slots(ids, rank, owner, cap):
    places = lax.broadcasted_iota(jnp.int32, (ids.shape[0], cap), 1)
    return jnp.where((ids == owner) & (rank == places), 1.0, 0.0).astype(BF16)


def send_body(n_expert, cap, own_ref, ids_ref, rw_ref, tokens_ref, cot_ref, *outs):
    ids = column(ids_ref[...])
    rank = ranks(ids)
    tokens = tokens_ref[...]
    scaled = (column(rw_ref[...]) * cot_ref[...].astype(F32)).astype(BF16)
    for k in range(n_expert):
        pick = slots(ids, rank, own_ref[0] ^ k, cap)
        outs[k][0, 0] = mm(pick, tokens, TN).astype(BF16)
        outs[k][0, 1] = mm(pick, scaled, TN).astype(BF16)


def side(refs, which):
    return jnp.concatenate([r[j, which] for r in refs for j in range(r.shape[0])], axis=0)


def part_body(half, n, *refs):
    rows, (wg_ref, wu_ref, wd_ref), outs = refs[:n], refs[n:n + 3], refs[n + 3:]
    x, g = side(rows, 0), side(rows, 1)
    parts = (mm(x, wg_ref[...], NN), mm(x, wu_ref[...], NN), mm(g, wd_ref[...], NT))
    size = outs[0].shape[0]
    for i in range(n):
        for j in range(3):
            outs[i][:, j * half:(j + 1) * half] = parts[j][i * size:(i + 1) * size].astype(BF16)


def join_body(p_ref, c_ref, o_ref):
    o_ref[...] = (p_ref[...].astype(F32) + c_ref[...].astype(F32)).astype(BF16)


def act_body(half, s_ref, m_ref, o_ref):
    gate = s_ref[:, :half].astype(F32) + m_ref[:, :half].astype(F32)
    upper = s_ref[:, half:2 * half].astype(F32) + m_ref[:, half:2 * half].astype(F32)
    hgrad = s_ref[:, 2 * half:].astype(F32) + m_ref[:, 2 * half:].astype(F32)
    sigma = jax.nn.sigmoid(gate)
    active = gate * sigma
    o_ref[:, :half] = (hgrad * upper * sigma * (1.0 + gate * (1.0 - sigma))).astype(BF16)
    o_ref[:, half:2 * half] = (hgrad * active).astype(BF16)
    o_ref[:, 2 * half:] = (active * upper).astype(BF16)


def out_body(half, n, *refs):
    acts, (wg_ref, wu_ref, o_ref) = refs[:n], refs[n:]
    a = jnp.concatenate([r[:, :2 * half] for r in acts], axis=0)
    o_ref[...] = (mm(a[:, :half], wg_ref[...], NT) + mm(a[:, half:], wu_ref[...], NT)).astype(BF16)


def wgrad_body(half, n, *refs):
    rows, acts, (gg_ref, gu_ref, gd_ref) = refs[:n], refs[n:2 * n], refs[2 * n:]
    x, g = side(rows, 0), side(rows, 1)
    a = jnp.concatenate([r[...] for r in acts], axis=0)
    gg_ref[0] = mm(x, a[:, :half], TN).astype(BF16)
    gu_ref[0] = mm(x, a[:, half:2 * half], TN).astype(BF16)
    gd_ref[0] = mm(a[:, 2 * half:], g, TN).astype(BF16)


def final_body(n_expert, cap, own_ref, ids_ref, rw_ref, *refs):
    ids = column(ids_ref[...])
    rank = ranks(ids)
    total = None
    for k in range(n_expert):
        term = mm(slots(ids, rank, own_ref[0] ^ k, cap), refs[k][...], NN)
        total = term if total is None else total + term
    refs[n_expert][...] = (column(rw_ref[...]) * total).astype(BF16)


def steps(tokens, cotangent, route_weight, expert_ids, gate_weight, up_weight, down_weight):
    n_expert = lax.axis_size("expert")
    n_rep = lax.axis_size("replica")
    n_seq = lax.axis_size("seq")
    assert n_seq == 4 and n_expert % 4 == 0
    count, quarter = tokens.shape
    half = gate_weight.shape[2]
    cap = -(-(3 * count // (2 * n_expert)) // 8) * 8
    each = n_expert // 4
    z = lax.axis_index("seq")
    is_edge = (z == 0) | (z == n_seq - 1)
    own = lax.axis_index("expert").reshape(1)
    w_gate, w_up, w_down = gate_weight[0], up_weight[0], down_weight[0]
    rw = route_weight.reshape(1, count)
    ids = expert_ids.reshape(1, count)
    keep = lambda *shape: pltpu.VMEM(shape, BF16)

    def swap(x, axis, k):
        return lax.ppermute(x, axis, [(i, i ^ k) for i in range(lax.axis_size(axis))])

    send = call(
        functools.partial(send_body, n_expert, cap), [keep(1, 2, cap, quarter)] * n_expert, 1,
        (own, ids, rw, tokens, cotangent), (1, 2, 3, 4),
    )
    got = [send[0]] + [swap(send[k], "expert", k) for k in range(1, n_expert)]
    rows = {}
    for j in range(4):
        blocks = got[j * each:(j + 1) * each]
        rows[0, j] = blocks[0] if each == 1 else jnp.concatenate(blocks, axis=0)
    for q in range(1, n_rep):
        for j in range(4):
            rows[q, j] = swap(rows[0, j], "replica", q)
    size = each * cap
    parts = {}
    for q in range(n_rep):
        for pair in ((0, 1), (2, 3)):
            done = call(
                functools.partial(part_body, half, 2), [keep(size, 3 * half)] * 2, 0,
                (*[rows[q, j] for j in pair], w_gate, w_up, w_down),
                (2, 3, 4) if (q, pair) == (0, (0, 1)) else (),
            )
            parts[q, pair[0]], parts[q, pair[1]] = done

    waves = [(0, 1), (0, 2), (0, 3)]
    waves += [(q, j) for q in range(1, n_rep) for j in (0, 2, 3, 1)] + [(0, 0)]
    lag = 3
    inward, outward, middle = [(0, 1), (3, 2)], [(1, 0), (2, 3)], [(1, 2), (2, 1)]
    acts, full = {}, {}
    for i in range(len(waves) + lag):
        now = waves[i] if i < len(waves) else None
        old = waves[i - lag] if i >= lag else None
        if old is None:
            came = lax.ppermute(parts[now], "seq", inward)
        elif now is None:
            came = lax.ppermute(acts[old], "seq", outward)
        else:
            came = lax.ppermute(jnp.where(is_edge, parts[now], acts[old]), "seq", inward + outward)
        if now is not None:
            pair = call(join_body, keep(size, 3 * half), 0, (parts[now], came))
            acts[now] = call(
                functools.partial(act_body, half), keep(size, 3 * half), 0,
                (pair, lax.ppermute(pair, "seq", middle)),
            )
        if old is not None:
            full[old] = jnp.where(is_edge, came, acts[old])

    def out(q, pair):
        return call(
            functools.partial(out_body, half, 2), keep(2 * size, quarter), 0,
            (*[full[q, j] for j in pair], w_gate, w_up),
        )

    high, low = out(0, (2, 3)).astype(F32), None
    for q in range(1, n_rep):
        high = high + swap(out(q, (2, 3)), "replica", q).astype(F32)
    low = out(0, (0, 1)).astype(F32)
    for q in range(1, n_rep):
        low = low + swap(out(q, (0, 1)), "replica", q).astype(F32)
    total = [t[k * cap:(k + 1) * cap].astype(BF16) for t in (low, high) for k in range(2 * each)]
    ret = [total[0]] + [swap(total[k], "expert", k) for k in range(1, n_expert)]
    sds = jax.ShapeDtypeStruct
    token_grad = call(
        functools.partial(final_body, n_expert, cap), sds((count, quarter), BF16), 1, (own, ids, rw, *ret)
    )
    gate_grad, up_grad, down_grad = call(
        functools.partial(wgrad_body, half, len(waves)),
        [sds((1, quarter, half), BF16), sds((1, quarter, half), BF16), sds((1, half, quarter), BF16)], 0,
        (*[rows[w] for w in waves], *[full[w] for w in waves]),
    )
    return (token_grad, gate_grad, up_grad, down_grad)


def solution(mesh):
    placed = (
        P(("expert", "replica"), "seq"),
        P(("expert", "replica"), "seq"),
        P(("expert", "replica")),
        P(("expert", "replica"), None),
        P("expert", "seq", "replica"),
        P("expert", "seq", "replica"),
        P("expert", "replica", "seq"),
    )
    return jax.shard_map(
        steps,
        mesh=mesh,
        in_specs=placed,
        out_specs=(
            P(("expert", "replica"), "seq"),
            P("expert", "seq", "replica"),
            P("expert", "seq", "replica"),
            P("expert", "replica", "seq"),
        ),
        check_vma=False,
    )
```

time: 153 us -> 128 us (0.84)
  blocking collectives: 25.6 us -> 0 us
  Pallas kernels: 40.3 us -> 19.5 us
  starting transfers between devices: 28.8 us -> 43.5 us
  waiting for transfers between devices: 44.5 us -> 49.5 us
  local copies, waits for them, and re-layouts: 9.16 us -> 12.8 us
  other arithmetic: 2.47 us -> 0.47 us
    all_to_all x2 -> x0, blocking collectives: 25.6 us -> none  [the longest x1 13.8 us: local(): lax.all_to_all(send_x, 'expert', 0, 0, tiled=True).reshape(rows, quarter)]
    pallas_call x13 -> x27, Pallas kernels: 40.3 us -> 19.5 us  [call(): pl.pallas_call(body, out_shape=outs, in_specs=[pl.BlockSpec(memory_space=...]
    ppermute x15 -> x31, starting transfers between devices: 25.4 us -> 43.5 us  [the longest x5 15.3 us: steps(): lax.ppermute(jnp.where(is_edge, parts[now], acts[old]), 'seq', inward + o...]
    ppermute x15 -> x31, waiting for transfers between devices: 41.2 us -> 49.5 us  [the longest x12 24.2 us: swap(): lax.ppermute(x, axis, [(i, i ^ k) for i in range(lax.axis_size(axis))])]
    unnamed x45 -> x40, local copies, waits for them, and re-layouts: 9.16 us -> 12.8 us
    all_to_all x1 -> x0, starting transfers between devices: 3.47 us -> none  [local(): returned = lax.all_to_all(back_rows, 'expert', 0, 0, tiled=True)]
    all_to_all x1 -> x0, waiting for transfers between devices: 3.31 us -> none  [local(): returned = lax.all_to_all(back_rows, 'expert', 0, 0, tiled=True)]
    convert_element_type x6 -> x0, other arithmetic: 1.58 us -> none  [the longest x4 1.44 us: local(): sums[i] = (parts[i].astype(F32) + got.astype(F32)).astype(BF16)]
  transfers between devices with their start and end apart: 16 -> 31, of which waited for: 7 -> 15; matrix products, arithmetic and copies ran while one was open for 1% -> 0% of each run, Pallas kernels for 20% -> 13%
where the time goes in v2:
time: 128 us; the launch traced here: 127 us
  waiting for transfers between devices  49.5 us (39%)
  starting transfers between devices  43.5 us (34%)
  Pallas kernels  19.5 us (15%)
  local copies, waits for them, and re-layouts  12.8 us (10%)
    ppermute x12, waiting for transfers between devices, swap(): lax.ppermute(x, axis, [(i, i ^ k) for i in range(lax.axis_size(axis))])  24.2 us
    pallas_call x27, Pallas kernels, call(): pl.pallas_call(body, out_shape=outs, in_specs=[pl.BlockSpec(memory_space=...  19.5 us
    ppermute x5, starting transfers between devices, steps(): lax.ppermute(jnp.where(is_edge, parts[now], acts[old]), 'seq', inward + o...  15.3 us
    ppermute x5, waiting for transfers between devices, steps(): lax.ppermute(jnp.where(is_edge, parts[now], acts[old]), 'seq', inward + o...  15 us
    unnamed x40, local copies, waits for them, and re-layouts  12.8 us
    ppermute x12, starting transfers between devices, swap(): lax.ppermute(x, axis, [(i, i ^ k) for i in range(lax.axis_size(axis))])  12 us
    ppermute x3, waiting for transfers between devices, steps(): came = lax.ppermute(acts[old], 'seq', outward)  6.86 us
    ppermute x3, starting transfers between devices, steps(): came = lax.ppermute(parts[now], 'seq', inward)  6.23 us
  transfers between devices with their start and end apart: 31, of which 15 were waited for; matrix products, arithmetic and copies ran while one was open for 0% of the time, Pallas kernels for 13%

profile of v2, /device:TPU:0, one launch (start us, length us, event | category | flops | bytes accessed | tf_op | source)
XLA Modules:
  0.0 127.0 jit_solution(12535167107718733911)
XLA Ops:
  1.3 1.0 copy-done.8
  2.3 1.0 copy-done.9
  3.3 1.0 shard_map.102
  4.3 3.1 %collective-permute-start.1 = (bf16[1,2,72,896]{3,2,1,0:T(8,128)(2,1)S(1)}, bf16[1,2,72,896]{3,2,1,0:T(8,128)(2,1)S(1)}, u32[]{:S(2)}, u32[]{:S(2)}) collective-permute-start(bf16[1,2,72,896]{3,2,1,0:T(8,128)(2,1)S(1)} %get-tuple-element.22), channel_id=1, source_target_pairs={{0,16},{8,24},{16,0},{24,8},{1,17},{9,25},{17,1},{25,9},{2,18},{10... | collective-permute-start | bytes 774152 | tf_op jit(solution)/shard_map/ppermute | solution.py:145
  7.6 6.9 %collective-permute-done.1.refs_0_.refs_1_ = bf16[1,2,72,896]{3,2,1,0:T(8,128)(2,1)S(1)} collective-permute-done((bf16[1,2,72,896]{3,2,1,0:T(8,128)(2,1)S(1)}, bf16[1,2,72,896]{3,2,1,0:T(8,128)(2,1)S(1)}, u32[]{:S(2)}, u32[]{:S(2)}) %collective-permute-start.1) | collective-permute-done | bytes 258080 | tf_op jit(solution)/shard_map/ppermute | solution.py:145
  14.4 3.9 %collective-permute-done.3.refs_1_.refs_2_ = bf16[1,2,72,896]{3,2,1,0:T(8,128)(2,1)S(1)} collective-permute-done((bf16[1,2,72,896]{3,2,1,0:T(8,128)(2,1)S(1)}, bf16[1,2,72,896]{3,2,1,0:T(8,128)(2,1)S(1)}, u32[]{:S(2)}, u32[]{:S(2)}) %collective-permute-start.3) | collective-permute-done | bytes 258080 | tf_op jit(solution)/shard_map/ppermute | solution.py:145
  18.4 1.2 copy-done
  19.5 1.2 copy-done.2
  20.7 1.2 copy-done.4
  22.7 3.5 %collective-permute-start.23 = (bf16[72,1536]{1,0:T(8,128)(2,1)S(1)}, bf16[72,1536]{1,0:T(8,128)(2,1)S(1)}, u32[]{:S(2)}, u32[]{:S(2)}) collective-permute-start(bf16[72,1536]{1,0:T(8,128)(2,1)S(1)} %get-tuple-element.30.p_ref), channel_id=1, source_target_pairs={{0,1},{3,2},{4,5},{7,6},{8,9},{11,10},{12,13},{15,14},{16,17},{19,... | collective-permute-start | bytes 663560 | tf_op jit(solution)/shard_map/ppermute | solution.py:179
  26.2 1.3 %collective-permute-start.5 = (bf16[72,1536]{1,0:T(8,128)(2,1)S(1)}, bf16[72,1536]{1,0:T(8,128)(2,1)S(1)}, u32[]{:S(2)}, u32[]{:S(2)}) collective-permute-start(bf16[72,1536]{1,0:T(8,128)(2,1)S(1)} %get-tuple-element.25.p_ref), channel_id=1, source_target_pairs={{0,1},{3,2},{4,5},{7,6},{8,9},{11,10},{12,13},{15,14},{16,17},{19,... | collective-permute-start | bytes 663560 | tf_op jit(solution)/shard_map/ppermute | solution.py:179
  27.5 1.7 %shard_map.103 = (bf16[72,1536]{1,0:T(8,128)(2,1)S(1)}, bf16[72,1536]{1,0:T(8,128)(2,1)S(1)}) custom-call(bf16[1,2,72,896]{3,2,1,0:T(8,128)(2,1)S(1)} %get-tuple-element.19.refs_0_.refs_7_, bf16[1,2,72,896]{3,2,1,0:T(8,128)(2,1)} %collective-permute-done.refs_1_.refs_0_, bf16[896,512]{1,0:T(8,128)(2,1)S(1)} %bitcast.7, bf16[896,512]{1,0:T(8,128)(2,1)S(1)} %bitcast.15, ...), custom_call_target="tpu_custom_call" | custom-call | tf_op jit(solution)/shard_map/pallas_call | solution.py:31
  29.3 1.4 %collective-permute-start.14 = (bf16[72,1536]{1,0:T(8,128)(2,1)S(1)}, bf16[72,1536]{1,0:T(8,128)(2,1)S(1)}, u32[]{:S(2)}, u32[]{:S(2)}) collective-permute-start(bf16[72,1536]{1,0:T(8,128)(2,1)S(1)} %get-tuple-element.27.p_ref), channel_id=1, source_target_pairs={{0,1},{3,2},{4,5},{7,6},{8,9},{11,10},{12,13},{15,14},{16,17},{19,... | collective-permute-start | bytes 663560 | tf_op jit(solution)/shard_map/ppermute | solution.py:179
  31.4 1.5 %collective-permute-start.2 = (bf16[1,2,72,896]{3,2,1,0:T(8,128)(2,1)S(1)}, bf16[1,2,72,896]{3,2,1,0:T(8,128)(2,1)}, u32[]{:S(2)}, u32[]{:S(2)}) collective-permute-start(bf16[1,2,72,896]{3,2,1,0:T(8,128)(2,1)S(1)} %collective-permute-done.1.refs_0_.refs_1_), channel_id=1, source_target_pairs={{0,4},{4,0},{1,5},{5,1},{2,6},{6,2},{3,7},{7,3},{8,12},{12,8},{9,1... | collective-permute-start | bytes 774152 | tf_op jit(solution)/shard_map/ppermute | solution.py:145
  33.5 1.5 %collective-permute-start.12 = (bf16[1,2,72,896]{3,2,1,0:T(8,128)(2,1)S(1)}, bf16[1,2,72,896]{3,2,1,0:T(8,128)(2,1)}, u32[]{:S(2)}, u32[]{:S(2)}) collective-permute-start(bf16[1,2,72,896]{3,2,1,0:T(8,128)(2,1)S(1)} %get-tuple-element.19.refs_0_.refs_7_), channel_id=1, source_target_pairs={{0,4},{4,0},{1,5},{5,1},{2,6},{6,2},{3,7},{7,3},{8,12},{12,8},{9,1... | collective-permute-start | bytes 774152 | tf_op jit(solution)/shard_map/ppermute | solution.py:145
  35.0 1.8 %collective-permute-done.5.c_ref = bf16[72,1536]{1,0:T(8,128)(2,1)S(1)} collective-permute-done((bf16[72,1536]{1,0:T(8,128)(2,1)S(1)}, bf16[72,1536]{1,0:T(8,128)(2,1)S(1)}, u32[]{:S(2)}, u32[]{:S(2)}) %collective-permute-start.5) | collective-permute-done | bytes 221216 | tf_op jit(solution)/shard_map/ppermute | solution.py:179
  37.4 1.5 %collective-permute-start.13 = (bf16[1,2,72,896]{3,2,1,0:T(8,128)(2,1)}, bf16[1,2,72,896]{3,2,1,0:T(8,128)(2,1)}, u32[]{:S(2)}, u32[]{:S(2)}) collective-permute-start(bf16[1,2,72,896]{3,2,1,0:T(8,128)(2,1)} %collective-permute-done.refs_1_.refs_0_), channel_id=1, source_target_pairs={{0,4},{4,0},{1,5},{5,1},{2,6},{6,2},{3,7},{7,3},{8,12},{12,8},{9,1... | collective-permute-start | bytes 774152 | tf_op jit(solution)/shard_map/ppermute | solution.py:145
  39.7 1.6 %collective-permute-done.14.c_ref = bf16[72,1536]{1,0:T(8,128)(2,1)S(1)} collective-permute-done((bf16[72,1536]{1,0:T(8,128)(2,1)S(1)}, bf16[72,1536]{1,0:T(8,128)(2,1)S(1)}, u32[]{:S(2)}, u32[]{:S(2)}) %collective-permute-start.14) | collective-permute-done | bytes 221216 | tf_op jit(solution)/shard_map/ppermute | solution.py:179
  42.0 1.3 %collective-permute-start.24 = (bf16[72,1536]{1,0:T(8,128)(2,1)}, bf16[72,1536]{1,0:T(8,128)(2,1)}, u32[]{:S(2)}, u32[]{:S(2)}) collective-permute-start(bf16[72,1536]{1,0:T(8,128)(2,1)} %shard_map.121.s_ref), channel_id=1, source_target_pairs={{1,2},{2,1},{5,6},{6,5},{9,10},{10,9},{13,14},{14,13},{17,18},{18,... | collective-permute-start | bytes 663560 | tf_op jit(solution)/shard_map/ppermute | solution.py:188
  43.3 0.9 copy-done.11
  44.2 0.9 copy-done.13
  45.3 0.9 copy-done.15
  46.2 0.9 copy-done.17
  48.6 1.8 %shard_map.104 = (bf16[72,1536]{1,0:T(8,128)(2,1)S(1)}, bf16[72,1536]{1,0:T(8,128)(2,1)S(1)}) custom-call(bf16[1,2,72,896]{3,2,1,0:T(8,128)(2,1)} %collective-permute-done.2.refs_0_.refs_4_, bf16[1,2,72,896]{3,2,1,0:T(8,128)(2,1)} %collective-permute-done.4.refs_1_.refs_5_, bf16[896,512]{1,0:T(8,128)(2,1)S(1)} %bitcast.8, bf16[896,512]{1,0:T(8,128)(2,1)S(1)} %bitcast.16, ...), custom_call_target="tpu_custom_call" | custom-call | tf_op jit(solution)/shard_map/pallas_call | solution.py:31
  50.4 1.3 %collective-permute-done.12.refs_0_.refs_3_ = bf16[1,2,72,896]{3,2,1,0:T(8,128)(2,1)} collective-permute-done((bf16[1,2,72,896]{3,2,1,0:T(8,128)(2,1)S(1)}, bf16[1,2,72,896]{3,2,1,0:T(8,128)(2,1)}, u32[]{:S(2)}, u32[]{:S(2)}) %collective-permute-start.12) | collective-permute-done | bytes 258080 | tf_op jit(solution)/shard_map/ppermute | solution.py:145
  51.7 5.1 %collective-permute-done.13.refs_1_.refs_6_ = bf16[1,2,72,896]{3,2,1,0:T(8,128)(2,1)} collective-permute-done((bf16[1,2,72,896]{3,2,1,0:T(8,128)(2,1)}, bf16[1,2,72,896]{3,2,1,0:T(8,128)(2,1)}, u32[]{:S(2)}, u32[]{:S(2)}) %collective-permute-start.13) | collective-permute-done | bytes 258080 | tf_op jit(solution)/shard_map/ppermute | solution.py:145
  56.8 1.8 %shard_map.112 = (bf16[72,1536]{1,0:T(8,128)(2,1)S(1)}, bf16[72,1536]{1,0:T(8,128)(2,1)S(1)}) custom-call(bf16[1,2,72,896]{3,2,1,0:T(8,128)(2,1)} %collective-permute-done.12.refs_0_.refs_3_, bf16[1,2,72,896]{3,2,1,0:T(8,128)(2,1)} %collective-permute-done.13.refs_1_.refs_6_, bf16[896,512]{1,0:T(8,128)(2,1)S(1)} %bitcast.9, bf16[896,512]{1,0:T(8,128)(2,1)S(1)} %bitcast.17, ...), custom_call_target="tpu_custom_call" | custom-call | tf_op jit(solution)/shard_map/pallas_call | solution.py:31
  58.6 1.2 shard_map.122
  59.8 2.9 %collective-permute-start.25 = (bf16[72,1536]{1,0:T(8,128)(2,1)S(1)}, bf16[72,1536]{1,0:T(8,128)(2,1)S(1)}, u32[]{:S(2)}, u32[]{:S(2)}) collective-permute-start(bf16[72,1536]{1,0:T(8,128)(2,1)S(1)} %broadcast_select_fusion.3), channel_id=1, source_target_pairs={{0,1},{3,2},{1,0},{2,3},{4,5},{7,6},{5,4},{6,7},{8,9},{11,10},{9,8... | collective-permute-start | bytes 663560 | tf_op jit(solution)/shard_map/ppermute | solution.py:183
  63.1 2.7 %collective-permute-start.16 = (bf16[72,1536]{1,0:T(8,128)(2,1)S(1)}, bf16[72,1536]{1,0:T(8,128)(2,1)S(1)}, u32[]{:S(2)}, u32[]{:S(2)}) collective-permute-start(bf16[72,1536]{1,0:T(8,128)(2,1)S(1)} %broadcast_select_fusion.9), channel_id=1, source_target_pairs={{0,1},{3,2},{1,0},{2,3},{4,5},{7,6},{5,4},{6,7},{8,9},{11,10},{9,8... | collective-permute-start | bytes 663560 | tf_op jit(solution)/shard_map/ppermute | solution.py:183
  65.8 3.2 %collective-permute-done.25.c_ref = bf16[72,1536]{1,0:T(8,128)(2,1)S(1)} collective-permute-done((bf16[72,1536]{1,0:T(8,128)(2,1)S(1)}, bf16[72,1536]{1,0:T(8,128)(2,1)S(1)}, u32[]{:S(2)}, u32[]{:S(2)}) %collective-permute-start.25) | collective-permute-done | bytes 221216 | tf_op jit(solution)/shard_map/ppermute | solution.py:183
  69.7 4.0 %collective-permute-done.7.c_ref = bf16[72,1536]{1,0:T(8,128)(2,1)S(1)} collective-permute-done((bf16[72,1536]{1,0:T(8,128)(2,1)S(1)}, bf16[72,1536]{1,0:T(8,128)(2,1)S(1)}, u32[]{:S(2)}, u32[]{:S(2)}) %collective-permute-start.7) | collective-permute-done | bytes 221216 | tf_op jit(solution)/shard_map/ppermute | solution.py:183
  74.4 2.5 %collective-permute-done.16.c_ref = bf16[72,1536]{1,0:T(8,128)(2,1)S(1)} collective-permute-done((bf16[72,1536]{1,0:T(8,128)(2,1)S(1)}, bf16[72,1536]{1,0:T(8,128)(2,1)S(1)}, u32[]{:S(2)}, u32[]{:S(2)}) %collective-permute-start.16) | collective-permute-done | bytes 221216 | tf_op jit(solution)/shard_map/ppermute | solution.py:183
  78.7 7.2 %collective-permute-start.9 = (bf16[72,1536]{1,0:T(8,128)(2,1)S(1)}, bf16[72,1536]{1,0:T(8,128)(2,1)S(1)}, u32[]{:S(2)}, u32[]{:S(2)}) collective-permute-start(bf16[72,1536]{1,0:T(8,128)(2,1)S(1)} %broadcast_select_fusion.11), channel_id=1, source_target_pairs={{0,1},{3,2},{1,0},{2,3},{4,5},{7,6},{5,4},{6,7},{8,9},{11,10},{9,8... | collective-permute-start | bytes 663560 | tf_op jit(solution)/shard_map/ppermute | solution.py:183
  86.0 2.5 %collective-permute-start.18 = (bf16[72,1536]{1,0:T(8,128)(2,1)S(1)}, bf16[72,1536]{1,0:T(8,128)(2,1)S(1)}, u32[]{:S(2)}, u32[]{:S(2)}) collective-permute-start(bf16[72,1536]{1,0:T(8,128)(2,1)S(1)} %broadcast_select_fusion.7), channel_id=1, source_target_pairs={{0,1},{3,2},{1,0},{2,3},{4,5},{7,6},{5,4},{6,7},{8,9},{11,10},{9,8... | collective-permute-start | bytes 663560 | tf_op jit(solution)/shard_map/ppermute | solution.py:183
  89.5 1.3 %collective-permute-start.27 = (bf16[72,1536]{1,0:T(8,128)(2,1)S(1)}, bf16[72,1536]{1,0:T(8,128)(2,1)S(1)}, u32[]{:S(2)}, u32[]{:S(2)}) collective-permute-start(bf16[72,1536]{1,0:T(8,128)(2,1)S(1)} %shard_map.125), channel_id=1, source_target_pairs={{1,0},{2,3},{5,4},{6,7},{9,8},{10,11},{13,12},{14,15},{17,16},{18,... | collective-permute-start | bytes 663560 | tf_op jit(solution)/shard_map/ppermute | solution.py:181
  90.8 1.3 %collective-permute-done.9.c_ref = bf16[72,1536]{1,0:T(8,128)(2,1)S(1)} collective-permute-done((bf16[72,1536]{1,0:T(8,128)(2,1)S(1)}, bf16[72,1536]{1,0:T(8,128)(2,1)S(1)}, u32[]{:S(2)}, u32[]{:S(2)}) %collective-permute-start.9) | collective-permute-done | bytes 221216 | tf_op jit(solution)/shard_map/ppermute | solution.py:183
  92.8 4.0 %collective-permute-done.18.c_ref = bf16[72,1536]{1,0:T(8,128)(2,1)S(1)} collective-permute-done((bf16[72,1536]{1,0:T(8,128)(2,1)S(1)}, bf16[72,1536]{1,0:T(8,128)(2,1)S(1)}, u32[]{:S(2)}, u32[]{:S(2)}) %collective-permute-start.18) | collective-permute-done | bytes 221216 | tf_op jit(solution)/shard_map/ppermute | solution.py:183
  97.6 1.7 %collective-permute-done.27 = bf16[72,1536]{1,0:T(8,128)(2,1)S(1)} collective-permute-done((bf16[72,1536]{1,0:T(8,128)(2,1)S(1)}, bf16[72,1536]{1,0:T(8,128)(2,1)S(1)}, u32[]{:S(2)}, u32[]{:S(2)}) %collective-permute-start.27) | collective-permute-done | bytes 221216 | tf_op jit(solution)/shard_map/ppermute | solution.py:181
  100.0 1.5 %collective-permute-start.28 = (bf16[144,896]{1,0:T(8,128)(2,1)S(1)}, bf16[144,896]{1,0:T(8,128)(2,1)S(1)}, u32[]{:S(2)}, u32[]{:S(2)}) collective-permute-start(bf16[144,896]{1,0:T(8,128)(2,1)S(1)} %shard_map.126), channel_id=1, source_target_pairs={{0,4},{4,0},{1,5},{5,1},{2,6},{6,2},{3,7},{7,3},{8,12},{12,8},{9,1... | collective-permute-start | bytes 774152 | tf_op jit(solution)/shard_map/ppermute | solution.py:145
  101.7 1.3 %collective-permute-start.11 = (bf16[72,1536]{1,0:T(8,128)(2,1)S(1)}, bf16[72,1536]{1,0:T(8,128)(2,1)S(1)}, u32[]{:S(2)}, u32[]{:S(2)}) collective-permute-start(bf16[72,1536]{1,0:T(8,128)(2,1)S(1)} %shard_map.111), channel_id=1, source_target_pairs={{1,0},{2,3},{5,4},{6,7},{9,8},{10,11},{13,12},{14,15},{17,16},{18,... | collective-permute-start | bytes 663560 | tf_op jit(solution)/shard_map/ppermute | solution.py:181
  103.2 1.3 %collective-permute-start.20 = (bf16[72,1536]{1,0:T(8,128)(2,1)S(1)}, bf16[72,1536]{1,0:T(8,128)(2,1)S(1)}, u32[]{:S(2)}, u32[]{:S(2)}) collective-permute-start(bf16[72,1536]{1,0:T(8,128)(2,1)S(1)} %shard_map.119), channel_id=1, source_target_pairs={{1,0},{2,3},{5,4},{6,7},{9,8},{10,11},{13,12},{14,15},{17,16},{18,... | collective-permute-start | bytes 663560 | tf_op jit(solution)/shard_map/ppermute | solution.py:181
  104.5 2.0 %collective-permute-done.28 = bf16[144,896]{1,0:T(8,128)(2,1)S(1)} collective-permute-done((bf16[144,896]{1,0:T(8,128)(2,1)S(1)}, bf16[144,896]{1,0:T(8,128)(2,1)S(1)}, u32[]{:S(2)}, u32[]{:S(2)}) %collective-permute-start.28) | collective-permute-done | bytes 258080 | tf_op jit(solution)/shard_map/ppermute | solution.py:145
  106.5 1.5 %collective-permute-start.29 = (bf16[72,896]{1,0:T(8,128)(2,1)S(1)}, bf16[72,896]{1,0:T(8,128)(2,1)S(1)}, u32[]{:S(2)}, u32[]{:S(2)}) collective-permute-start(bf16[72,896]{1,0:T(8,128)(2,1)S(1)} %get-tuple-element.35), channel_id=1, source_target_pairs={{0,16},{8,24},{16,0},{24,8},{1,17},{9,25},{17,1},{25,9},{2,18},{10... | collective-permute-start | bytes 387080 | tf_op jit(solution)/shard_map/ppermute | solution.py:145
  108.1 5.2 %collective-permute-done.20 = bf16[72,1536]{1,0:T(8,128)(2,1)S(1)} collective-permute-done((bf16[72,1536]{1,0:T(8,128)(2,1)S(1)}, bf16[72,1536]{1,0:T(8,128)(2,1)S(1)}, u32[]{:S(2)}, u32[]{:S(2)}) %collective-permute-start.20) | collective-permute-done | bytes 221216 | tf_op jit(solution)/shard_map/ppermute | solution.py:181
  115.3 5.0 %collective-permute-done.21 = bf16[144,896]{1,0:T(8,128)(2,1)S(1)} collective-permute-done((bf16[144,896]{1,0:T(8,128)(2,1)S(1)}, bf16[144,896]{1,0:T(8,128)(2,1)S(1)}, u32[]{:S(2)}, u32[]{:S(2)}) %collective-permute-start.21) | collective-permute-done | bytes 258080 | tf_op jit(solution)/shard_map/ppermute | solution.py:145
  120.6 4.8 %shard_map.128 = (bf16[1,896,512]{2,1,0:T(8,128)(2,1)}, bf16[1,896,512]{2,1,0:T(8,128)(2,1)}, bf16[1,512,896]{2,1,0:T(8,128)(2,1)}) custom-call(bf16[1,2,72,896]{3,2,1,0:T(8,128)(2,1)} %collective-permute-done.refs_1_.refs_0_, bf16[1,2,72,896]{3,2,1,0:T(8,128)(2,1)S(1)} %collective-permute-done.1.refs_0_.refs_1_, ...), custom_call_target="tpu_custom_call" | custom-call | tf_op jit(solution)/shard_map/pallas_call | solution.py:31
  125.4 1.6 %shard_map.127 = bf16[192,896]{1,0:T(8,128)(2,1)} custom-call(s32[1]{0:T(128)} %bitcast.own_ref, s32[1,192]{1,0:T(1,128)S(1)} %bitcast.27, f32[1,192]{1,0:T(1,128)S(1)} %bitcast.29, bf16[72,896]{1,0:T(8,128)(2,1)S(1)} %get-tuple-element.37.refs_0_, bf16[72,896]{1,0:T(8,128)(2,1)S(1)} %collective-permute-done.22.refs_1_, ...), custom_call_target="tpu_custom_call" | custom-call | tf_op jit(solution)/shard_map/pallas_call | solution.py:31
  (98 shorter events, 15.9 us)
Async XLA Ops:
  1.3 1.0 copy-start.8
  2.3 1.0 copy-start.9
  4.3 10.1 %collective-permute-start.1 = (bf16[1,2,72,896]{3,2,1,0:T(8,128)(2,1)S(1)}, bf16[1,2,72,896]{3,2,1,0:T(8,128)(2,1)S(1)}, u32[]{:S(2)}, u32[]{:S(2)}) collective-permute-start(bf16[1,2,72,896]{3,2,1,0:T(8,128)(2,1)S(1)} %get-tuple-element.22), channel_id=1, source_target_pairs={{0,16},{8,24},{16,0},{24,8},{1,17},{9,25},{17,1},{25,9},{2,18},{10... | collective-permute-start | bytes 774152 | tf_op jit(solution)/shard_map/ppermute | solution.py:145
  7.4 11.0 %collective-permute-start.3 = (bf16[1,2,72,896]{3,2,1,0:T(8,128)(2,1)S(1)}, bf16[1,2,72,896]{3,2,1,0:T(8,128)(2,1)S(1)}, u32[]{:S(2)}, u32[]{:S(2)}) collective-permute-start(bf16[1,2,72,896]{3,2,1,0:T(8,128)(2,1)S(1)} %get-tuple-element.23), channel_id=1, source_target_pairs={{0,24},{8,16},{16,8},{24,0},{1,25},{9,17},{17,9},{25,1},{2,26},{10... | collective-permute-start | bytes 774152 | tf_op jit(solution)/shard_map/ppermute | solution.py:145
  7.4 20.2 %collective-permute-start = (bf16[1,2,72,896]{3,2,1,0:T(8,128)(2,1)S(1)}, bf16[1,2,72,896]{3,2,1,0:T(8,128)(2,1)}, u32[]{:S(2)}, u32[]{:S(2)}) collective-permute-start(bf16[1,2,72,896]{3,2,1,0:T(8,128)(2,1)S(1)} %get-tuple-element.20), channel_id=1, source_target_pairs={{0,8},{8,0},{16,24},{24,16},{1,9},{9,1},{17,25},{25,17},{2,10},{10... | collective-permute-start | bytes 774152 | tf_op jit(solution)/shard_map/ppermute | solution.py:145
  18.4 1.2 copy-start
  19.5 1.2 copy-start.2
  20.7 1.2 copy-start.4
  21.9 5.6 %copy-start.1 = (bf16[1,896,512]{2,1,0:T(8,128)(2,1)S(1)}, bf16[1,896,512]{2,1,0:T(8,128)(2,1)}, u32[]{:S(2)}) copy-start(bf16[1,896,512]{2,1,0:T(8,128)(2,1)} %param.11) | copy-start | bytes 2752516
  22.7 6.6 %copy-start.10 = (bf16[72,1536]{1,0:T(8,128)(2,1)}, bf16[72,1536]{1,0:T(8,128)(2,1)S(1)}, u32[]{:S(2)}) copy-start(bf16[72,1536]{1,0:T(8,128)(2,1)S(1)} %get-tuple-element.25.p_ref) | copy-start | bytes 663556
  22.7 10.8 %collective-permute-start.23 = (bf16[72,1536]{1,0:T(8,128)(2,1)S(1)}, bf16[72,1536]{1,0:T(8,128)(2,1)S(1)}, u32[]{:S(2)}, u32[]{:S(2)}) collective-permute-start(bf16[72,1536]{1,0:T(8,128)(2,1)S(1)} %get-tuple-element.30.p_ref), channel_id=1, source_target_pairs={{0,1},{3,2},{4,5},{7,6},{8,9},{11,10},{12,13},{15,14},{16,17},{19,... | collective-permute-start | bytes 663560 | tf_op jit(solution)/shard_map/ppermute | solution.py:179
  26.2 10.5 %collective-permute-start.5 = (bf16[72,1536]{1,0:T(8,128)(2,1)S(1)}, bf16[72,1536]{1,0:T(8,128)(2,1)S(1)}, u32[]{:S(2)}, u32[]{:S(2)}) collective-permute-start(bf16[72,1536]{1,0:T(8,128)(2,1)S(1)} %get-tuple-element.25.p_ref), channel_id=1, source_target_pairs={{0,1},{3,2},{4,5},{7,6},{8,9},{11,10},{12,13},{15,14},{16,17},{19,... | collective-permute-start | bytes 663560 | tf_op jit(solution)/shard_map/ppermute | solution.py:179
  29.3 10.4 %copy-start.6 = (bf16[72,1536]{1,0:T(8,128)(2,1)}, bf16[72,1536]{1,0:T(8,128)(2,1)S(1)}, u32[]{:S(2)}) copy-start(bf16[72,1536]{1,0:T(8,128)(2,1)S(1)} %get-tuple-element.21.p_ref) | copy-start | bytes 663556
  29.3 19.3 %copy-start.3 = (bf16[1,896,512]{2,1,0:T(8,128)(2,1)S(1)}, bf16[1,896,512]{2,1,0:T(8,128)(2,1)}, u32[]{:S(2)}) copy-start(bf16[1,896,512]{2,1,0:T(8,128)(2,1)} %param.12) | copy-start | bytes 2752516
  29.3 19.3 %copy-start.5 = (bf16[1,512,896]{2,1,0:T(8,128)(2,1)S(1)}, bf16[1,512,896]{2,1,0:T(8,128)(2,1)}, u32[]{:S(2)}) copy-start(bf16[1,512,896]{2,1,0:T(8,128)(2,1)} %param.13) | copy-start | bytes 2752516
  29.3 12.0 %collective-permute-start.14 = (bf16[72,1536]{1,0:T(8,128)(2,1)S(1)}, bf16[72,1536]{1,0:T(8,128)(2,1)S(1)}, u32[]{:S(2)}, u32[]{:S(2)}) collective-permute-start(bf16[72,1536]{1,0:T(8,128)(2,1)S(1)} %get-tuple-element.27.p_ref), channel_id=1, source_target_pairs={{0,1},{3,2},{4,5},{7,6},{8,9},{11,10},{12,13},{15,14},{16,17},{19,... | collective-permute-start | bytes 663560 | tf_op jit(solution)/shard_map/ppermute | solution.py:179
  30.7 0.7 copy-start.14
  31.4 15.7 %collective-permute-start.2 = (bf16[1,2,72,896]{3,2,1,0:T(8,128)(2,1)S(1)}, bf16[1,2,72,896]{3,2,1,0:T(8,128)(2,1)}, u32[]{:S(2)}, u32[]{:S(2)}) collective-permute-start(bf16[1,2,72,896]{3,2,1,0:T(8,128)(2,1)S(1)} %collective-permute-done.1.refs_0_.refs_1_), channel_id=1, source_target_pairs={{0,4},{4,0},{1,5},{5,1},{2,6},{6,2},{3,7},{7,3},{8,12},{12,8},{9,1... | collective-permute-start | bytes 774152 | tf_op jit(solution)/shard_map/ppermute | solution.py:145
  32.9 14.9 %collective-permute-start.4 = (bf16[1,2,72,896]{3,2,1,0:T(8,128)(2,1)S(1)}, bf16[1,2,72,896]{3,2,1,0:T(8,128)(2,1)}, u32[]{:S(2)}, u32[]{:S(2)}) collective-permute-start(bf16[1,2,72,896]{3,2,1,0:T(8,128)(2,1)S(1)} %collective-permute-done.3.refs_1_.refs_2_), channel_id=1, source_target_pairs={{0,4},{4,0},{1,5},{5,1},{2,6},{6,2},{3,7},{7,3},{8,12},{12,8},{9,1... | collective-permute-start | bytes 774152 | tf_op jit(solution)/shard_map/ppermute | solution.py:145
  33.5 18.2 %collective-permute-start.12 = (bf16[1,2,72,896]{3,2,1,0:T(8,128)(2,1)S(1)}, bf16[1,2,72,896]{3,2,1,0:T(8,128)(2,1)}, u32[]{:S(2)}, u32[]{:S(2)}) collective-permute-start(bf16[1,2,72,896]{3,2,1,0:T(8,128)(2,1)S(1)} %get-tuple-element.19.refs_0_.refs_7_), channel_id=1, source_target_pairs={{0,4},{4,0},{1,5},{5,1},{2,6},{6,2},{3,7},{7,3},{8,12},{12,8},{9,1... | collective-permute-start | bytes 774152 | tf_op jit(solution)/shard_map/ppermute | solution.py:145
  36.7 0.7 copy-start.12
  37.4 19.3 %collective-permute-start.13 = (bf16[1,2,72,896]{3,2,1,0:T(8,128)(2,1)}, bf16[1,2,72,896]{3,2,1,0:T(8,128)(2,1)}, u32[]{:S(2)}, u32[]{:S(2)}) collective-permute-start(bf16[1,2,72,896]{3,2,1,0:T(8,128)(2,1)} %collective-permute-done.refs_1_.refs_0_), channel_id=1, source_target_pairs={{0,4},{4,0},{1,5},{5,1},{2,6},{6,2},{3,7},{7,3},{8,12},{12,8},{9,1... | collective-permute-start | bytes 774152 | tf_op jit(solution)/shard_map/ppermute | solution.py:145
  42.0 16.6 %collective-permute-start.24 = (bf16[72,1536]{1,0:T(8,128)(2,1)}, bf16[72,1536]{1,0:T(8,128)(2,1)}, u32[]{:S(2)}, u32[]{:S(2)}) collective-permute-start(bf16[72,1536]{1,0:T(8,128)(2,1)} %shard_map.121.s_ref), channel_id=1, source_target_pairs={{1,2},{2,1},{5,6},{6,5},{9,10},{10,9},{13,14},{14,13},{17,18},{18,... | collective-permute-start | bytes 663560 | tf_op jit(solution)/shard_map/ppermute | solution.py:188
  43.3 0.9 copy-start.11
  44.2 0.9 copy-start.13
  45.2 0.9 copy-start.15
  46.2 0.9 copy-start.17
  47.2 15.5 %collective-permute-start.6 = (bf16[72,1536]{1,0:T(8,128)(2,1)S(1)}, bf16[72,1536]{1,0:T(8,128)(2,1)S(1)}, u32[]{:S(2)}, u32[]{:S(2)}) collective-permute-start(bf16[72,1536]{1,0:T(8,128)(2,1)S(1)} %shard_map.106.s_ref), channel_id=1, source_target_pairs={{1,2},{2,1},{5,6},{6,5},{9,10},{10,9},{13,14},{14,13},{17,18},{18,... | collective-permute-start | bytes 663560 | tf_op jit(solution)/shard_map/ppermute | solution.py:188
  47.9 15.1 %collective-permute-start.15 = (bf16[72,1536]{1,0:T(8,128)(2,1)S(1)}, bf16[72,1536]{1,0:T(8,128)(2,1)S(1)}, u32[]{:S(2)}, u32[]{:S(2)}) collective-permute-start(bf16[72,1536]{1,0:T(8,128)(2,1)S(1)} %shard_map.113.s_ref), channel_id=1, source_target_pairs={{1,2},{2,1},{5,6},{6,5},{9,10},{10,9},{13,14},{14,13},{17,18},{18,... | collective-permute-start | bytes 663560 | tf_op jit(solution)/shard_map/ppermute | solution.py:188
  59.8 9.2 %collective-permute-start.25 = (bf16[72,1536]{1,0:T(8,128)(2,1)S(1)}, bf16[72,1536]{1,0:T(8,128)(2,1)S(1)}, u32[]{:S(2)}, u32[]{:S(2)}) collective-permute-start(bf16[72,1536]{1,0:T(8,128)(2,1)S(1)} %broadcast_select_fusion.3), channel_id=1, source_target_pairs={{0,1},{3,2},{1,0},{2,3},{4,5},{7,6},{5,4},{6,7},{8,9},{11,10},{9,8... | collective-permute-start | bytes 663560 | tf_op jit(solution)/shard_map/ppermute | solution.py:183
  62.8 10.9 %collective-permute-start.7 = (bf16[72,1536]{1,0:T(8,128)(2,1)S(1)}, bf16[72,1536]{1,0:T(8,128)(2,1)S(1)}, u32[]{:S(2)}, u32[]{:S(2)}) collective-permute-start(bf16[72,1536]{1,0:T(8,128)(2,1)S(1)} %broadcast_select_fusion.12), channel_id=1, source_target_pairs={{0,1},{3,2},{1,0},{2,3},{4,5},{7,6},{5,4},{6,7},{8,9},{11,10},{9,8... | collective-permute-start | bytes 663560 | tf_op jit(solution)/shard_map/ppermute | solution.py:183
  63.1 13.9 %collective-permute-start.16 = (bf16[72,1536]{1,0:T(8,128)(2,1)S(1)}, bf16[72,1536]{1,0:T(8,128)(2,1)S(1)}, u32[]{:S(2)}, u32[]{:S(2)}) collective-permute-start(bf16[72,1536]{1,0:T(8,128)(2,1)S(1)} %broadcast_select_fusion.9), channel_id=1, source_target_pairs={{0,1},{3,2},{1,0},{2,3},{4,5},{7,6},{5,4},{6,7},{8,9},{11,10},{9,8... | collective-permute-start | bytes 663560 | tf_op jit(solution)/shard_map/ppermute | solution.py:183
  69.0 20.3 %collective-permute-start.26 = (bf16[72,1536]{1,0:T(8,128)(2,1)S(1)}, bf16[72,1536]{1,0:T(8,128)(2,1)S(1)}, u32[]{:S(2)}, u32[]{:S(2)}) collective-permute-start(bf16[72,1536]{1,0:T(8,128)(2,1)S(1)} %shard_map.124.s_ref), channel_id=1, source_target_pairs={{1,2},{2,1},{5,6},{6,5},{9,10},{10,9},{13,14},{14,13},{17,18},{18,... | collective-permute-start | bytes 663560 | tf_op jit(solution)/shard_map/ppermute | solution.py:188
  73.8 4.0 %collective-permute-start.8 = (bf16[72,1536]{1,0:T(8,128)(2,1)S(1)}, bf16[72,1536]{1,0:T(8,128)(2,1)S(1)}, u32[]{:S(2)}, u32[]{:S(2)}) collective-permute-start(bf16[72,1536]{1,0:T(8,128)(2,1)S(1)} %shard_map.108.s_ref), channel_id=1, source_target_pairs={{1,2},{2,1},{5,6},{6,5},{9,10},{10,9},{13,14},{14,13},{17,18},{18,... | collective-permute-start | bytes 663560 | tf_op jit(solution)/shard_map/ppermute | solution.py:188
  77.0 8.9 %collective-permute-start.17 = (bf16[72,1536]{1,0:T(8,128)(2,1)S(1)}, bf16[72,1536]{1,0:T(8,128)(2,1)S(1)}, u32[]{:S(2)}, u32[]{:S(2)}) collective-permute-start(bf16[72,1536]{1,0:T(8,128)(2,1)S(1)} %shard_map.116.s_ref), channel_id=1, source_target_pairs={{1,2},{2,1},{5,6},{6,5},{9,10},{10,9},{13,14},{14,13},{17,18},{18,... | collective-permute-start | bytes 663560 | tf_op jit(solution)/shard_map/ppermute | solution.py:188
  77.8 0.9 copy-start.7
  78.7 13.4 %collective-permute-start.9 = (bf16[72,1536]{1,0:T(8,128)(2,1)S(1)}, bf16[72,1536]{1,0:T(8,128)(2,1)S(1)}, u32[]{:S(2)}, u32[]{:S(2)}) collective-permute-start(bf16[72,1536]{1,0:T(8,128)(2,1)S(1)} %broadcast_select_fusion.11), channel_id=1, source_target_pairs={{0,1},{3,2},{1,0},{2,3},{4,5},{7,6},{5,4},{6,7},{8,9},{11,10},{9,8... | collective-permute-start | bytes 663560 | tf_op jit(solution)/shard_map/ppermute | solution.py:183
  86.0 10.8 %collective-permute-start.18 = (bf16[72,1536]{1,0:T(8,128)(2,1)S(1)}, bf16[72,1536]{1,0:T(8,128)(2,1)S(1)}, u32[]{:S(2)}, u32[]{:S(2)}) collective-permute-start(bf16[72,1536]{1,0:T(8,128)(2,1)S(1)} %broadcast_select_fusion.7), channel_id=1, source_target_pairs={{0,1},{3,2},{1,0},{2,3},{4,5},{7,6},{5,4},{6,7},{8,9},{11,10},{9,8... | collective-permute-start | bytes 663560 | tf_op jit(solution)/shard_map/ppermute | solution.py:183
  89.5 9.8 %collective-permute-start.27 = (bf16[72,1536]{1,0:T(8,128)(2,1)S(1)}, bf16[72,1536]{1,0:T(8,128)(2,1)S(1)}, u32[]{:S(2)}, u32[]{:S(2)}) collective-permute-start(bf16[72,1536]{1,0:T(8,128)(2,1)S(1)} %shard_map.125), channel_id=1, source_target_pairs={{1,0},{2,3},{5,4},{6,7},{9,8},{10,11},{13,12},{14,15},{17,16},{18,... | collective-permute-start | bytes 663560 | tf_op jit(solution)/shard_map/ppermute | solution.py:181
  92.1 9.4 %collective-permute-start.10 = (bf16[72,1536]{1,0:T(8,128)(2,1)S(1)}, bf16[72,1536]{1,0:T(8,128)(2,1)S(1)}, u32[]{:S(2)}, u32[]{:S(2)}) collective-permute-start(bf16[72,1536]{1,0:T(8,128)(2,1)S(1)} %shard_map.110.s_ref), channel_id=1, source_target_pairs={{1,2},{2,1},{5,6},{6,5},{9,10},{10,9},{13,14},{14,13},{17,18},{18,... | collective-permute-start | bytes 663560 | tf_op jit(solution)/shard_map/ppermute | solution.py:188
  96.9 6.1 %collective-permute-start.19 = (bf16[72,1536]{1,0:T(8,128)(2,1)S(1)}, bf16[72,1536]{1,0:T(8,128)(2,1)S(1)}, u32[]{:S(2)}, u32[]{:S(2)}) collective-permute-start(bf16[72,1536]{1,0:T(8,128)(2,1)S(1)} %shard_map.118.s_ref), channel_id=1, source_target_pairs={{1,2},{2,1},{5,6},{6,5},{9,10},{10,9},{13,14},{14,13},{17,18},{18,... | collective-permute-start | bytes 663560 | tf_op jit(solution)/shard_map/ppermute | solution.py:188
  100.0 6.4 %collective-permute-start.28 = (bf16[144,896]{1,0:T(8,128)(2,1)S(1)}, bf16[144,896]{1,0:T(8,128)(2,1)S(1)}, u32[]{:S(2)}, u32[]{:S(2)}) collective-permute-start(bf16[144,896]{1,0:T(8,128)(2,1)S(1)} %shard_map.126), channel_id=1, source_target_pairs={{0,4},{4,0},{1,5},{5,1},{2,6},{6,2},{3,7},{7,3},{8,12},{12,8},{9,1... | collective-permute-start | bytes 774152 | tf_op jit(solution)/shard_map/ppermute | solution.py:145
  101.7 12.9 %collective-permute-start.11 = (bf16[72,1536]{1,0:T(8,128)(2,1)S(1)}, bf16[72,1536]{1,0:T(8,128)(2,1)S(1)}, u32[]{:S(2)}, u32[]{:S(2)}) collective-permute-start(bf16[72,1536]{1,0:T(8,128)(2,1)S(1)} %shard_map.111), channel_id=1, source_target_pairs={{1,0},{2,3},{5,4},{6,7},{9,8},{10,11},{13,12},{14,15},{17,16},{18,... | collective-permute-start | bytes 663560 | tf_op jit(solution)/shard_map/ppermute | solution.py:181
  103.2 10.1 %collective-permute-start.20 = (bf16[72,1536]{1,0:T(8,128)(2,1)S(1)}, bf16[72,1536]{1,0:T(8,128)(2,1)S(1)}, u32[]{:S(2)}, u32[]{:S(2)}) collective-permute-start(bf16[72,1536]{1,0:T(8,128)(2,1)S(1)} %shard_map.119), channel_id=1, source_target_pairs={{1,0},{2,3},{5,4},{6,7},{9,8},{10,11},{13,12},{14,15},{17,16},{18,... | collective-permute-start | bytes 663560 | tf_op jit(solution)/shard_map/ppermute | solution.py:181
  106.5 18.9 %collective-permute-start.29 = (bf16[72,896]{1,0:T(8,128)(2,1)S(1)}, bf16[72,896]{1,0:T(8,128)(2,1)S(1)}, u32[]{:S(2)}, u32[]{:S(2)}) collective-permute-start(bf16[72,896]{1,0:T(8,128)(2,1)S(1)} %get-tuple-element.35), channel_id=1, source_target_pairs={{0,16},{8,24},{16,0},{24,8},{1,17},{9,25},{17,1},{25,9},{2,18},{10... | collective-permute-start | bytes 387080 | tf_op jit(solution)/shard_map/ppermute | solution.py:145
  108.1 17.3 %collective-permute-start.30 = (bf16[72,896]{1,0:T(8,128)(2,1)S(1)}, bf16[72,896]{1,0:T(8,128)(2,1)S(1)}, u32[]{:S(2)}, u32[]{:S(2)}) collective-permute-start(bf16[72,896]{1,0:T(8,128)(2,1)S(1)} %get-tuple-element.34), channel_id=1, source_target_pairs={{0,24},{8,16},{16,8},{24,0},{1,25},{9,17},{17,9},{25,1},{2,26},{10... | collective-permute-start | bytes 387080 | tf_op jit(solution)/shard_map/ppermute | solution.py:145
  114.0 6.4 %collective-permute-start.21 = (bf16[144,896]{1,0:T(8,128)(2,1)S(1)}, bf16[144,896]{1,0:T(8,128)(2,1)S(1)}, u32[]{:S(2)}, u32[]{:S(2)}) collective-permute-start(bf16[144,896]{1,0:T(8,128)(2,1)S(1)} %shard_map.120), channel_id=1, source_target_pairs={{0,4},{4,0},{1,5},{5,1},{2,6},{6,2},{3,7},{7,3},{8,12},{12,8},{9,1... | collective-permute-start | bytes 774152 | tf_op jit(solution)/shard_map/ppermute | solution.py:145
  120.5 4.9 %collective-permute-start.22 = (bf16[72,896]{1,0:T(8,128)(2,1)S(1)}, bf16[72,896]{1,0:T(8,128)(2,1)S(1)}, u32[]{:S(2)}, u32[]{:S(2)}) collective-permute-start(bf16[72,896]{1,0:T(8,128)(2,1)S(1)} %get-tuple-element.36), channel_id=1, source_target_pairs={{0,8},{8,0},{16,24},{24,16},{1,9},{9,1},{17,25},{25,17},{2,10},{10... | collective-permute-start | bytes 387080 | tf_op jit(solution)/shard_map/ppermute | solution.py:145
  (3 other events, 2.1 us)

commit v3 on v2

v3 whole, which is shorter than its diff:
```python
import functools

import jax
import jax.numpy as jnp
from jax import lax
from jax.experimental import pallas as pl
from jax.experimental.pallas import tpu as pltpu
from jax.sharding import PartitionSpec as P


F32 = jnp.float32
BF16 = jnp.bfloat16
VMEM = pltpu.VMEM


def mm(left, right, dims):
    return lax.dot_general(left, right, (dims, ((), ())), preferred_element_type=F32)


NN = ((1,), (0,))
NT = ((1,), (1,))
TN = ((0,), (0,))


def vm(x):
    return pltpu.with_memory_space_constraint(x, pltpu.VMEM)


def hbm(x):
    return pltpu.with_memory_space_constraint(x, pltpu.HBM)


def call(body, outs, args, raw=()):
    return pl.pallas_call(
        body,
        out_shape=outs,
        in_specs=[pl.BlockSpec(memory_space=VMEM)] * len(args),
        out_specs=jax.tree.map(lambda _: pl.BlockSpec(memory_space=VMEM), outs),
        compiler_params=pltpu.CompilerParams(vmem_limit_bytes=12 << 20),
    )(*[hbm(a) if i in raw else vm(a) for i, a in enumerate(args)])


def column(row):
    count = row.shape[1]
    eye = lax.broadcasted_iota(jnp.int32, (count, count), 0) == lax.broadcasted_iota(jnp.int32, (count, count), 1)
    return jnp.sum(jnp.where(eye, row, jnp.zeros_like(row)), axis=1, keepdims=True)


def ranks(ids):
    count = ids.shape[0]
    lanes = lax.broadcasted_iota(jnp.int32, (count, 128), 1)
    onehot = jnp.where(ids == lanes, 1.0, 0.0)
    lower = jnp.where(
        lax.broadcasted_iota(jnp.int32, (count, count), 0) > lax.broadcasted_iota(jnp.int32, (count, count), 1), 1.0, 0.0
    )
    before = mm(lower.astype(BF16), onehot.astype(BF16), NN)
    return jnp.sum(before * onehot, axis=1, keepdims=True).astype(jnp.int32)


def slots(ids, rank, owner, cap):
    places = lax.broadcasted_iota(jnp.int32, (ids.shape[0], cap), 1)
    return jnp.where((ids == owner) & (rank == places), 1.0, 0.0).astype(BF16)


def send_body(n_expert, cap, ids_ref, rw_ref, tokens_ref, cot_ref, *outs):
    ids = column(ids_ref[...])
    rank = ranks(ids)
    tokens = tokens_ref[...]
    scaled = (column(rw_ref[...]) * cot_ref[...].astype(F32)).astype(BF16)
    for k in range(n_expert):
        pick = slots(ids, rank, lax.axis_index("expert") ^ k, cap)
        outs[k][0, 0] = mm(pick, tokens, TN).astype(BF16)
        outs[k][0, 1] = mm(pick, scaled, TN).astype(BF16)


def side(refs, which):
    return jnp.concatenate([r[j, which] for r in refs for j in range(r.shape[0])], axis=0)


def part_body(half, n, *refs):
    rows, (wg_ref, wu_ref, wd_ref), outs = refs[:n], refs[n:n + 3], refs[n + 3:]
    x, g = side(rows, 0), side(rows, 1)
    parts = (mm(x, wg_ref[...], NN), mm(x, wu_ref[...], NN), mm(g, wd_ref[...], NT))
    size = outs[0].shape[0]
    for i in range(n):
        for j in range(3):
            outs[i][:, j * half:(j + 1) * half] = parts[j][i * size:(i + 1) * size].astype(BF16)


def at_edge():
    z = lax.axis_index("seq")
    return (z == 0) | (z == 3)


def join_body(now, old, *refs):
    came_ref = refs[0]
    if now:
        part_ref, pair_ref = refs[1], refs[-1 - old]
        pair_ref[...] = (part_ref[...].astype(F32) + came_ref[...].astype(F32)).astype(BF16)
    if old:
        act_ref, full_ref = refs[1 + now], refs[-1]

        @pl.when(at_edge())
        def _():
            full_ref[...] = came_ref[...]

        @pl.when(jnp.logical_not(at_edge()))
        def _():
            full_ref[...] = act_ref[...]


def act_body(half, mixed, s_ref, m_ref, *refs):
    o_ref = refs[mixed]
    gate = s_ref[:, :half].astype(F32) + m_ref[:, :half].astype(F32)
    upper = s_ref[:, half:2 * half].astype(F32) + m_ref[:, half:2 * half].astype(F32)
    hgrad = s_ref[:, 2 * half:].astype(F32) + m_ref[:, 2 * half:].astype(F32)
    sigma = jax.nn.sigmoid(gate)
    active = gate * sigma
    o_ref[:, :half] = (hgrad * upper * sigma * (1.0 + gate * (1.0 - sigma))).astype(BF16)
    o_ref[:, half:2 * half] = (hgrad * active).astype(BF16)
    o_ref[:, 2 * half:] = (active * upper).astype(BF16)
    if mixed:
        part_ref, send_ref = refs[0], refs[2]

        @pl.when(at_edge())
        def _():
            send_ref[...] = part_ref[...]

        @pl.when(jnp.logical_not(at_edge()))
        def _():
            send_ref[...] = o_ref[...]


def out_body(half, n, *refs):
    acts, (wg_ref, wu_ref, o_ref) = refs[:n], refs[n:]
    a = jnp.concatenate([r[:, :2 * half] for r in acts], axis=0)
    o_ref[...] = (mm(a[:, :half], wg_ref[...], NT) + mm(a[:, half:], wu_ref[...], NT)).astype(BF16)


def total_body(start, mine_ref, *refs):
    o_ref = refs[-1]
    value = mine_ref[start:start + o_ref.shape[0]].astype(F32)
    for r in refs[:-1]:
        value = value + r[...].astype(F32)
    o_ref[...] = value.astype(BF16)


def wgrad_body(half, n, last, *refs):
    rows, acts, rest = refs[:n], refs[n:2 * n], refs[2 * n:]
    x, g = side(rows, 0), side(rows, 1)
    a = jnp.concatenate([r[...] for r in acts], axis=0)
    gx, gd = mm(x, a[:, :2 * half], TN), mm(a[:, 2 * half:], g, TN)
    if last:
        px_ref, pd_ref, gg_ref, gu_ref, gd_ref = rest
        gg_ref[0] = (px_ref[:, :half] + gx[:, :half]).astype(BF16)
        gu_ref[0] = (px_ref[:, half:] + gx[:, half:]).astype(BF16)
        gd_ref[0] = (pd_ref[...] + gd).astype(BF16)
    else:
        rest[0][...] = gx
        rest[1][...] = gd


def final_body(n_expert, cap, ids_ref, rw_ref, *refs):
    ids = column(ids_ref[...])
    rank = ranks(ids)
    total = None
    for k in range(n_expert):
        term = mm(slots(ids, rank, lax.axis_index("expert") ^ k, cap), refs[k][...], NN)
        total = term if total is None else total + term
    refs[n_expert][...] = (column(rw_ref[...]) * total).astype(BF16)


def steps(tokens, cotangent, route_weight, expert_ids, gate_weight, up_weight, down_weight):
    n_expert = lax.axis_size("expert")
    n_rep = lax.axis_size("replica")
    n_seq = lax.axis_size("seq")
    assert n_seq == 4 and n_expert % 4 == 0
    count, quarter = tokens.shape
    half = gate_weight.shape[2]
    cap = -(-(3 * count // (2 * n_expert)) // 8) * 8
    each = n_expert // 4
    w_gate, w_up, w_down = gate_weight[0], up_weight[0], down_weight[0]
    rw = route_weight.reshape(1, count)
    ids = expert_ids.reshape(1, count)
    keep = lambda *shape: pltpu.VMEM(shape, BF16)

    def swap(x, axis, k):
        return lax.ppermute(x, axis, [(i, i ^ k) for i in range(lax.axis_size(axis))])

    send = call(
        functools.partial(send_body, n_expert, cap), [keep(1, 2, cap, quarter)] * n_expert,
        (ids, rw, tokens, cotangent), (0, 1, 2, 3),
    )
    got = [send[0]] + [swap(send[k], "expert", k) for k in range(1, n_expert)]
    rows = {}
    for j in range(4):
        blocks = got[j * each:(j + 1) * each]
        rows[0, j] = blocks[0] if each == 1 else jnp.concatenate(blocks, axis=0)
    for q in range(1, n_rep):
        for j in range(4):
            rows[q, j] = swap(rows[0, j], "replica", q)
    size = each * cap
    parts = {}
    for q in range(n_rep):
        for pair in ((0, 1), (2, 3)):
            done = call(
                functools.partial(part_body, half, 2), [keep(size, 3 * half)] * 2,
                (*[rows[q, j] for j in pair], w_gate, w_up, w_down),
                (2, 3, 4) if (q, pair) == (0, (0, 1)) else (),
            )
            parts[q, pair[0]], parts[q, pair[1]] = done

    waves = [(0, 1), (0, 2), (0, 3)]
    waves += [(q, j) for q in range(1, n_rep) for j in (2, 3, 1, 0)] + [(0, 0)]
    lag = 3
    inward, outward, middle = [(0, 1), (3, 2)], [(1, 0), (2, 3)], [(1, 2), (2, 1)]
    acts, full = {}, {}
    leaving = {i: parts[waves[i]] for i in range(lag)}
    wave = keep(size, 3 * half)
    for i in range(len(waves) + lag):
        now = waves[i] if i < len(waves) else None
        old = waves[i - lag] if i >= lag else None
        pairs = (inward if now else []) + (outward if old else [])
        came = lax.ppermute(leaving[i], "seq", pairs)
        done = call(
            functools.partial(join_body, int(now is not None), int(old is not None)),
            [wave] * ((now is not None) + (old is not None)),
            (came, *([parts[now]] if now else []), *([acts[old]] if old else [])),
        )
        if old is not None:
            full[old] = done[-1]
        if now is not None:
            following = [parts[waves[i + lag]]] if i + lag < len(waves) else []
            both = call(
                functools.partial(act_body, half, len(following)), [wave] * (1 + len(following)),
                (done[0], lax.ppermute(done[0], "seq", middle), *following),
            )
            acts[now], leaving[i + lag] = both[0], both[-1]

    def out(q, js):
        return call(
            functools.partial(out_body, half, len(js)), keep(len(js) * size, quarter),
            (*[full[q, j] for j in js], w_gate, w_up),
        )

    mine = {}
    for js in ((2, 3), (1,), (0,)):
        rows_of = out(0, js)
        for n, j in enumerate(js):
            mine[j] = (n, rows_of)
    total = {}
    for j in range(4):
        back = [swap(out(q, (j,)), "replica", q) for q in range(1, n_rep)]
        n, rows_of = mine[j]
        total[j] = call(functools.partial(total_body, n * size), keep(size, quarter), (rows_of, *back))
    ret = [total[k // each][k % each * cap:(k % each + 1) * cap] for k in range(n_expert)]
    ret = [ret[0]] + [swap(ret[k], "expert", k) for k in range(1, n_expert)]
    sds = jax.ShapeDtypeStruct
    token_grad = call(functools.partial(final_body, n_expert, cap), sds((count, quarter), BF16), (ids, rw, *ret))
    early, late = waves[:-2], waves[-2:]
    part_x, part_d = call(
        functools.partial(wgrad_body, half, len(early), False),
        [pltpu.VMEM((quarter, 2 * half), F32), pltpu.VMEM((half, quarter), F32)],
        (*[rows[w] for w in early], *[full[w] for w in early]),
    )
    gate_grad, up_grad, down_grad = call(
        functools.partial(wgrad_body, half, len(late), True),
        [sds((1, quarter, half), BF16), sds((1, quarter, half), BF16), sds((1, half, quarter), BF16)],
        (*[rows[w] for w in late], *[full[w] for w in late], part_x, part_d),
    )
    return (token_grad, gate_grad, up_grad, down_grad)


def solution(mesh):
    placed = (
        P(("expert", "replica"), "seq"),
        P(("expert", "replica"), "seq"),
        P(("expert", "replica")),
        P(("expert", "replica"), None),
        P("expert", "seq", "replica"),
        P("expert", "seq", "replica"),
        P("expert", "replica", "seq"),
    )
    return jax.shard_map(
        steps,
        mesh=mesh,
        in_specs=placed,
        out_specs=(
            P(("expert", "replica"), "seq"),
            P("expert", "seq", "replica"),
            P("expert", "seq", "replica"),
            P("expert", "replica", "seq"),
        ),
        check_vma=False,
    )
```

time: 128 us -> 98.4 us (0.77)
  waiting for transfers between devices: 49.5 us -> 28.3 us
  local copies, waits for them, and re-layouts: 12.8 us -> 0.03 us
  starting transfers between devices: 43.5 us -> 49.2 us
    ppermute x19, waiting for transfers between devices: 25.3 us -> 10.7 us  [the longest x11 10.7 us: steps(): came = lax.ppermute(leaving[i], 'seq', pairs)]
    unnamed x40 -> x10, local copies, waits for them, and re-layouts: 12.8 us -> 0.03 us
    ppermute x12 -> x14, waiting for transfers between devices: 24.2 us -> 17.6 us  [swap(): lax.ppermute(x, axis, [(i, i ^ k) for i in range(lax.axis_size(axis))])]
    ppermute x19, starting transfers between devices: 31.5 us -> 35.9 us  [the longest x11 30.5 us: steps(): came = lax.ppermute(leaving[i], 'seq', pairs)]
    ppermute x12 -> x14, starting transfers between devices: 12 us -> 13.4 us  [swap(): lax.ppermute(x, axis, [(i, i ^ k) for i in range(lax.axis_size(axis))])]
    pallas_call x27 -> x38, Pallas kernels: 19.5 us -> 18.9 us  [call(): pl.pallas_call(body, out_shape=outs, in_specs=[pl.BlockSpec(memory_space=...]
  transfers between devices with their start and end apart: 31 -> 33, of which waited for: 15 -> 11; matrix products, arithmetic and copies ran while one was open for 0% -> 0% of each run, Pallas kernels for 13% -> 15%
where the time goes in v3:
time: 98.4 us; the launch traced here: 97.5 us
  starting transfers between devices  49.2 us (50%)
  waiting for transfers between devices  28.3 us (29%)
  Pallas kernels  18.9 us (19%)
  between operations  1.15 us (1%)
    ppermute x11, starting transfers between devices, steps(): came = lax.ppermute(leaving[i], 'seq', pairs)  30.5 us
    pallas_call x38, Pallas kernels, call(): pl.pallas_call(body, out_shape=outs, in_specs=[pl.BlockSpec(memory_space=...  18.9 us
    ppermute x14, waiting for transfers between devices, swap(): lax.ppermute(x, axis, [(i, i ^ k) for i in range(lax.axis_size(axis))])  17.6 us
    ppermute x14, starting transfers between devices, swap(): lax.ppermute(x, axis, [(i, i ^ k) for i in range(lax.axis_size(axis))])  13.4 us
    ppermute x11, waiting for transfers between devices, steps(): came = lax.ppermute(leaving[i], 'seq', pairs)  10.7 us
    ppermute x8, starting transfers between devices, steps(): lax.ppermute(done[0], 'seq', middle)  5.4 us
  transfers between devices with their start and end apart: 33, of which 11 were waited for; matrix products, arithmetic and copies ran while one was open for 0% of the time, Pallas kernels for 15%

profile of v3, /device:TPU:0, one launch (start us, length us, event | category | flops | bytes accessed | tf_op | source)
XLA Modules:
  0.0 97.5 jit_solution(5902521021598371816)
XLA Ops:
  0.7 2.3 %shard_map.102 = (bf16[1,2,72,896]{3,2,1,0:T(8,128)(2,1)S(1)}, bf16[1,2,72,896]{3,2,1,0:T(8,128)(2,1)S(1)}, bf16[1,2,72,896]{3,2,1,0:T(8,128)(2,1)S(1)}, bf16[1,2,72,896]{3,2,1,0:T(8,128)(2,1)S(1)}) custom-call(s32[1,192]{1,0:T(1,128)} %bitcast.31, f32[1,192]{1,0:T(1,128)} %bitcast.33, bf16[192,896]{1,0:T(8,128)(2,1)} %tokens_ref.1, bf16[192,896]{1,0:T(8,128)(2,1)} %cot_ref.1), custom_call_target="tpu_custom_call" | custom-call | tf_op jit(solution)/shard_map/pallas_call | solution.py:34
  3.5 2.6 %collective-permute-start = (bf16[1,2,72,896]{3,2,1,0:T(8,128)(2,1)S(1)}, bf16[1,2,72,896]{3,2,1,0:T(8,128)(2,1)S(1)}, u32[]{:S(2)}, u32[]{:S(2)}) collective-permute-start(bf16[1,2,72,896]{3,2,1,0:T(8,128)(2,1)S(1)} %get-tuple-element.41), channel_id=1, source_target_pairs={{0,16},{8,24},{16,0},{24,8},{1,17},{9,25},{17,1},{25,9},{2,18},{10... | collective-permute-start | bytes 774152 | tf_op jit(solution)/shard_map/ppermute | solution.py:188
  6.1 2.5 %shard_map.108 = (bf16[72,1536]{1,0:T(8,128)(2,1)S(1)}, bf16[72,1536]{1,0:T(8,128)(2,1)S(1)}) custom-call(bf16[1,2,72,896]{3,2,1,0:T(8,128)(2,1)S(1)} %get-tuple-element.48.refs_0_.refs_1_, bf16[1,2,72,896]{3,2,1,0:T(8,128)(2,1)S(1)} %collective-permute-done.8.refs_1_.refs_0_, bf16[896,512]{1,0:T(8,128)(2,1)} %bitcast.5, bf16[896,512]{1,0:T(8,128)(2,1)} %bitcast.16, ...), custom_call_target="tpu_custom_call" | custom-call | tf_op jit(solution)/shard_map/pallas_call | solution.py:34
  8.6 3.7 %collective-permute-start.12 = (bf16[72,1536]{1,0:T(8,128)(2,1)S(1)}, bf16[72,1536]{1,0:T(8,128)(2,1)S(1)}, u32[]{:S(2)}, u32[]{:S(2)}) collective-permute-start(bf16[72,1536]{1,0:T(8,128)(2,1)S(1)} %get-tuple-element.54.refs_1_), channel_id=1, source_target_pairs={{0,1},{3,2},{4,5},{7,6},{8,9},{11,10},{12,13},{15,14},{16,17},{19,... | collective-permute-start | bytes 663560 | tf_op jit(solution)/shard_map/ppermute | solution.py:224
  12.3 0.8 collective-permute-done.refs_0_.refs_1_
  13.1 5.0 %collective-permute-done.1.refs_1_.refs_2_ = bf16[1,2,72,896]{3,2,1,0:T(8,128)(2,1)S(1)} collective-permute-done((bf16[1,2,72,896]{3,2,1,0:T(8,128)(2,1)S(1)}, bf16[1,2,72,896]{3,2,1,0:T(8,128)(2,1)S(1)}, u32[]{:S(2)}, u32[]{:S(2)}) %collective-permute-start.1) | collective-permute-done | bytes 258080 | tf_op jit(solution)/shard_map/ppermute | solution.py:188
  18.2 0.8 shard_map.103
  18.9 3.4 %collective-permute-start.2 = (bf16[72,1536]{1,0:T(8,128)(2,1)S(1)}, bf16[72,1536]{1,0:T(8,128)(2,1)S(1)}, u32[]{:S(2)}, u32[]{:S(2)}) collective-permute-start(bf16[72,1536]{1,0:T(8,128)(2,1)S(1)} %get-tuple-element.43.refs_1_), channel_id=1, source_target_pairs={{0,1},{3,2},{4,5},{7,6},{8,9},{11,10},{12,13},{15,14},{16,17},{19,... | collective-permute-start | bytes 663560 | tf_op jit(solution)/shard_map/ppermute | solution.py:224
  22.4 1.6 %collective-permute-start.4 = (bf16[1,2,72,896]{3,2,1,0:T(8,128)(2,1)S(1)}, bf16[1,2,72,896]{3,2,1,0:T(8,128)(2,1)S(1)}, u32[]{:S(2)}, u32[]{:S(2)}) collective-permute-start(bf16[1,2,72,896]{3,2,1,0:T(8,128)(2,1)S(1)} %collective-permute-done.refs_0_.refs_1_), channel_id=1, source_target_pairs={{0,4},{4,0},{1,5},{5,1},{2,6},{6,2},{3,7},{7,3},{8,12},{12,8},{9,1... | collective-permute-start | bytes 774152 | tf_op jit(solution)/shard_map/ppermute | solution.py:188
  24.5 0.7 collective-permute-start.13
  25.2 4.1 %collective-permute-start.22 = (bf16[72,1536]{1,0:T(8,128)(2,1)S(1)}, bf16[72,1536]{1,0:T(8,128)(2,1)S(1)}, u32[]{:S(2)}, u32[]{:S(2)}) collective-permute-start(bf16[72,1536]{1,0:T(8,128)(2,1)S(1)} %get-tuple-element.64.refs_1_), channel_id=1, source_target_pairs={{0,1},{3,2},{4,5},{7,6},{8,9},{11,10},{12,13},{15,14},{16,17},{19,... | collective-permute-start | bytes 663560 | tf_op jit(solution)/shard_map/ppermute | solution.py:224
  29.4 0.7 collective-permute-start.3
  30.1 1.5 %collective-permute-done.4.refs_0_.refs_3_ = bf16[1,2,72,896]{3,2,1,0:T(8,128)(2,1)S(1)} collective-permute-done((bf16[1,2,72,896]{3,2,1,0:T(8,128)(2,1)S(1)}, bf16[1,2,72,896]{3,2,1,0:T(8,128)(2,1)S(1)}, u32[]{:S(2)}, u32[]{:S(2)}) %collective-permute-start.4) | collective-permute-done | bytes 258080 | tf_op jit(solution)/shard_map/ppermute | solution.py:188
  31.5 4.7 %collective-permute-done.5.refs_1_.refs_4_ = bf16[1,2,72,896]{3,2,1,0:T(8,128)(2,1)S(1)} collective-permute-done((bf16[1,2,72,896]{3,2,1,0:T(8,128)(2,1)S(1)}, bf16[1,2,72,896]{3,2,1,0:T(8,128)(2,1)S(1)}, u32[]{:S(2)}, u32[]{:S(2)}) %collective-permute-start.5) | collective-permute-done | bytes 258080 | tf_op jit(solution)/shard_map/ppermute | solution.py:188
  36.3 0.8 shard_map.105
  37.3 1.6 %collective-permute-start.16 = (bf16[1,2,72,896]{3,2,1,0:T(8,128)(2,1)S(1)}, bf16[1,2,72,896]{3,2,1,0:T(8,128)(2,1)S(1)}, u32[]{:S(2)}, u32[]{:S(2)}) collective-permute-start(bf16[1,2,72,896]{3,2,1,0:T(8,128)(2,1)S(1)} %get-tuple-element.48.refs_0_.refs_1_), channel_id=1, source_target_pairs={{0,4},{4,0},{1,5},{5,1},{2,6},{6,2},{3,7},{7,3},{8,12},{12,8},{9,1... | collective-permute-start | bytes 774152 | tf_op jit(solution)/shard_map/ppermute | solution.py:188
  39.4 0.7 collective-permute-start.23
  40.2 4.8 %collective-permute-start.6 = (bf16[72,1536]{1,0:T(8,128)(2,1)S(1)}, bf16[72,1536]{1,0:T(8,128)(2,1)S(1)}, u32[]{:S(2)}, u32[]{:S(2)}) collective-permute-start(bf16[72,1536]{1,0:T(8,128)(2,1)S(1)} %get-tuple-element.45), channel_id=1, source_target_pairs={{0,1},{3,2},{1,0},{2,3},{4,5},{7,6},{5,4},{6,7},{8,9},{11,10},{9,8... | collective-permute-start | bytes 663560 | tf_op jit(solution)/shard_map/ppermute | solution.py:224
  45.2 0.7 collective-permute-start.15
  46.4 3.9 %collective-permute-done.17.refs_1_.refs_5_ = bf16[1,2,72,896]{3,2,1,0:T(8,128)(2,1)S(1)} collective-permute-done((bf16[1,2,72,896]{3,2,1,0:T(8,128)(2,1)S(1)}, bf16[1,2,72,896]{3,2,1,0:T(8,128)(2,1)S(1)}, u32[]{:S(2)}, u32[]{:S(2)}) %collective-permute-start.17) | collective-permute-done | bytes 258080 | tf_op jit(solution)/shard_map/ppermute | solution.py:188
  50.3 0.8 shard_map.117
  51.2 1.7 %collective-permute-start.24 = (bf16[72,1536]{1,0:T(8,128)(2,1)S(1)}, bf16[72,1536]{1,0:T(8,128)(2,1)S(1)}, u32[]{:S(2)}, u32[]{:S(2)}) collective-permute-start(bf16[72,1536]{1,0:T(8,128)(2,1)S(1)} %get-tuple-element.66), channel_id=1, source_target_pairs={{0,1},{3,2},{1,0},{2,3},{4,5},{7,6},{5,4},{6,7},{8,9},{11,10},{9,8... | collective-permute-start | bytes 663560 | tf_op jit(solution)/shard_map/ppermute | solution.py:224
  53.0 0.7 collective-permute-start.7
  53.9 3.2 %collective-permute-start.18 = (bf16[72,1536]{1,0:T(8,128)(2,1)S(1)}, bf16[72,1536]{1,0:T(8,128)(2,1)S(1)}, u32[]{:S(2)}, u32[]{:S(2)}) collective-permute-start(bf16[72,1536]{1,0:T(8,128)(2,1)S(1)} %get-tuple-element.60), channel_id=1, source_target_pairs={{0,1},{3,2},{1,0},{2,3},{4,5},{7,6},{5,4},{6,7},{8,9},{11,10},{9,8... | collective-permute-start | bytes 663560 | tf_op jit(solution)/shard_map/ppermute | solution.py:224
  57.1 1.5 %collective-permute-done.24.refs_0_ = bf16[72,1536]{1,0:T(8,128)(2,1)S(1)} collective-permute-done((bf16[72,1536]{1,0:T(8,128)(2,1)S(1)}, bf16[72,1536]{1,0:T(8,128)(2,1)S(1)}, u32[]{:S(2)}, u32[]{:S(2)}) %collective-permute-start.24) | collective-permute-done | bytes 221216 | tf_op jit(solution)/shard_map/ppermute | solution.py:224
  58.7 0.7 collective-permute-start.25
  59.5 5.5 %collective-permute-start.9 = (bf16[72,1536]{1,0:T(8,128)(2,1)S(1)}, bf16[72,1536]{1,0:T(8,128)(2,1)S(1)}, u32[]{:S(2)}, u32[]{:S(2)}) collective-permute-start(bf16[72,1536]{1,0:T(8,128)(2,1)S(1)} %get-tuple-element.51), channel_id=1, source_target_pairs={{0,1},{3,2},{1,0},{2,3},{4,5},{7,6},{5,4},{6,7},{8,9},{11,10},{9,8... | collective-permute-start | bytes 663560 | tf_op jit(solution)/shard_map/ppermute | solution.py:224
  65.1 0.7 collective-permute-start.19
  65.9 1.3 %collective-permute-start.26 = (bf16[72,1536]{1,0:T(8,128)(2,1)S(1)}, bf16[72,1536]{1,0:T(8,128)(2,1)S(1)}, u32[]{:S(2)}, u32[]{:S(2)}) collective-permute-start(bf16[72,1536]{1,0:T(8,128)(2,1)S(1)} %shard_map.128.refs_1_), channel_id=1, source_target_pairs={{1,0},{2,3},{5,4},{6,7},{9,8},{10,11},{13,12},{14,15},{17,16},{18,... | collective-permute-start | bytes 663560 | tf_op jit(solution)/shard_map/ppermute | solution.py:224
  67.2 3.8 %collective-permute-done.9.refs_0_ = bf16[72,1536]{1,0:T(8,128)(2,1)S(1)} collective-permute-done((bf16[72,1536]{1,0:T(8,128)(2,1)S(1)}, bf16[72,1536]{1,0:T(8,128)(2,1)S(1)}, u32[]{:S(2)}, u32[]{:S(2)}) %collective-permute-start.9) | collective-permute-done | bytes 221216 | tf_op jit(solution)/shard_map/ppermute | solution.py:224
  71.1 0.7 collective-permute-start.10
  71.9 1.3 %collective-permute-start.20 = (bf16[72,1536]{1,0:T(8,128)(2,1)S(1)}, bf16[72,1536]{1,0:T(8,128)(2,1)S(1)}, u32[]{:S(2)}, u32[]{:S(2)}) collective-permute-start(bf16[72,1536]{1,0:T(8,128)(2,1)S(1)} %shard_map.120.refs_1_), channel_id=1, source_target_pairs={{1,0},{2,3},{5,4},{6,7},{9,8},{10,11},{13,12},{14,15},{17,16},{18,... | collective-permute-start | bytes 663560 | tf_op jit(solution)/shard_map/ppermute | solution.py:224
  73.2 5.1 %collective-permute-done.26.refs_0_ = bf16[72,1536]{1,0:T(8,128)(2,1)S(1)} collective-permute-done((bf16[72,1536]{1,0:T(8,128)(2,1)S(1)}, bf16[72,1536]{1,0:T(8,128)(2,1)S(1)}, u32[]{:S(2)}, u32[]{:S(2)}) %collective-permute-start.26) | collective-permute-done | bytes 221216 | tf_op jit(solution)/shard_map/ppermute | solution.py:224
  78.3 0.7 shard_map.130
  79.0 1.6 %collective-permute-start.27 = (bf16[72,896]{1,0:T(8,128)(2,1)S(1)}, bf16[72,896]{1,0:T(8,128)(2,1)S(1)}, u32[]{:S(2)}, u32[]{:S(2)}) collective-permute-start(bf16[72,896]{1,0:T(8,128)(2,1)S(1)} %shard_map.130), channel_id=1, source_target_pairs={{0,4},{4,0},{1,5},{5,1},{2,6},{6,2},{3,7},{7,3},{8,12},{12,8},{9,1... | collective-permute-start | bytes 387080 | tf_op jit(solution)/shard_map/ppermute | solution.py:188
  80.5 0.7 shard_map.133
  81.8 0.7 shard_map.135
  82.5 1.6 %collective-permute-start.31 = (bf16[72,896]{1,0:T(8,128)(2,1)S(1)}, bf16[72,896]{1,0:T(8,128)(2,1)S(1)}, u32[]{:S(2)}, u32[]{:S(2)}) collective-permute-start(bf16[72,896]{1,0:T(8,128)(2,1)S(1)} %shard_map.135), channel_id=1, source_target_pairs={{0,4},{4,0},{1,5},{5,1},{2,6},{6,2},{3,7},{7,3},{8,12},{12,8},{9,1... | collective-permute-start | bytes 387080 | tf_op jit(solution)/shard_map/ppermute | solution.py:188
  84.2 1.3 %collective-permute-start.11 = (bf16[72,1536]{1,0:T(8,128)(2,1)S(1)}, bf16[72,1536]{1,0:T(8,128)(2,1)S(1)}, u32[]{:S(2)}, u32[]{:S(2)}) collective-permute-start(bf16[72,1536]{1,0:T(8,128)(2,1)S(1)} %shard_map.111.refs_1_), channel_id=1, source_target_pairs={{1,0},{2,3},{5,4},{6,7},{9,8},{10,11},{13,12},{14,15},{17,16},{18,... | collective-permute-start | bytes 663560 | tf_op jit(solution)/shard_map/ppermute | solution.py:224
  85.5 0.7 shard_map.124.mine_ref
  86.2 0.7 shard_map.132.mine_ref
  87.1 0.7 shard_map.122
  88.4 1.5 %collective-permute-start.30 = (bf16[72,896]{1,0:T(8,128)(2,1)S(1)}, bf16[72,896]{1,0:T(8,128)(2,1)S(1)}, u32[]{:S(2)}, u32[]{:S(2)}) collective-permute-start(bf16[72,896]{1,0:T(8,128)(2,1)S(1)} %shard_map.134), channel_id=1, source_target_pairs={{0,16},{8,24},{16,0},{24,8},{1,17},{9,25},{17,1},{25,9},{2,18},{10... | collective-permute-start | bytes 387080 | tf_op jit(solution)/shard_map/ppermute | solution.py:188
  90.0 1.7 %shard_map.138 = (f32[896,1024]{1,0:T(8,128)S(1)}, f32[512,896]{1,0:T(8,128)S(1)}) custom-call(bf16[1,2,72,896]{3,2,1,0:T(8,128)(2,1)S(1)} %collective-permute-done.8.refs_1_.refs_0_, bf16[1,2,72,896]{3,2,1,0:T(8,128)(2,1)S(1)} %collective-permute-done.refs_0_.refs_1_, bf16[1,2,72,896]{3,2,1,0:T(8,128)(2,1)S(1)} %collective-permute-done.1.refs_1_.refs_2_, ...), custom_call_target="tpu_custom_call" | custom-call | tf_op jit(solution)/shard_map/pallas_call | solution.py:34
  92.0 0.7 shard_map.113.mine_ref
  92.7 2.0 %shard_map.139 = (bf16[1,896,512]{2,1,0:T(8,128)(2,1)}, bf16[1,896,512]{2,1,0:T(8,128)(2,1)}, bf16[1,512,896]{2,1,0:T(8,128)(2,1)}) custom-call(bf16[1,2,72,896]{3,2,1,0:T(8,128)(2,1)S(1)} %collective-permute-done.16.refs_0_, bf16[1,2,72,896]{3,2,1,0:T(8,128)(2,1)S(1)} %get-tuple-element.48.refs_0_.refs_1_, bf16[72,1536]{1,0:T(8,128)(2,1)S(1)} %shard_map.121.refs_0_.refs_2_, ...), custom_call_target="tpu_custom_call" | custom-call | tf_op jit(solution)/shard_map/pallas_call | solution.py:34
  94.8 1.1 %collective-permute-done.32.refs_3_ = bf16[72,896]{1,0:T(8,128)(2,1)S(1)} collective-permute-done((bf16[72,896]{1,0:T(8,128)(2,1)S(1)}, bf16[72,896]{1,0:T(8,128)(2,1)S(1)}, u32[]{:S(2)}, u32[]{:S(2)}) %collective-permute-start.32) | collective-permute-done | bytes 129056 | tf_op jit(solution)/shard_map/ppermute | solution.py:188
  95.9 1.6 %shard_map.137 = bf16[192,896]{1,0:T(8,128)(2,1)} custom-call(s32[1,192]{1,0:T(1,128)S(1)} %bitcast.32, f32[1,192]{1,0:T(1,128)S(1)} %bitcast.34, bf16[72,896]{1,0:T(8,128)(2,1)S(1)} %shard_map.123.refs_0_, bf16[72,896]{1,0:T(8,128)(2,1)S(1)} %collective-permute-done.28.refs_1_, bf16[72,896]{1,0:T(8,128)(2,1)S(1)} %collective-permute-done.30.refs_2_, ...), custom_call_target="tpu_custom_call" | custom-call | tf_op jit(solution)/shard_map/pallas_call | solution.py:34
  (66 shorter events, 5.6 us)
Async XLA Ops:
  0.6 17.5 %copy-start.2 = (bf16[1,512,896]{2,1,0:T(8,128)(2,1)S(1)}, bf16[1,512,896]{2,1,0:T(8,128)(2,1)}, u32[]{:S(2)}) copy-start(bf16[1,512,896]{2,1,0:T(8,128)(2,1)} %param.13) | copy-start | bytes 2752516
  0.6 17.5 %copy-start.1 = (bf16[1,896,512]{2,1,0:T(8,128)(2,1)S(1)}, bf16[1,896,512]{2,1,0:T(8,128)(2,1)}, u32[]{:S(2)}) copy-start(bf16[1,896,512]{2,1,0:T(8,128)(2,1)} %param.12) | copy-start | bytes 2752516
  0.7 17.5 %copy-start = (bf16[1,896,512]{2,1,0:T(8,128)(2,1)S(1)}, bf16[1,896,512]{2,1,0:T(8,128)(2,1)}, u32[]{:S(2)}) copy-start(bf16[1,896,512]{2,1,0:T(8,128)(2,1)} %param.11) | copy-start | bytes 2752516
  2.9 3.2 %collective-permute-start.8 = (bf16[1,2,72,896]{3,2,1,0:T(8,128)(2,1)S(1)}, bf16[1,2,72,896]{3,2,1,0:T(8,128)(2,1)S(1)}, u32[]{:S(2)}, u32[]{:S(2)}) collective-permute-start(bf16[1,2,72,896]{3,2,1,0:T(8,128)(2,1)S(1)} %get-tuple-element.49), channel_id=1, source_target_pairs={{0,8},{8,0},{16,24},{24,16},{1,9},{9,1},{17,25},{25,17},{2,10},{10... | collective-permute-start | bytes 774152 | tf_op jit(solution)/shard_map/ppermute | solution.py:188
  3.5 9.7 %collective-permute-start = (bf16[1,2,72,896]{3,2,1,0:T(8,128)(2,1)S(1)}, bf16[1,2,72,896]{3,2,1,0:T(8,128)(2,1)S(1)}, u32[]{:S(2)}, u32[]{:S(2)}) collective-permute-start(bf16[1,2,72,896]{3,2,1,0:T(8,128)(2,1)S(1)} %get-tuple-element.41), channel_id=1, source_target_pairs={{0,16},{8,24},{16,0},{24,8},{1,17},{9,25},{17,1},{25,9},{2,18},{10... | collective-permute-start | bytes 774152 | tf_op jit(solution)/shard_map/ppermute | solution.py:188
  6.1 12.1 %collective-permute-start.1 = (bf16[1,2,72,896]{3,2,1,0:T(8,128)(2,1)S(1)}, bf16[1,2,72,896]{3,2,1,0:T(8,128)(2,1)S(1)}, u32[]{:S(2)}, u32[]{:S(2)}) collective-permute-start(bf16[1,2,72,896]{3,2,1,0:T(8,128)(2,1)S(1)} %get-tuple-element.42), channel_id=1, source_target_pairs={{0,24},{8,16},{16,8},{24,0},{1,25},{9,17},{17,9},{25,1},{2,26},{10... | collective-permute-start | bytes 774152 | tf_op jit(solution)/shard_map/ppermute | solution.py:188
  8.6 15.8 %collective-permute-start.12 = (bf16[72,1536]{1,0:T(8,128)(2,1)S(1)}, bf16[72,1536]{1,0:T(8,128)(2,1)S(1)}, u32[]{:S(2)}, u32[]{:S(2)}) collective-permute-start(bf16[72,1536]{1,0:T(8,128)(2,1)S(1)} %get-tuple-element.54.refs_1_), channel_id=1, source_target_pairs={{0,1},{3,2},{4,5},{7,6},{8,9},{11,10},{12,13},{15,14},{16,17},{19,... | collective-permute-start | bytes 663560 | tf_op jit(solution)/shard_map/ppermute | solution.py:224
  18.9 10.4 %collective-permute-start.2 = (bf16[72,1536]{1,0:T(8,128)(2,1)S(1)}, bf16[72,1536]{1,0:T(8,128)(2,1)S(1)}, u32[]{:S(2)}, u32[]{:S(2)}) collective-permute-start(bf16[72,1536]{1,0:T(8,128)(2,1)S(1)} %get-tuple-element.43.refs_1_), channel_id=1, source_target_pairs={{0,1},{3,2},{4,5},{7,6},{8,9},{11,10},{12,13},{15,14},{16,17},{19,... | collective-permute-start | bytes 663560 | tf_op jit(solution)/shard_map/ppermute | solution.py:224
  22.4 9.2 %collective-permute-start.4 = (bf16[1,2,72,896]{3,2,1,0:T(8,128)(2,1)S(1)}, bf16[1,2,72,896]{3,2,1,0:T(8,128)(2,1)S(1)}, u32[]{:S(2)}, u32[]{:S(2)}) collective-permute-start(bf16[1,2,72,896]{3,2,1,0:T(8,128)(2,1)S(1)} %collective-permute-done.refs_0_.refs_1_), channel_id=1, source_target_pairs={{0,4},{4,0},{1,5},{5,1},{2,6},{6,2},{3,7},{7,3},{8,12},{12,8},{9,1... | collective-permute-start | bytes 774152 | tf_op jit(solution)/shard_map/ppermute | solution.py:188
  23.9 12.3 %collective-permute-start.5 = (bf16[1,2,72,896]{3,2,1,0:T(8,128)(2,1)S(1)}, bf16[1,2,72,896]{3,2,1,0:T(8,128)(2,1)S(1)}, u32[]{:S(2)}, u32[]{:S(2)}) collective-permute-start(bf16[1,2,72,896]{3,2,1,0:T(8,128)(2,1)S(1)} %collective-permute-done.1.refs_1_.refs_2_), channel_id=1, source_target_pairs={{0,4},{4,0},{1,5},{5,1},{2,6},{6,2},{3,7},{7,3},{8,12},{12,8},{9,1... | collective-permute-start | bytes 774152 | tf_op jit(solution)/shard_map/ppermute | solution.py:188
  24.5 12.5 %collective-permute-start.13 = (bf16[72,1536]{1,0:T(8,128)(2,1)S(1)}, bf16[72,1536]{1,0:T(8,128)(2,1)S(1)}, u32[]{:S(2)}, u32[]{:S(2)}) collective-permute-start(bf16[72,1536]{1,0:T(8,128)(2,1)S(1)} %shard_map.114.s_ref), channel_id=1, source_target_pairs={{1,2},{2,1},{5,6},{6,5},{9,10},{10,9},{13,14},{14,13},{17,18},{18,... | collective-permute-start | bytes 663560 | tf_op jit(solution)/shard_map/ppermute | solution.py:236
  25.2 14.1 %collective-permute-start.22 = (bf16[72,1536]{1,0:T(8,128)(2,1)S(1)}, bf16[72,1536]{1,0:T(8,128)(2,1)S(1)}, u32[]{:S(2)}, u32[]{:S(2)}) collective-permute-start(bf16[72,1536]{1,0:T(8,128)(2,1)S(1)} %get-tuple-element.64.refs_1_), channel_id=1, source_target_pairs={{0,1},{3,2},{4,5},{7,6},{8,9},{11,10},{12,13},{15,14},{16,17},{19,... | collective-permute-start | bytes 663560 | tf_op jit(solution)/shard_map/ppermute | solution.py:224
  29.4 10.7 %collective-permute-start.3 = (bf16[72,1536]{1,0:T(8,128)(2,1)S(1)}, bf16[72,1536]{1,0:T(8,128)(2,1)S(1)}, u32[]{:S(2)}, u32[]{:S(2)}) collective-permute-start(bf16[72,1536]{1,0:T(8,128)(2,1)S(1)} %shard_map.104.s_ref), channel_id=1, source_target_pairs={{1,2},{2,1},{5,6},{6,5},{9,10},{10,9},{13,14},{14,13},{17,18},{18,... | collective-permute-start | bytes 663560 | tf_op jit(solution)/shard_map/ppermute | solution.py:236
  37.2 7.9 %collective-permute-start.14 = (bf16[72,1536]{1,0:T(8,128)(2,1)S(1)}, bf16[72,1536]{1,0:T(8,128)(2,1)S(1)}, u32[]{:S(2)}, u32[]{:S(2)}) collective-permute-start(bf16[72,1536]{1,0:T(8,128)(2,1)S(1)} %get-tuple-element.56), channel_id=1, source_target_pairs={{0,1},{3,2},{1,0},{2,3},{4,5},{7,6},{5,4},{6,7},{8,9},{11,10},{9,8... | collective-permute-start | bytes 663560 | tf_op jit(solution)/shard_map/ppermute | solution.py:224
  37.3 9.2 %collective-permute-start.16 = (bf16[1,2,72,896]{3,2,1,0:T(8,128)(2,1)S(1)}, bf16[1,2,72,896]{3,2,1,0:T(8,128)(2,1)S(1)}, u32[]{:S(2)}, u32[]{:S(2)}) collective-permute-start(bf16[1,2,72,896]{3,2,1,0:T(8,128)(2,1)S(1)} %get-tuple-element.48.refs_0_.refs_1_), channel_id=1, source_target_pairs={{0,4},{4,0},{1,5},{5,1},{2,6},{6,2},{3,7},{7,3},{8,12},{12,8},{9,1... | collective-permute-start | bytes 774152 | tf_op jit(solution)/shard_map/ppermute | solution.py:188
  38.8 11.5 %collective-permute-start.17 = (bf16[1,2,72,896]{3,2,1,0:T(8,128)(2,1)S(1)}, bf16[1,2,72,896]{3,2,1,0:T(8,128)(2,1)S(1)}, u32[]{:S(2)}, u32[]{:S(2)}) collective-permute-start(bf16[1,2,72,896]{3,2,1,0:T(8,128)(2,1)S(1)} %collective-permute-done.8.refs_1_.refs_0_), channel_id=1, source_target_pairs={{0,4},{4,0},{1,5},{5,1},{2,6},{6,2},{3,7},{7,3},{8,12},{12,8},{9,1... | collective-permute-start | bytes 774152 | tf_op jit(solution)/shard_map/ppermute | solution.py:188
  39.4 11.7 %collective-permute-start.23 = (bf16[72,1536]{1,0:T(8,128)(2,1)S(1)}, bf16[72,1536]{1,0:T(8,128)(2,1)S(1)}, u32[]{:S(2)}, u32[]{:S(2)}) collective-permute-start(bf16[72,1536]{1,0:T(8,128)(2,1)S(1)} %shard_map.125.s_ref), channel_id=1, source_target_pairs={{1,2},{2,1},{5,6},{6,5},{9,10},{10,9},{13,14},{14,13},{17,18},{18,... | collective-permute-start | bytes 663560 | tf_op jit(solution)/shard_map/ppermute | solution.py:236
  40.2 12.7 %collective-permute-start.6 = (bf16[72,1536]{1,0:T(8,128)(2,1)S(1)}, bf16[72,1536]{1,0:T(8,128)(2,1)S(1)}, u32[]{:S(2)}, u32[]{:S(2)}) collective-permute-start(bf16[72,1536]{1,0:T(8,128)(2,1)S(1)} %get-tuple-element.45), channel_id=1, source_target_pairs={{0,1},{3,2},{1,0},{2,3},{4,5},{7,6},{5,4},{6,7},{8,9},{11,10},{9,8... | collective-permute-start | bytes 663560 | tf_op jit(solution)/shard_map/ppermute | solution.py:224
  45.2 8.6 %collective-permute-start.15 = (bf16[72,1536]{1,0:T(8,128)(2,1)S(1)}, bf16[72,1536]{1,0:T(8,128)(2,1)S(1)}, u32[]{:S(2)}, u32[]{:S(2)}) collective-permute-start(bf16[72,1536]{1,0:T(8,128)(2,1)S(1)} %get-tuple-element.58.s_ref), channel_id=1, source_target_pairs={{1,2},{2,1},{5,6},{6,5},{9,10},{10,9},{13,14},{14,13},{17,18},{18,... | collective-permute-start | bytes 663560 | tf_op jit(solution)/shard_map/ppermute | solution.py:236
  51.2 7.4 %collective-permute-start.24 = (bf16[72,1536]{1,0:T(8,128)(2,1)S(1)}, bf16[72,1536]{1,0:T(8,128)(2,1)S(1)}, u32[]{:S(2)}, u32[]{:S(2)}) collective-permute-start(bf16[72,1536]{1,0:T(8,128)(2,1)S(1)} %get-tuple-element.66), channel_id=1, source_target_pairs={{0,1},{3,2},{1,0},{2,3},{4,5},{7,6},{5,4},{6,7},{8,9},{11,10},{9,8... | collective-permute-start | bytes 663560 | tf_op jit(solution)/shard_map/ppermute | solution.py:224
  53.0 6.3 %collective-permute-start.7 = (bf16[72,1536]{1,0:T(8,128)(2,1)S(1)}, bf16[72,1536]{1,0:T(8,128)(2,1)S(1)}, u32[]{:S(2)}, u32[]{:S(2)}) collective-permute-start(bf16[72,1536]{1,0:T(8,128)(2,1)S(1)} %get-tuple-element.47.s_ref), channel_id=1, source_target_pairs={{1,2},{2,1},{5,6},{6,5},{9,10},{10,9},{13,14},{14,13},{17,18},{18,... | collective-permute-start | bytes 663560 | tf_op jit(solution)/shard_map/ppermute | solution.py:236
  53.9 11.1 %collective-permute-start.18 = (bf16[72,1536]{1,0:T(8,128)(2,1)S(1)}, bf16[72,1536]{1,0:T(8,128)(2,1)S(1)}, u32[]{:S(2)}, u32[]{:S(2)}) collective-permute-start(bf16[72,1536]{1,0:T(8,128)(2,1)S(1)} %get-tuple-element.60), channel_id=1, source_target_pairs={{0,1},{3,2},{1,0},{2,3},{4,5},{7,6},{5,4},{6,7},{8,9},{11,10},{9,8... | collective-permute-start | bytes 663560 | tf_op jit(solution)/shard_map/ppermute | solution.py:224
  58.7 7.1 %collective-permute-start.25 = (bf16[72,1536]{1,0:T(8,128)(2,1)S(1)}, bf16[72,1536]{1,0:T(8,128)(2,1)S(1)}, u32[]{:S(2)}, u32[]{:S(2)}) collective-permute-start(bf16[72,1536]{1,0:T(8,128)(2,1)S(1)} %get-tuple-element.68.s_ref), channel_id=1, source_target_pairs={{1,2},{2,1},{5,6},{6,5},{9,10},{10,9},{13,14},{14,13},{17,18},{18,... | collective-permute-start | bytes 663560 | tf_op jit(solution)/shard_map/ppermute | solution.py:236
  59.5 11.5 %collective-permute-start.9 = (bf16[72,1536]{1,0:T(8,128)(2,1)S(1)}, bf16[72,1536]{1,0:T(8,128)(2,1)S(1)}, u32[]{:S(2)}, u32[]{:S(2)}) collective-permute-start(bf16[72,1536]{1,0:T(8,128)(2,1)S(1)} %get-tuple-element.51), channel_id=1, source_target_pairs={{0,1},{3,2},{1,0},{2,3},{4,5},{7,6},{5,4},{6,7},{8,9},{11,10},{9,8... | collective-permute-start | bytes 663560 | tf_op jit(solution)/shard_map/ppermute | solution.py:224
  65.1 6.7 %collective-permute-start.19 = (bf16[72,1536]{1,0:T(8,128)(2,1)S(1)}, bf16[72,1536]{1,0:T(8,128)(2,1)S(1)}, u32[]{:S(2)}, u32[]{:S(2)}) collective-permute-start(bf16[72,1536]{1,0:T(8,128)(2,1)S(1)} %get-tuple-element.62.s_ref), channel_id=1, source_target_pairs={{1,2},{2,1},{5,6},{6,5},{9,10},{10,9},{13,14},{14,13},{17,18},{18,... | collective-permute-start | bytes 663560 | tf_op jit(solution)/shard_map/ppermute | solution.py:236
  65.9 12.4 %collective-permute-start.26 = (bf16[72,1536]{1,0:T(8,128)(2,1)S(1)}, bf16[72,1536]{1,0:T(8,128)(2,1)S(1)}, u32[]{:S(2)}, u32[]{:S(2)}) collective-permute-start(bf16[72,1536]{1,0:T(8,128)(2,1)S(1)} %shard_map.128.refs_1_), channel_id=1, source_target_pairs={{1,0},{2,3},{5,4},{6,7},{9,8},{10,11},{13,12},{14,15},{17,16},{18,... | collective-permute-start | bytes 663560 | tf_op jit(solution)/shard_map/ppermute | solution.py:224
  71.1 13.0 %collective-permute-start.10 = (bf16[72,1536]{1,0:T(8,128)(2,1)S(1)}, bf16[72,1536]{1,0:T(8,128)(2,1)S(1)}, u32[]{:S(2)}, u32[]{:S(2)}) collective-permute-start(bf16[72,1536]{1,0:T(8,128)(2,1)S(1)} %get-tuple-element.53.s_ref), channel_id=1, source_target_pairs={{1,2},{2,1},{5,6},{6,5},{9,10},{10,9},{13,14},{14,13},{17,18},{18,... | collective-permute-start | bytes 663560 | tf_op jit(solution)/shard_map/ppermute | solution.py:236
  71.9 15.2 %collective-permute-start.20 = (bf16[72,1536]{1,0:T(8,128)(2,1)S(1)}, bf16[72,1536]{1,0:T(8,128)(2,1)S(1)}, u32[]{:S(2)}, u32[]{:S(2)}) collective-permute-start(bf16[72,1536]{1,0:T(8,128)(2,1)S(1)} %shard_map.120.refs_1_), channel_id=1, source_target_pairs={{1,0},{2,3},{5,4},{6,7},{9,8},{10,11},{13,12},{14,15},{17,16},{18,... | collective-permute-start | bytes 663560 | tf_op jit(solution)/shard_map/ppermute | solution.py:224
  79.0 7.9 %collective-permute-start.27 = (bf16[72,896]{1,0:T(8,128)(2,1)S(1)}, bf16[72,896]{1,0:T(8,128)(2,1)S(1)}, u32[]{:S(2)}, u32[]{:S(2)}) collective-permute-start(bf16[72,896]{1,0:T(8,128)(2,1)S(1)} %shard_map.130), channel_id=1, source_target_pairs={{0,4},{4,0},{1,5},{5,1},{2,6},{6,2},{3,7},{7,3},{8,12},{12,8},{9,1... | collective-permute-start | bytes 387080 | tf_op jit(solution)/shard_map/ppermute | solution.py:188
  81.2 5.8 %collective-permute-start.29 = (bf16[72,896]{1,0:T(8,128)(2,1)S(1)}, bf16[72,896]{1,0:T(8,128)(2,1)S(1)}, u32[]{:S(2)}, u32[]{:S(2)}) collective-permute-start(bf16[72,896]{1,0:T(8,128)(2,1)S(1)} %shard_map.133), channel_id=1, source_target_pairs={{0,4},{4,0},{1,5},{5,1},{2,6},{6,2},{3,7},{7,3},{8,12},{12,8},{9,1... | collective-permute-start | bytes 387080 | tf_op jit(solution)/shard_map/ppermute | solution.py:188
  82.5 7.4 %collective-permute-start.31 = (bf16[72,896]{1,0:T(8,128)(2,1)S(1)}, bf16[72,896]{1,0:T(8,128)(2,1)S(1)}, u32[]{:S(2)}, u32[]{:S(2)}) collective-permute-start(bf16[72,896]{1,0:T(8,128)(2,1)S(1)} %shard_map.135), channel_id=1, source_target_pairs={{0,4},{4,0},{1,5},{5,1},{2,6},{6,2},{3,7},{7,3},{8,12},{12,8},{9,1... | collective-permute-start | bytes 387080 | tf_op jit(solution)/shard_map/ppermute | solution.py:188
  84.2 7.8 %collective-permute-start.11 = (bf16[72,1536]{1,0:T(8,128)(2,1)S(1)}, bf16[72,1536]{1,0:T(8,128)(2,1)S(1)}, u32[]{:S(2)}, u32[]{:S(2)}) collective-permute-start(bf16[72,1536]{1,0:T(8,128)(2,1)S(1)} %shard_map.111.refs_1_), channel_id=1, source_target_pairs={{1,0},{2,3},{5,4},{6,7},{9,8},{10,11},{13,12},{14,15},{17,16},{18,... | collective-permute-start | bytes 663560 | tf_op jit(solution)/shard_map/ppermute | solution.py:224
  86.9 7.8 %collective-permute-start.28 = (bf16[72,896]{1,0:T(8,128)(2,1)S(1)}, bf16[72,896]{1,0:T(8,128)(2,1)S(1)}, u32[]{:S(2)}, u32[]{:S(2)}) collective-permute-start(bf16[72,896]{1,0:T(8,128)(2,1)S(1)} %shard_map.131), channel_id=1, source_target_pairs={{0,8},{8,0},{16,24},{24,16},{1,9},{9,1},{17,25},{25,17},{2,10},{10... | collective-permute-start | bytes 387080 | tf_op jit(solution)/shard_map/ppermute | solution.py:188
  87.8 6.9 %collective-permute-start.21 = (bf16[72,896]{1,0:T(8,128)(2,1)S(1)}, bf16[72,896]{1,0:T(8,128)(2,1)S(1)}, u32[]{:S(2)}, u32[]{:S(2)}) collective-permute-start(bf16[72,896]{1,0:T(8,128)(2,1)S(1)} %shard_map.122), channel_id=1, source_target_pairs={{0,4},{4,0},{1,5},{5,1},{2,6},{6,2},{3,7},{7,3},{8,12},{12,8},{9,1... | collective-permute-start | bytes 387080 | tf_op jit(solution)/shard_map/ppermute | solution.py:188
  88.4 6.4 %collective-permute-start.30 = (bf16[72,896]{1,0:T(8,128)(2,1)S(1)}, bf16[72,896]{1,0:T(8,128)(2,1)S(1)}, u32[]{:S(2)}, u32[]{:S(2)}) collective-permute-start(bf16[72,896]{1,0:T(8,128)(2,1)S(1)} %shard_map.134), channel_id=1, source_target_pairs={{0,16},{8,24},{16,0},{24,8},{1,17},{9,25},{17,1},{25,9},{2,18},{10... | collective-permute-start | bytes 387080 | tf_op jit(solution)/shard_map/ppermute | solution.py:188
  89.9 6.0 %collective-permute-start.32 = (bf16[72,896]{1,0:T(8,128)(2,1)S(1)}, bf16[72,896]{1,0:T(8,128)(2,1)S(1)}, u32[]{:S(2)}, u32[]{:S(2)}) collective-permute-start(bf16[72,896]{1,0:T(8,128)(2,1)S(1)} %shard_map.136), channel_id=1, source_target_pairs={{0,24},{8,16},{16,8},{24,0},{1,25},{9,17},{17,9},{25,1},{2,26},{10... | collective-permute-start | bytes 387080 | tf_op jit(solution)/shard_map/ppermute | solution.py:188
  92.7 3.2 %copy-start.3 = (s32[192,1]{0,1:T(1,128)S(1)}, s32[192,1]{0,1:T(1,128)}, u32[]{:S(2)}) copy-start(s32[192,1]{0,1:T(1,128)} %param.10) | copy-start | bytes 2308
  92.7 3.2 %copy-start.4 = (f32[192]{0:T(256)S(1)}, f32[192]{0:T(256)}, u32[]{:S(2)}) copy-start(f32[192]{0:T(256)} %param.9) | copy-start | bytes 2308

commit v4 on v3

--- a/solution.py
+++ b/solution.py
@@ -69,6 +69,7 @@
     scaled = (column(rw_ref[...]) * cot_ref[...].astype(F32)).astype(BF16)
     for k in range(n_expert):
         pick = slots(ids, rank, lax.axis_index("expert") ^ k, cap)
+        outs[n_expert][k] = pick
         outs[k][0, 0] = mm(pick, tokens, TN).astype(BF16)
         outs[k][0, 1] = mm(pick, scaled, TN).astype(BF16)
 
@@ -132,17 +133,19 @@
 
 
 def out_body(half, n, *refs):
-    acts, (wg_ref, wu_ref, o_ref) = refs[:n], refs[n:]
+    acts, (wg_ref, wu_ref), outs = refs[:n], refs[n:n + 2], refs[n + 2:]
     a = jnp.concatenate([r[:, :2 * half] for r in acts], axis=0)
-    o_ref[...] = (mm(a[:, :half], wg_ref[...], NT) + mm(a[:, half:], wu_ref[...], NT)).astype(BF16)
-
-
-def total_body(start, mine_ref, *refs):
-    o_ref = refs[-1]
-    value = mine_ref[start:start + o_ref.shape[0]].astype(F32)
-    for r in refs[:-1]:
+    o = (mm(a[:, :half], wg_ref[...], NT) + mm(a[:, half:], wu_ref[...], NT)).astype(BF16)
+    size = o.shape[0] // n
+    for i in range(n):
+        outs[i][...] = o[i * size:(i + 1) * size]
+
+
+def total_body(*refs):
+    value = refs[0][...].astype(F32)
+    for r in refs[1:-1]:
         value = value + r[...].astype(F32)
-    o_ref[...] = value.astype(BF16)
+    refs[-1][...] = value.astype(BF16)
 
 
 def wgrad_body(half, n, last, *refs):
@@ -160,12 +163,10 @@
         rest[1][...] = gd
 
 
-def final_body(n_expert, cap, ids_ref, rw_ref, *refs):
-    ids = column(ids_ref[...])
-    rank = ranks(ids)
+def final_body(n_expert, rw_ref, pick_ref, *refs):
     total = None
     for k in range(n_expert):
-        term = mm(slots(ids, rank, lax.axis_index("expert") ^ k, cap), refs[k][...], NN)
+        term = mm(pick_ref[k], refs[k][...], NN)
         total = term if total is None else total + term
     refs[n_expert][...] = (column(rw_ref[...]) * total).astype(BF16)
 
@@ -188,7 +189,7 @@
         return lax.ppermute(x, axis, [(i, i ^ k) for i in range(lax.axis_size(axis))])
 
     send = call(
-        functools.partial(send_body, n_expert, cap), [keep(1, 2, cap, quarter)] * n_expert,
+        functools.partial(send_body, n_expert, cap), [keep(1, 2, cap, quarter)] * n_expert + [keep(n_expert, count, cap)],
         (ids, rw, tokens, cotangent), (0, 1, 2, 3),
     )
     got = [send[0]] + [swap(send[k], "expert", k) for k in range(1, n_expert)]
@@ -202,16 +203,16 @@
     size = each * cap
     parts = {}
     for q in range(n_rep):
-        for pair in ((0, 1), (2, 3)):
+        for js in ((0, 1), (2, 3)) if q == 0 else ((0,), (1,), (2,), (3,)):
             done = call(
-                functools.partial(part_body, half, 2), [keep(size, 3 * half)] * 2,
-                (*[rows[q, j] for j in pair], w_gate, w_up, w_down),
-                (2, 3, 4) if (q, pair) == (0, (0, 1)) else (),
+                functools.partial(part_body, half, len(js)), [keep(size, 3 * half)] * len(js),
+                (*[rows[q, j] for j in js], w_gate, w_up, w_down),
+                (2, 3, 4) if (q, js[0]) == (0, 0) else (),
             )
-            parts[q, pair[0]], parts[q, pair[1]] = done
-
-    waves = [(0, 1), (0, 2), (0, 3)]
-    waves += [(q, j) for q in range(1, n_rep) for j in (2, 3, 1, 0)] + [(0, 0)]
+            for n, j in enumerate(js):
+                parts[q, j] = done[n]
+
+    waves = [(0, 1)] + [(q, j) for j in range(4) for q in range(1, n_rep)] + [(0, 2), (0, 3), (0, 0)]
     lag = 3
     inward, outward, middle = [(0, 1), (3, 2)], [(1, 0), (2, 3)], [(1, 2), (2, 1)]
     acts, full = {}, {}
@@ -237,26 +238,23 @@
             )
             acts[now], leaving[i + lag] = both[0], both[-1]
 
-    def out(q, js):
-        return call(
-            functools.partial(out_body, half, len(js)), keep(len(js) * size, quarter),
-            (*[full[q, j] for j in js], w_gate, w_up),
+    groups = [[(0, 1)] + [(q, 0) for q in range(1, n_rep)]]
+    groups += [[(q, j)] for j in range(1, 4) for q in range(1, n_rep)] + [[(0, 2)], [(0, 3)], [(0, 0)]]
+    outs = {}
+    for group in groups:
+        done = call(
+            functools.partial(out_body, half, len(group)), [keep(size, quarter)] * len(group),
+            (*[full[w] for w in group], w_gate, w_up),
         )
-
-    mine = {}
-    for js in ((2, 3), (1,), (0,)):
-        rows_of = out(0, js)
-        for n, j in enumerate(js):
-            mine[j] = (n, rows_of)
+        outs.update(zip(group, done))
     total = {}
     for j in range(4):
-        back = [swap(out(q, (j,)), "replica", q) for q in range(1, n_rep)]
-        n, rows_of = mine[j]
-        total[j] = call(functools.partial(total_body, n * size), keep(size, quarter), (rows_of, *back))
+        back = [swap(outs[q, j], "replica", q) for q in range(1, n_rep)]
+        total[j] = call(total_body, keep(size, quarter), (outs[0, j], *back))
     ret = [total[k // each][k % each * cap:(k % each + 1) * cap] for k in range(n_expert)]
     ret = [ret[0]] + [swap(ret[k], "expert", k) for k in range(1, n_expert)]
     sds = jax.ShapeDtypeStruct
-    token_grad = call(functools.partial(final_body, n_expert, cap), sds((count, quarter), BF16), (ids, rw, *ret))
+    token_grad = call(functools.partial(final_body, n_expert), sds((count, quarter), BF16), (rw, send[n_expert], *ret))
     early, late = waves[:-2], waves[-2:]
     part_x, part_d = call(
         functools.partial(wgrad_body, half, len(early), False),

time: 98.4 us -> 88.6 us (0.900)
  starting transfers between devices: 49.2 us -> 43.6 us
  waiting for transfers between devices: 28.3 us -> 23.5 us
    ppermute x14, waiting for transfers between devices: 17.6 us -> 9.46 us  [swap(): lax.ppermute(x, axis, [(i, i ^ k) for i in range(lax.axis_size(axis))])]
    ppermute x11, starting transfers between devices: 30.5 us -> 25.1 us  [steps(): came = lax.ppermute(leaving[i], 'seq', pairs)]
    ppermute x11, waiting for transfers between devices: 10.7 us -> 14 us  [steps(): came = lax.ppermute(leaving[i], 'seq', pairs)]
    pallas_call x38 -> x40, Pallas kernels: 18.9 us -> 19.8 us  [call(): pl.pallas_call(body, out_shape=outs, in_specs=[pl.BlockSpec(memory_space=...]
  transfers between devices with their start and end apart: 33 -> 33, of which waited for: 11 -> 15; matrix products, arithmetic and copies ran while one was open for 0% -> 0% of each run, Pallas kernels for 15% -> 19%
where the time goes in v4:
time: 88.6 us; the launch traced here: 88.1 us
  starting transfers between devices  43.6 us (49%)
  waiting for transfers between devices  23.5 us (27%)
  Pallas kernels  19.8 us (22%)
  between operations  1.16 us (1%)
    ppermute x11, starting transfers between devices, steps(): came = lax.ppermute(leaving[i], 'seq', pairs)  25.1 us
    pallas_call x40, Pallas kernels, call(): pl.pallas_call(body, out_shape=outs, in_specs=[pl.BlockSpec(memory_space=...  19.8 us
    ppermute x11, waiting for transfers between devices, steps(): came = lax.ppermute(leaving[i], 'seq', pairs)  14 us
    ppermute x14, starting transfers between devices, swap(): lax.ppermute(x, axis, [(i, i ^ k) for i in range(lax.axis_size(axis))])  13.1 us
    ppermute x14, waiting for transfers between devices, swap(): lax.ppermute(x, axis, [(i, i ^ k) for i in range(lax.axis_size(axis))])  9.46 us
    ppermute x8, starting transfers between devices, steps(): lax.ppermute(done[0], 'seq', middle)  5.4 us
  transfers between devices with their start and end apart: 33, of which 15 were waited for; matrix products, arithmetic and copies ran while one was open for 0% of the time, Pallas kernels for 19%

profile of v4, /device:TPU:0, one launch (start us, length us, event | category | flops | bytes accessed | tf_op | source)
XLA Modules:
  0.0 88.1 jit_solution(15593404714541036403)
XLA Ops:
  0.7 2.3 %shard_map.102 = (bf16[1,2,72,896]{3,2,1,0:T(8,128)(2,1)S(1)}, bf16[1,2,72,896]{3,2,1,0:T(8,128)(2,1)S(1)}, bf16[1,2,72,896]{3,2,1,0:T(8,128)(2,1)S(1)}, bf16[1,...) custom-call(s32[1,192]{1,0:T(1,128)} %bitcast.39, f32[1,192]{1,0:T(1,128)} %bitcast.37, bf16[192,896]{1,0:T(8,128)(2,1)} %tokens_ref.1, ...), custom_call_target="tpu_custom_call" | custom-call | tf_op jit(solution)/shard_map/pallas_call | solution.py:34
  3.5 2.6 %collective-permute-start = (bf16[1,2,72,896]{3,2,1,0:T(8,128)(2,1)S(1)}, bf16[1,2,72,896]{3,2,1,0:T(8,128)(2,1)S(1)}, u32[]{:S(2)}, u32[]{:S(2)}) collective-permute-start(bf16[1,2,72,896]{3,2,1,0:T(8,128)(2,1)S(1)} %get-tuple-element.41.refs_0_.refs_1_), channel_id=1, source_target_pairs={{0,4},{4,0},{1,5},{5,1},{2,6},{6,2},{3,7},{7,3},{8,12},{12,8},{9,1... | collective-permute-start | bytes 774152 | tf_op jit(solution)/shard_map/ppermute | solution.py:189
  6.1 1.5 %collective-permute-start.13 = (bf16[1,2,72,896]{3,2,1,0:T(8,128)(2,1)S(1)}, bf16[1,2,72,896]{3,2,1,0:T(8,128)(2,1)S(1)}, u32[]{:S(2)}, u32[]{:S(2)}) collective-permute-start(bf16[1,2,72,896]{3,2,1,0:T(8,128)(2,1)S(1)} %get-tuple-element.52), channel_id=1, source_target_pairs={{0,16},{8,24},{16,0},{24,8},{1,17},{9,25},{17,1},{25,9},{2,18},{10... | collective-permute-start | bytes 774152 | tf_op jit(solution)/shard_map/ppermute | solution.py:189
  7.6 2.5 %shard_map.108 = (bf16[72,1536]{1,0:T(8,128)(2,1)S(1)}, bf16[72,1536]{1,0:T(8,128)(2,1)S(1)}) custom-call(bf16[1,2,72,896]{3,2,1,0:T(8,128)(2,1)S(1)} %get-tuple-element.41.refs_0_.refs_1_, bf16[1,2,72,896]{3,2,1,0:T(8,128)(2,1)S(1)} %collective-permute-done.7.refs_1_.refs_0_, bf16[896,512]{1,0:T(8,128)(2,1)} %bitcast.5, bf16[896,512]{1,0:T(8,128)(2,1)} %bitcast.18, ...), custom_call_target="tpu_custom_call" | custom-call | tf_op jit(solution)/shard_map/pallas_call | solution.py:34
  10.1 3.5 %collective-permute-start.11 = (bf16[72,1536]{1,0:T(8,128)(2,1)S(1)}, bf16[72,1536]{1,0:T(8,128)(2,1)S(1)}, u32[]{:S(2)}, u32[]{:S(2)}) collective-permute-start(bf16[72,1536]{1,0:T(8,128)(2,1)S(1)} %get-tuple-element.51.refs_1_), channel_id=1, source_target_pairs={{0,1},{3,2},{4,5},{7,6},{8,9},{11,10},{12,13},{15,14},{16,17},{19,... | collective-permute-start | bytes 663560 | tf_op jit(solution)/shard_map/ppermute | solution.py:225
  13.7 0.7 shard_map.103.refs_1_
  14.4 2.9 %collective-permute-start.1 = (bf16[72,1536]{1,0:T(8,128)(2,1)S(1)}, bf16[72,1536]{1,0:T(8,128)(2,1)S(1)}, u32[]{:S(2)}, u32[]{:S(2)}) collective-permute-start(bf16[72,1536]{1,0:T(8,128)(2,1)S(1)} %shard_map.103.refs_1_), channel_id=1, source_target_pairs={{0,1},{3,2},{4,5},{7,6},{8,9},{11,10},{12,13},{15,14},{16,17},{19,... | collective-permute-start | bytes 663560 | tf_op jit(solution)/shard_map/ppermute | solution.py:225
  17.4 1.6 %collective-permute-start.17 = (bf16[1,2,72,896]{3,2,1,0:T(8,128)(2,1)S(1)}, bf16[1,2,72,896]{3,2,1,0:T(8,128)(2,1)S(1)}, u32[]{:S(2)}, u32[]{:S(2)}) collective-permute-start(bf16[1,2,72,896]{3,2,1,0:T(8,128)(2,1)S(1)} %collective-permute-done.7.refs_1_.refs_0_), channel_id=1, source_target_pairs={{0,4},{4,0},{1,5},{5,1},{2,6},{6,2},{3,7},{7,3},{8,12},{12,8},{9,1... | collective-permute-start | bytes 774152 | tf_op jit(solution)/shard_map/ppermute | solution.py:189
  19.5 0.7 collective-permute-start.12
  20.2 1.7 %collective-permute-done.3.refs_1_.refs_0_ = bf16[1,2,72,896]{3,2,1,0:T(8,128)(2,1)S(1)} collective-permute-done((bf16[1,2,72,896]{3,2,1,0:T(8,128)(2,1)S(1)}, bf16[1,2,72,896]{3,2,1,0:T(8,128)(2,1)S(1)}, u32[]{:S(2)}, u32[]{:S(2)}) %collective-permute-start.3) | collective-permute-done | bytes 258080 | tf_op jit(solution)/shard_map/ppermute | solution.py:189
  23.1 0.7 collective-permute-start.2
  23.8 2.8 %collective-permute-done.17.refs_0_.refs_2_ = bf16[1,2,72,896]{3,2,1,0:T(8,128)(2,1)S(1)} collective-permute-done((bf16[1,2,72,896]{3,2,1,0:T(8,128)(2,1)S(1)}, bf16[1,2,72,896]{3,2,1,0:T(8,128)(2,1)S(1)}, u32[]{:S(2)}, u32[]{:S(2)}) %collective-permute-start.17) | collective-permute-done | bytes 258080 | tf_op jit(solution)/shard_map/ppermute | solution.py:189
  26.5 0.7 shard_map.120.refs_1_
  27.3 4.5 %collective-permute-start.18 = (bf16[72,1536]{1,0:T(8,128)(2,1)S(1)}, bf16[72,1536]{1,0:T(8,128)(2,1)S(1)}, u32[]{:S(2)}, u32[]{:S(2)}) collective-permute-start(bf16[72,1536]{1,0:T(8,128)(2,1)S(1)} %shard_map.120.refs_1_), channel_id=1, source_target_pairs={{0,1},{3,2},{4,5},{7,6},{8,9},{11,10},{12,13},{15,14},{16,17},{19,... | collective-permute-start | bytes 663560 | tf_op jit(solution)/shard_map/ppermute | solution.py:225
  32.0 0.7 shard_map.115.refs_0_.refs_1_
  33.0 2.9 %collective-permute-done.4.refs_0_.refs_4_ = bf16[1,2,72,896]{3,2,1,0:T(8,128)(2,1)S(1)} collective-permute-done((bf16[1,2,72,896]{3,2,1,0:T(8,128)(2,1)S(1)}, bf16[1,2,72,896]{3,2,1,0:T(8,128)(2,1)S(1)}, u32[]{:S(2)}, u32[]{:S(2)}) %collective-permute-start.4) | collective-permute-done | bytes 258080 | tf_op jit(solution)/shard_map/ppermute | solution.py:189
  35.9 0.7 shard_map.105.refs_0_.refs_1_
  37.6 0.7 collective-permute-start.19
  38.2 4.0 %collective-permute-done.15.refs_0_ = bf16[72,1536]{1,0:T(8,128)(2,1)S(1)} collective-permute-done((bf16[72,1536]{1,0:T(8,128)(2,1)S(1)}, bf16[72,1536]{1,0:T(8,128)(2,1)S(1)}, u32[]{:S(2)}, u32[]{:S(2)}) %collective-permute-start.15) | collective-permute-done | bytes 221216 | tf_op jit(solution)/shard_map/ppermute | solution.py:225
  42.3 0.7 collective-permute-start.25
  43.0 1.7 %collective-permute-done.5.refs_0_ = bf16[72,1536]{1,0:T(8,128)(2,1)S(1)} collective-permute-done((bf16[72,1536]{1,0:T(8,128)(2,1)S(1)}, bf16[72,1536]{1,0:T(8,128)(2,1)S(1)}, u32[]{:S(2)}, u32[]{:S(2)}) %collective-permute-start.5) | collective-permute-done | bytes 221216 | tf_op jit(solution)/shard_map/ppermute | solution.py:225
  44.8 0.7 collective-permute-start.6
  45.5 0.8 shard_map.122
  46.4 5.3 %collective-permute-start.20 = (bf16[72,1536]{1,0:T(8,128)(2,1)S(1)}, bf16[72,1536]{1,0:T(8,128)(2,1)S(1)}, u32[]{:S(2)}, u32[]{:S(2)}) collective-permute-start(bf16[72,1536]{1,0:T(8,128)(2,1)S(1)} %get-tuple-element.60), channel_id=1, source_target_pairs={{0,1},{3,2},{1,0},{2,3},{4,5},{7,6},{5,4},{6,7},{8,9},{11,10},{9,8... | collective-permute-start | bytes 663560 | tf_op jit(solution)/shard_map/ppermute | solution.py:225
  51.9 2.7 %collective-permute-start.26 = (bf16[72,1536]{1,0:T(8,128)(2,1)S(1)}, bf16[72,1536]{1,0:T(8,128)(2,1)S(1)}, u32[]{:S(2)}, u32[]{:S(2)}) collective-permute-start(bf16[72,1536]{1,0:T(8,128)(2,1)S(1)} %get-tuple-element.66), channel_id=1, source_target_pairs={{0,1},{3,2},{1,0},{2,3},{4,5},{7,6},{5,4},{6,7},{8,9},{11,10},{9,8... | collective-permute-start | bytes 663560 | tf_op jit(solution)/shard_map/ppermute | solution.py:225
  54.8 2.2 %collective-permute-start.8 = (bf16[72,1536]{1,0:T(8,128)(2,1)S(1)}, bf16[72,1536]{1,0:T(8,128)(2,1)S(1)}, u32[]{:S(2)}, u32[]{:S(2)}) collective-permute-start(bf16[72,1536]{1,0:T(8,128)(2,1)S(1)} %get-tuple-element.48), channel_id=1, source_target_pairs={{0,1},{3,2},{1,0},{2,3},{4,5},{7,6},{5,4},{6,7},{8,9},{11,10},{9,8... | collective-permute-start | bytes 663560 | tf_op jit(solution)/shard_map/ppermute | solution.py:225
  57.5 0.7 collective-permute-start.23
  58.2 2.8 %collective-permute-done.26.refs_0_ = bf16[72,1536]{1,0:T(8,128)(2,1)S(1)} collective-permute-done((bf16[72,1536]{1,0:T(8,128)(2,1)S(1)}, bf16[72,1536]{1,0:T(8,128)(2,1)S(1)}, u32[]{:S(2)}, u32[]{:S(2)}) %collective-permute-start.26) | collective-permute-done | bytes 221216 | tf_op jit(solution)/shard_map/ppermute | solution.py:225
  61.0 0.7 collective-permute-start.29
  61.7 1.6 %collective-permute-done.8.refs_0_ = bf16[72,1536]{1,0:T(8,128)(2,1)S(1)} collective-permute-done((bf16[72,1536]{1,0:T(8,128)(2,1)S(1)}, bf16[72,1536]{1,0:T(8,128)(2,1)S(1)}, u32[]{:S(2)}, u32[]{:S(2)}) %collective-permute-start.8) | collective-permute-done | bytes 221216 | tf_op jit(solution)/shard_map/ppermute | solution.py:225
  64.2 1.3 %collective-permute-start.24 = (bf16[72,1536]{1,0:T(8,128)(2,1)S(1)}, bf16[72,1536]{1,0:T(8,128)(2,1)S(1)}, u32[]{:S(2)}, u32[]{:S(2)}) collective-permute-start(bf16[72,1536]{1,0:T(8,128)(2,1)S(1)} %shard_map.127.refs_1_), channel_id=1, source_target_pairs={{1,0},{2,3},{5,4},{6,7},{9,8},{10,11},{13,12},{14,15},{17,16},{18,... | collective-permute-start | bytes 663560 | tf_op jit(solution)/shard_map/ppermute | solution.py:225
  65.5 0.7 shard_map.125
  66.2 0.8 collective-permute-start.21
  67.2 1.3 %collective-permute-start.30 = (bf16[72,1536]{1,0:T(8,128)(2,1)S(1)}, bf16[72,1536]{1,0:T(8,128)(2,1)S(1)}, u32[]{:S(2)}, u32[]{:S(2)}) collective-permute-start(bf16[72,1536]{1,0:T(8,128)(2,1)S(1)} %shard_map.134.refs_1_), channel_id=1, source_target_pairs={{1,0},{2,3},{5,4},{6,7},{9,8},{10,11},{13,12},{14,15},{17,16},{18,... | collective-permute-start | bytes 663560 | tf_op jit(solution)/shard_map/ppermute | solution.py:225
  68.5 0.7 shard_map.132
  69.1 1.3 %collective-permute-start.27 = (bf16[72,896]{1,0:T(8,128)(2,1)S(1)}, bf16[72,896]{1,0:T(8,128)(2,1)S(1)}, u32[]{:S(2)}, u32[]{:S(2)}) collective-permute-start(bf16[72,896]{1,0:T(8,128)(2,1)S(1)} %shard_map.132), channel_id=1, source_target_pairs={{0,4},{4,0},{1,5},{5,1},{2,6},{6,2},{3,7},{7,3},{8,12},{12,8},{9,1... | collective-permute-start | bytes 387080 | tf_op jit(solution)/shard_map/ppermute | solution.py:189
  71.1 0.8 collective-permute-start.31
  72.6 1.3 %collective-permute-start.10 = (bf16[72,1536]{1,0:T(8,128)(2,1)S(1)}, bf16[72,1536]{1,0:T(8,128)(2,1)S(1)}, u32[]{:S(2)}, u32[]{:S(2)}) collective-permute-start(bf16[72,1536]{1,0:T(8,128)(2,1)S(1)} %shard_map.111.refs_1_), channel_id=1, source_target_pairs={{1,0},{2,3},{5,4},{6,7},{9,8},{10,11},{13,12},{14,15},{17,16},{18,... | collective-permute-start | bytes 663560 | tf_op jit(solution)/shard_map/ppermute | solution.py:225
  73.9 0.7 shard_map.118
  74.9 1.5 %collective-permute-start.16 = (bf16[72,896]{1,0:T(8,128)(2,1)S(1)}, bf16[72,896]{1,0:T(8,128)(2,1)S(1)}, u32[]{:S(2)}, u32[]{:S(2)}) collective-permute-start(bf16[72,896]{1,0:T(8,128)(2,1)S(1)} %get-tuple-element.57), channel_id=1, source_target_pairs={{0,4},{4,0},{1,5},{5,1},{2,6},{6,2},{3,7},{7,3},{8,12},{12,8},{9,1... | collective-permute-start | bytes 387080 | tf_op jit(solution)/shard_map/ppermute | solution.py:189
  76.4 0.7 shard_map.129.refs_0_
  77.2 2.0 %collective-permute-done.30.refs_0_ = bf16[72,1536]{1,0:T(8,128)(2,1)S(1)} collective-permute-done((bf16[72,1536]{1,0:T(8,128)(2,1)S(1)}, bf16[72,1536]{1,0:T(8,128)(2,1)S(1)}, u32[]{:S(2)}, u32[]{:S(2)}) %collective-permute-start.30) | collective-permute-done | bytes 221216 | tf_op jit(solution)/shard_map/ppermute | solution.py:225
  79.2 1.1 %collective-permute-start.28 = (bf16[72,896]{1,0:T(8,128)(2,1)S(1)}, bf16[72,896]{1,0:T(8,128)(2,1)S(1)}, u32[]{:S(2)}, u32[]{:S(2)}) collective-permute-start(bf16[72,896]{1,0:T(8,128)(2,1)S(1)} %shard_map.133), channel_id=1, source_target_pairs={{0,16},{8,24},{16,0},{24,8},{1,17},{9,25},{17,1},{25,9},{2,18},{10... | collective-permute-start | bytes 387080 | tf_op jit(solution)/shard_map/ppermute | solution.py:189
  80.3 0.7 shard_map.136.refs_0_
  81.2 1.7 %shard_map.140 = (f32[896,1024]{1,0:T(8,128)S(1)}, f32[512,896]{1,0:T(8,128)S(1)}) custom-call(bf16[1,2,72,896]{3,2,1,0:T(8,128)(2,1)S(1)} %collective-permute-done.7.refs_1_.refs_0_, bf16[1,2,72,896]{3,2,1,0:T(8,128)(2,1)S(1)} %collective-permute-done.refs_0_.refs_1_, bf16[1,2,72,896]{3,2,1,0:T(8,128)(2,1)S(1)} %collective-permute-done.17.refs_0_.refs_2_, ...), custom_call_target="tpu_custom_call" | custom-call | tf_op jit(solution)/shard_map/pallas_call | solution.py:34
  83.7 2.0 %shard_map.141 = (bf16[1,896,512]{2,1,0:T(8,128)(2,1)}, bf16[1,896,512]{2,1,0:T(8,128)(2,1)}, bf16[1,512,896]{2,1,0:T(8,128)(2,1)}) custom-call(bf16[1,2,72,896]{3,2,1,0:T(8,128)(2,1)S(1)} %collective-permute-done.3.refs_1_.refs_0_, bf16[1,2,72,896]{3,2,1,0:T(8,128)(2,1)S(1)} %get-tuple-element.41.refs_0_.refs_1_, ...), custom_call_target="tpu_custom_call" | custom-call | tf_op jit(solution)/shard_map/pallas_call | solution.py:34
  85.7 1.2 %collective-permute-done.32.refs_3_ = bf16[72,896]{1,0:T(8,128)(2,1)S(1)} collective-permute-done((bf16[72,896]{1,0:T(8,128)(2,1)S(1)}, bf16[72,896]{1,0:T(8,128)(2,1)S(1)}, u32[]{:S(2)}, u32[]{:S(2)}) %collective-permute-start.32) | collective-permute-done | bytes 129056 | tf_op jit(solution)/shard_map/ppermute | solution.py:189
  86.9 1.2 %shard_map.139 = bf16[192,896]{1,0:T(8,128)(2,1)} custom-call(f32[1,192]{1,0:T(1,128)S(1)} %bitcast.38, bf16[4,192,72]{2,1,0:T(8,128)(2,1)S(1)} %get-tuple-element.40.pick_ref, bf16[72,896]{1,0:T(8,128)(2,1)S(1)} %shard_map.119.refs_0_, bf16[72,896]{1,0:T(8,128)(2,1)S(1)} %collective-permute-done.22.refs_1_, ...), custom_call_target="tpu_custom_call" | custom-call | tf_op jit(solution)/shard_map/pallas_call | solution.py:34
  (66 shorter events, 8.4 us)
Async XLA Ops:
  0.6 13.0 %copy-start.2 = (bf16[1,512,896]{2,1,0:T(8,128)(2,1)S(1)}, bf16[1,512,896]{2,1,0:T(8,128)(2,1)}, u32[]{:S(2)}) copy-start(bf16[1,512,896]{2,1,0:T(8,128)(2,1)} %param.13) | copy-start | bytes 2752516
  0.6 13.0 %copy-start.1 = (bf16[1,896,512]{2,1,0:T(8,128)(2,1)S(1)}, bf16[1,896,512]{2,1,0:T(8,128)(2,1)}, u32[]{:S(2)}) copy-start(bf16[1,896,512]{2,1,0:T(8,128)(2,1)} %param.12) | copy-start | bytes 2752516
  0.7 13.0 %copy-start = (bf16[1,896,512]{2,1,0:T(8,128)(2,1)S(1)}, bf16[1,896,512]{2,1,0:T(8,128)(2,1)}, u32[]{:S(2)}) copy-start(bf16[1,896,512]{2,1,0:T(8,128)(2,1)} %param.11) | copy-start | bytes 2752516
  2.9 4.6 %collective-permute-start.7 = (bf16[1,2,72,896]{3,2,1,0:T(8,128)(2,1)S(1)}, bf16[1,2,72,896]{3,2,1,0:T(8,128)(2,1)S(1)}, u32[]{:S(2)}, u32[]{:S(2)}) collective-permute-start(bf16[1,2,72,896]{3,2,1,0:T(8,128)(2,1)S(1)} %get-tuple-element.46), channel_id=1, source_target_pairs={{0,8},{8,0},{16,24},{24,16},{1,9},{9,1},{17,25},{25,17},{2,10},{10... | collective-permute-start | bytes 774152 | tf_op jit(solution)/shard_map/ppermute | solution.py:189
  3.5 10.2 %collective-permute-start = (bf16[1,2,72,896]{3,2,1,0:T(8,128)(2,1)S(1)}, bf16[1,2,72,896]{3,2,1,0:T(8,128)(2,1)S(1)}, u32[]{:S(2)}, u32[]{:S(2)}) collective-permute-start(bf16[1,2,72,896]{3,2,1,0:T(8,128)(2,1)S(1)} %get-tuple-element.41.refs_0_.refs_1_), channel_id=1, source_target_pairs={{0,4},{4,0},{1,5},{5,1},{2,6},{6,2},{3,7},{7,3},{8,12},{12,8},{9,1... | collective-permute-start | bytes 774152 | tf_op jit(solution)/shard_map/ppermute | solution.py:189
  6.1 12.9 %collective-permute-start.13 = (bf16[1,2,72,896]{3,2,1,0:T(8,128)(2,1)S(1)}, bf16[1,2,72,896]{3,2,1,0:T(8,128)(2,1)S(1)}, u32[]{:S(2)}, u32[]{:S(2)}) collective-permute-start(bf16[1,2,72,896]{3,2,1,0:T(8,128)(2,1)S(1)} %get-tuple-element.52), channel_id=1, source_target_pairs={{0,16},{8,24},{16,0},{24,8},{1,17},{9,25},{17,1},{25,9},{2,18},{10... | collective-permute-start | bytes 774152 | tf_op jit(solution)/shard_map/ppermute | solution.py:189
  10.1 9.4 %collective-permute-start.11 = (bf16[72,1536]{1,0:T(8,128)(2,1)S(1)}, bf16[72,1536]{1,0:T(8,128)(2,1)S(1)}, u32[]{:S(2)}, u32[]{:S(2)}) collective-permute-start(bf16[72,1536]{1,0:T(8,128)(2,1)S(1)} %get-tuple-element.51.refs_1_), channel_id=1, source_target_pairs={{0,1},{3,2},{4,5},{7,6},{8,9},{11,10},{12,13},{15,14},{16,17},{19,... | collective-permute-start | bytes 663560 | tf_op jit(solution)/shard_map/ppermute | solution.py:225
  13.6 8.4 %collective-permute-start.3 = (bf16[1,2,72,896]{3,2,1,0:T(8,128)(2,1)S(1)}, bf16[1,2,72,896]{3,2,1,0:T(8,128)(2,1)S(1)}, u32[]{:S(2)}, u32[]{:S(2)}) collective-permute-start(bf16[1,2,72,896]{3,2,1,0:T(8,128)(2,1)S(1)} %get-tuple-element.42), channel_id=1, source_target_pairs={{0,24},{8,16},{16,8},{24,0},{1,25},{9,17},{17,9},{25,1},{2,26},{10... | collective-permute-start | bytes 774152 | tf_op jit(solution)/shard_map/ppermute | solution.py:189
  14.4 8.6 %collective-permute-start.1 = (bf16[72,1536]{1,0:T(8,128)(2,1)S(1)}, bf16[72,1536]{1,0:T(8,128)(2,1)S(1)}, u32[]{:S(2)}, u32[]{:S(2)}) collective-permute-start(bf16[72,1536]{1,0:T(8,128)(2,1)S(1)} %shard_map.103.refs_1_), channel_id=1, source_target_pairs={{0,1},{3,2},{4,5},{7,6},{8,9},{11,10},{12,13},{15,14},{16,17},{19,... | collective-permute-start | bytes 663560 | tf_op jit(solution)/shard_map/ppermute | solution.py:225
  17.4 9.2 %collective-permute-start.17 = (bf16[1,2,72,896]{3,2,1,0:T(8,128)(2,1)S(1)}, bf16[1,2,72,896]{3,2,1,0:T(8,128)(2,1)S(1)}, u32[]{:S(2)}, u32[]{:S(2)}) collective-permute-start(bf16[1,2,72,896]{3,2,1,0:T(8,128)(2,1)S(1)} %collective-permute-done.7.refs_1_.refs_0_), channel_id=1, source_target_pairs={{0,4},{4,0},{1,5},{5,1},{2,6},{6,2},{3,7},{7,3},{8,12},{12,8},{9,1... | collective-permute-start | bytes 774152 | tf_op jit(solution)/shard_map/ppermute | solution.py:189
  18.9 13.1 %collective-permute-start.14 = (bf16[1,2,72,896]{3,2,1,0:T(8,128)(2,1)S(1)}, bf16[1,2,72,896]{3,2,1,0:T(8,128)(2,1)S(1)}, u32[]{:S(2)}, u32[]{:S(2)}) collective-permute-start(bf16[1,2,72,896]{3,2,1,0:T(8,128)(2,1)S(1)} %collective-permute-done.13.refs_0_.refs_5_), channel_id=1, source_target_pairs={{0,4},{4,0},{1,5},{5,1},{2,6},{6,2},{3,7},{7,3},{8,12},{12,8},{9,1... | collective-permute-start | bytes 774152 | tf_op jit(solution)/shard_map/ppermute | solution.py:189
  19.5 13.3 %collective-permute-start.12 = (bf16[72,1536]{1,0:T(8,128)(2,1)S(1)}, bf16[72,1536]{1,0:T(8,128)(2,1)S(1)}, u32[]{:S(2)}, u32[]{:S(2)}) collective-permute-start(bf16[72,1536]{1,0:T(8,128)(2,1)S(1)} %shard_map.114.s_ref), channel_id=1, source_target_pairs={{1,2},{2,1},{5,6},{6,5},{9,10},{10,9},{13,14},{14,13},{17,18},{18,... | collective-permute-start | bytes 663560 | tf_op jit(solution)/shard_map/ppermute | solution.py:237
  21.9 14.0 %collective-permute-start.4 = (bf16[1,2,72,896]{3,2,1,0:T(8,128)(2,1)S(1)}, bf16[1,2,72,896]{3,2,1,0:T(8,128)(2,1)S(1)}, u32[]{:S(2)}, u32[]{:S(2)}) collective-permute-start(bf16[1,2,72,896]{3,2,1,0:T(8,128)(2,1)S(1)} %collective-permute-done.3.refs_1_.refs_0_), channel_id=1, source_target_pairs={{0,4},{4,0},{1,5},{5,1},{2,6},{6,2},{3,7},{7,3},{8,12},{12,8},{9,1... | collective-permute-start | bytes 774152 | tf_op jit(solution)/shard_map/ppermute | solution.py:189
  23.1 13.6 %collective-permute-start.2 = (bf16[72,1536]{1,0:T(8,128)(2,1)S(1)}, bf16[72,1536]{1,0:T(8,128)(2,1)S(1)}, u32[]{:S(2)}, u32[]{:S(2)}) collective-permute-start(bf16[72,1536]{1,0:T(8,128)(2,1)S(1)} %shard_map.104.s_ref), channel_id=1, source_target_pairs={{1,2},{2,1},{5,6},{6,5},{9,10},{10,9},{13,14},{14,13},{17,18},{18,... | collective-permute-start | bytes 663560 | tf_op jit(solution)/shard_map/ppermute | solution.py:237
  27.3 10.3 %collective-permute-start.18 = (bf16[72,1536]{1,0:T(8,128)(2,1)S(1)}, bf16[72,1536]{1,0:T(8,128)(2,1)S(1)}, u32[]{:S(2)}, u32[]{:S(2)}) collective-permute-start(bf16[72,1536]{1,0:T(8,128)(2,1)S(1)} %shard_map.120.refs_1_), channel_id=1, source_target_pairs={{0,1},{3,2},{4,5},{7,6},{8,9},{11,10},{12,13},{15,14},{16,17},{19,... | collective-permute-start | bytes 663560 | tf_op jit(solution)/shard_map/ppermute | solution.py:225
  32.9 9.3 %collective-permute-start.15 = (bf16[72,1536]{1,0:T(8,128)(2,1)S(1)}, bf16[72,1536]{1,0:T(8,128)(2,1)S(1)}, u32[]{:S(2)}, u32[]{:S(2)}) collective-permute-start(bf16[72,1536]{1,0:T(8,128)(2,1)S(1)} %get-tuple-element.53), channel_id=1, source_target_pairs={{0,1},{3,2},{1,0},{2,3},{4,5},{7,6},{5,4},{6,7},{8,9},{11,10},{9,8... | collective-permute-start | bytes 663560 | tf_op jit(solution)/shard_map/ppermute | solution.py:225
  36.8 8.0 %collective-permute-start.5 = (bf16[72,1536]{1,0:T(8,128)(2,1)S(1)}, bf16[72,1536]{1,0:T(8,128)(2,1)S(1)}, u32[]{:S(2)}, u32[]{:S(2)}) collective-permute-start(bf16[72,1536]{1,0:T(8,128)(2,1)S(1)} %get-tuple-element.43), channel_id=1, source_target_pairs={{0,1},{3,2},{1,0},{2,3},{4,5},{7,6},{5,4},{6,7},{8,9},{11,10},{9,8... | collective-permute-start | bytes 663560 | tf_op jit(solution)/shard_map/ppermute | solution.py:225
  37.6 8.7 %collective-permute-start.19 = (bf16[72,1536]{1,0:T(8,128)(2,1)S(1)}, bf16[72,1536]{1,0:T(8,128)(2,1)S(1)}, u32[]{:S(2)}, u32[]{:S(2)}) collective-permute-start(bf16[72,1536]{1,0:T(8,128)(2,1)S(1)} %shard_map.121.s_ref), channel_id=1, source_target_pairs={{1,2},{2,1},{5,6},{6,5},{9,10},{10,9},{13,14},{14,13},{17,18},{18,... | collective-permute-start | bytes 663560 | tf_op jit(solution)/shard_map/ppermute | solution.py:237
  42.3 9.4 %collective-permute-start.25 = (bf16[72,1536]{1,0:T(8,128)(2,1)S(1)}, bf16[72,1536]{1,0:T(8,128)(2,1)S(1)}, u32[]{:S(2)}, u32[]{:S(2)}) collective-permute-start(bf16[72,1536]{1,0:T(8,128)(2,1)S(1)} %get-tuple-element.64.s_ref), channel_id=1, source_target_pairs={{1,2},{2,1},{5,6},{6,5},{9,10},{10,9},{13,14},{14,13},{17,18},{18,... | collective-permute-start | bytes 663560 | tf_op jit(solution)/shard_map/ppermute | solution.py:237
  44.8 9.8 %collective-permute-start.6 = (bf16[72,1536]{1,0:T(8,128)(2,1)S(1)}, bf16[72,1536]{1,0:T(8,128)(2,1)S(1)}, u32[]{:S(2)}, u32[]{:S(2)}) collective-permute-start(bf16[72,1536]{1,0:T(8,128)(2,1)S(1)} %get-tuple-element.45.s_ref), channel_id=1, source_target_pairs={{1,2},{2,1},{5,6},{6,5},{9,10},{10,9},{13,14},{14,13},{17,18},{18,... | collective-permute-start | bytes 663560 | tf_op jit(solution)/shard_map/ppermute | solution.py:237
  46.4 11.0 %collective-permute-start.20 = (bf16[72,1536]{1,0:T(8,128)(2,1)S(1)}, bf16[72,1536]{1,0:T(8,128)(2,1)S(1)}, u32[]{:S(2)}, u32[]{:S(2)}) collective-permute-start(bf16[72,1536]{1,0:T(8,128)(2,1)S(1)} %get-tuple-element.60), channel_id=1, source_target_pairs={{0,1},{3,2},{1,0},{2,3},{4,5},{7,6},{5,4},{6,7},{8,9},{11,10},{9,8... | collective-permute-start | bytes 663560 | tf_op jit(solution)/shard_map/ppermute | solution.py:225
  51.9 9.1 %collective-permute-start.26 = (bf16[72,1536]{1,0:T(8,128)(2,1)S(1)}, bf16[72,1536]{1,0:T(8,128)(2,1)S(1)}, u32[]{:S(2)}, u32[]{:S(2)}) collective-permute-start(bf16[72,1536]{1,0:T(8,128)(2,1)S(1)} %get-tuple-element.66), channel_id=1, source_target_pairs={{0,1},{3,2},{1,0},{2,3},{4,5},{7,6},{5,4},{6,7},{8,9},{11,10},{9,8... | collective-permute-start | bytes 663560 | tf_op jit(solution)/shard_map/ppermute | solution.py:225
  54.8 8.6 %collective-permute-start.8 = (bf16[72,1536]{1,0:T(8,128)(2,1)S(1)}, bf16[72,1536]{1,0:T(8,128)(2,1)S(1)}, u32[]{:S(2)}, u32[]{:S(2)}) collective-permute-start(bf16[72,1536]{1,0:T(8,128)(2,1)S(1)} %get-tuple-element.48), channel_id=1, source_target_pairs={{0,1},{3,2},{1,0},{2,3},{4,5},{7,6},{5,4},{6,7},{8,9},{11,10},{9,8... | collective-permute-start | bytes 663560 | tf_op jit(solution)/shard_map/ppermute | solution.py:225
  57.5 6.6 %collective-permute-start.23 = (bf16[72,1536]{1,0:T(8,128)(2,1)S(1)}, bf16[72,1536]{1,0:T(8,128)(2,1)S(1)}, u32[]{:S(2)}, u32[]{:S(2)}) collective-permute-start(bf16[72,1536]{1,0:T(8,128)(2,1)S(1)} %get-tuple-element.63.s_ref), channel_id=1, source_target_pairs={{1,2},{2,1},{5,6},{6,5},{9,10},{10,9},{13,14},{14,13},{17,18},{18,... | collective-permute-start | bytes 663560 | tf_op jit(solution)/shard_map/ppermute | solution.py:237
  61.0 6.0 %collective-permute-start.29 = (bf16[72,1536]{1,0:T(8,128)(2,1)S(1)}, bf16[72,1536]{1,0:T(8,128)(2,1)S(1)}, u32[]{:S(2)}, u32[]{:S(2)}) collective-permute-start(bf16[72,1536]{1,0:T(8,128)(2,1)S(1)} %get-tuple-element.69.s_ref), channel_id=1, source_target_pairs={{1,2},{2,1},{5,6},{6,5},{9,10},{10,9},{13,14},{14,13},{17,18},{18,... | collective-permute-start | bytes 663560 | tf_op jit(solution)/shard_map/ppermute | solution.py:237
  63.4 7.7 %collective-permute-start.9 = (bf16[72,1536]{1,0:T(8,128)(2,1)S(1)}, bf16[72,1536]{1,0:T(8,128)(2,1)S(1)}, u32[]{:S(2)}, u32[]{:S(2)}) collective-permute-start(bf16[72,1536]{1,0:T(8,128)(2,1)S(1)} %get-tuple-element.50.s_ref), channel_id=1, source_target_pairs={{1,2},{2,1},{5,6},{6,5},{9,10},{10,9},{13,14},{14,13},{17,18},{18,... | collective-permute-start | bytes 663560 | tf_op jit(solution)/shard_map/ppermute | solution.py:237
  64.2 10.7 %collective-permute-start.24 = (bf16[72,1536]{1,0:T(8,128)(2,1)S(1)}, bf16[72,1536]{1,0:T(8,128)(2,1)S(1)}, u32[]{:S(2)}, u32[]{:S(2)}) collective-permute-start(bf16[72,1536]{1,0:T(8,128)(2,1)S(1)} %shard_map.127.refs_1_), channel_id=1, source_target_pairs={{1,0},{2,3},{5,4},{6,7},{9,8},{10,11},{13,12},{14,15},{17,16},{18,... | collective-permute-start | bytes 663560 | tf_op jit(solution)/shard_map/ppermute | solution.py:225
  66.2 6.4 %collective-permute-start.21 = (bf16[72,896]{1,0:T(8,128)(2,1)S(1)}, bf16[72,896]{1,0:T(8,128)(2,1)S(1)}, u32[]{:S(2)}, u32[]{:S(2)}) collective-permute-start(bf16[72,896]{1,0:T(8,128)(2,1)S(1)} %shard_map.125), channel_id=1, source_target_pairs={{0,4},{4,0},{1,5},{5,1},{2,6},{6,2},{3,7},{7,3},{8,12},{12,8},{9,1... | collective-permute-start | bytes 387080 | tf_op jit(solution)/shard_map/ppermute | solution.py:189
  67.2 12.1 %collective-permute-start.30 = (bf16[72,1536]{1,0:T(8,128)(2,1)S(1)}, bf16[72,1536]{1,0:T(8,128)(2,1)S(1)}, u32[]{:S(2)}, u32[]{:S(2)}) collective-permute-start(bf16[72,1536]{1,0:T(8,128)(2,1)S(1)} %shard_map.134.refs_1_), channel_id=1, source_target_pairs={{1,0},{2,3},{5,4},{6,7},{9,8},{10,11},{13,12},{14,15},{17,16},{18,... | collective-permute-start | bytes 663560 | tf_op jit(solution)/shard_map/ppermute | solution.py:225
  69.1 7.9 %collective-permute-start.27 = (bf16[72,896]{1,0:T(8,128)(2,1)S(1)}, bf16[72,896]{1,0:T(8,128)(2,1)S(1)}, u32[]{:S(2)}, u32[]{:S(2)}) collective-permute-start(bf16[72,896]{1,0:T(8,128)(2,1)S(1)} %shard_map.132), channel_id=1, source_target_pairs={{0,4},{4,0},{1,5},{5,1},{2,6},{6,2},{3,7},{7,3},{8,12},{12,8},{9,1... | collective-permute-start | bytes 387080 | tf_op jit(solution)/shard_map/ppermute | solution.py:189
  71.1 9.9 %collective-permute-start.31 = (bf16[72,896]{1,0:T(8,128)(2,1)S(1)}, bf16[72,896]{1,0:T(8,128)(2,1)S(1)}, u32[]{:S(2)}, u32[]{:S(2)}) collective-permute-start(bf16[72,896]{1,0:T(8,128)(2,1)S(1)} %shard_map.137), channel_id=1, source_target_pairs={{0,4},{4,0},{1,5},{5,1},{2,6},{6,2},{3,7},{7,3},{8,12},{12,8},{9,1... | collective-permute-start | bytes 387080 | tf_op jit(solution)/shard_map/ppermute | solution.py:189
  72.6 10.3 %collective-permute-start.10 = (bf16[72,1536]{1,0:T(8,128)(2,1)S(1)}, bf16[72,1536]{1,0:T(8,128)(2,1)S(1)}, u32[]{:S(2)}, u32[]{:S(2)}) collective-permute-start(bf16[72,1536]{1,0:T(8,128)(2,1)S(1)} %shard_map.111.refs_1_), channel_id=1, source_target_pairs={{1,0},{2,3},{5,4},{6,7},{9,8},{10,11},{13,12},{14,15},{17,16},{18,... | collective-permute-start | bytes 663560 | tf_op jit(solution)/shard_map/ppermute | solution.py:225
  74.9 8.7 %collective-permute-start.16 = (bf16[72,896]{1,0:T(8,128)(2,1)S(1)}, bf16[72,896]{1,0:T(8,128)(2,1)S(1)}, u32[]{:S(2)}, u32[]{:S(2)}) collective-permute-start(bf16[72,896]{1,0:T(8,128)(2,1)S(1)} %get-tuple-element.57), channel_id=1, source_target_pairs={{0,4},{4,0},{1,5},{5,1},{2,6},{6,2},{3,7},{7,3},{8,12},{12,8},{9,1... | collective-permute-start | bytes 387080 | tf_op jit(solution)/shard_map/ppermute | solution.py:189
  77.1 8.6 %collective-permute-start.22 = (bf16[72,896]{1,0:T(8,128)(2,1)S(1)}, bf16[72,896]{1,0:T(8,128)(2,1)S(1)}, u32[]{:S(2)}, u32[]{:S(2)}) collective-permute-start(bf16[72,896]{1,0:T(8,128)(2,1)S(1)} %shard_map.126), channel_id=1, source_target_pairs={{0,8},{8,0},{16,24},{24,16},{1,9},{9,1},{17,25},{25,17},{2,10},{10... | collective-permute-start | bytes 387080 | tf_op jit(solution)/shard_map/ppermute | solution.py:189
  79.2 6.5 %collective-permute-start.28 = (bf16[72,896]{1,0:T(8,128)(2,1)S(1)}, bf16[72,896]{1,0:T(8,128)(2,1)S(1)}, u32[]{:S(2)}, u32[]{:S(2)}) collective-permute-start(bf16[72,896]{1,0:T(8,128)(2,1)S(1)} %shard_map.133), channel_id=1, source_target_pairs={{0,16},{8,24},{16,0},{24,8},{1,17},{9,25},{17,1},{25,9},{2,18},{10... | collective-permute-start | bytes 387080 | tf_op jit(solution)/shard_map/ppermute | solution.py:189
  81.1 5.8 %collective-permute-start.32 = (bf16[72,896]{1,0:T(8,128)(2,1)S(1)}, bf16[72,896]{1,0:T(8,128)(2,1)S(1)}, u32[]{:S(2)}, u32[]{:S(2)}) collective-permute-start(bf16[72,896]{1,0:T(8,128)(2,1)S(1)} %shard_map.138), channel_id=1, source_target_pairs={{0,24},{8,16},{16,8},{24,0},{1,25},{9,17},{17,9},{25,1},{2,26},{10... | collective-permute-start | bytes 387080 | tf_op jit(solution)/shard_map/ppermute | solution.py:189
  83.6 3.3 %copy-start.3 = (f32[192]{0:T(256)S(1)}, f32[192]{0:T(256)}, u32[]{:S(2)}) copy-start(f32[192]{0:T(256)} %param.9) | copy-start | bytes 2308

commit v5 on v4

--- a/solution.py
+++ b/solution.py
@@ -46,32 +46,27 @@
     return jnp.sum(jnp.where(eye, row, jnp.zeros_like(row)), axis=1, keepdims=True)
 
 
-def ranks(ids):
-    count = ids.shape[0]
-    lanes = lax.broadcasted_iota(jnp.int32, (count, 128), 1)
-    onehot = jnp.where(ids == lanes, 1.0, 0.0)
-    lower = jnp.where(
-        lax.broadcasted_iota(jnp.int32, (count, count), 0) > lax.broadcasted_iota(jnp.int32, (count, count), 1), 1.0, 0.0
-    )
-    before = mm(lower.astype(BF16), onehot.astype(BF16), NN)
-    return jnp.sum(before * onehot, axis=1, keepdims=True).astype(jnp.int32)
-
-
-def slots(ids, rank, owner, cap):
-    places = lax.broadcasted_iota(jnp.int32, (ids.shape[0], cap), 1)
-    return jnp.where((ids == owner) & (rank == places), 1.0, 0.0).astype(BF16)
+def ranks(ids, n_expert):
+    count = ids.shape[1]
+    onehot = jnp.where(lax.broadcasted_iota(jnp.int32, (max(n_expert, 16), count), 0) == ids, 1.0, 0.0)
+    upper = jnp.where(
+        lax.broadcasted_iota(jnp.int32, (count, count), 0) < lax.broadcasted_iota(jnp.int32, (count, count), 1), 1.0, 0.0
+    )
+    before = mm(onehot.astype(BF16), upper.astype(BF16), NN)
+    return jnp.sum(before * onehot, axis=0, keepdims=True).astype(jnp.int32)
 
 
 def send_body(n_expert, cap, ids_ref, rw_ref, tokens_ref, cot_ref, *outs):
-    ids = column(ids_ref[...])
-    rank = ranks(ids)
-    tokens = tokens_ref[...]
-    scaled = (column(rw_ref[...]) * cot_ref[...].astype(F32)).astype(BF16)
+    ids, rw = ids_ref[...], rw_ref[...]
+    rank = ranks(ids, n_expert)
+    places = lax.broadcasted_iota(jnp.int32, (cap, ids.shape[1]), 0)
     for k in range(n_expert):
-        pick = slots(ids, rank, lax.axis_index("expert") ^ k, cap)
+        here = (ids == lax.axis_index("expert") ^ k) & (rank == places)
+        pick = jnp.where(here, 1.0, 0.0).astype(BF16)
+        weight = jnp.sum(jnp.where(here, rw, 0.0), axis=1, keepdims=True)
         outs[n_expert][k] = pick
-        outs[k][0, 0] = mm(pick, tokens, TN).astype(BF16)
-        outs[k][0, 1] = mm(pick, scaled, TN).astype(BF16)
+        outs[k][0, 0] = mm(pick, tokens_ref[...], NN).astype(BF16)
+        outs[k][0, 1] = (weight * mm(pick, cot_ref[...], NN)).astype(BF16)
 
 
 def side(refs, which):
@@ -166,7 +161,7 @@
 def final_body(n_expert, rw_ref, pick_ref, *refs):
     total = None
     for k in range(n_expert):
-        term = mm(pick_ref[k], refs[k][...], NN)
+        term = mm(pick_ref[k], refs[k][...], TN)
         total = term if total is None else total + term
     refs[n_expert][...] = (column(rw_ref[...]) * total).astype(BF16)
 
@@ -189,7 +184,7 @@
         return lax.ppermute(x, axis, [(i, i ^ k) for i in range(lax.axis_size(axis))])
 
     send = call(
-        functools.partial(send_body, n_expert, cap), [keep(1, 2, cap, quarter)] * n_expert + [keep(n_expert, count, cap)],
+        functools.partial(send_body, n_expert, cap), [keep(1, 2, cap, quarter)] * n_expert + [keep(n_expert, cap, count)],
         (ids, rw, tokens, cotangent), (0, 1, 2, 3),
     )
     got = [send[0]] + [swap(send[k], "expert", k) for k in range(1, n_expert)]

time: 88.6 us -> 88.4 us (level)
  no operation moved by 1% of the time
where the time goes in v5:
time: 88.4 us; the launch traced here: 88 us
  starting transfers between devices  43.7 us (49%)
  waiting for transfers between devices  23.4 us (26%)
  Pallas kernels  19.7 us (22%)
  between operations  1.16 us (1%)
    ppermute x11, starting transfers between devices, steps(): came = lax.ppermute(leaving[i], 'seq', pairs)  25.1 us
    pallas_call x40, Pallas kernels, call(): pl.pallas_call(body, out_shape=outs, in_specs=[pl.BlockSpec(memory_space=...  19.7 us
    ppermute x11, waiting for transfers between devices, steps(): came = lax.ppermute(leaving[i], 'seq', pairs)  14 us
    ppermute x14, starting transfers between devices, swap(): lax.ppermute(x, axis, [(i, i ^ k) for i in range(lax.axis_size(axis))])  13.1 us
    ppermute x14, waiting for transfers between devices, swap(): lax.ppermute(x, axis, [(i, i ^ k) for i in range(lax.axis_size(axis))])  9.42 us
    ppermute x8, starting transfers between devices, steps(): lax.ppermute(done[0], 'seq', middle)  5.4 us
  transfers between devices with their start and end apart: 33, of which 15 were waited for; matrix products, arithmetic and copies ran while one was open for 0% of the time, Pallas kernels for 19%

profile of v5, /device:TPU:0, one launch (start us, length us, event | category | flops | bytes accessed | tf_op | source)
XLA Modules:
  0.0 88.0 jit_solution(14766525432636587049)
XLA Ops:
  0.7 2.1 %shard_map.102 = (bf16[1,2,72,896]{3,2,1,0:T(8,128)(2,1)S(1)}, bf16[1,2,72,896]{3,2,1,0:T(8,128)(2,1)S(1)}, bf16[1,2,72,896]{3,2,1,0:T(8,128)(2,1)S(1)}, bf16[1,...) custom-call(s32[1,192]{1,0:T(1,128)} %bitcast.39, f32[1,192]{1,0:T(1,128)} %bitcast.37, bf16[192,896]{1,0:T(8,128)(2,1)} %tokens_ref.1, ...), custom_call_target="tpu_custom_call" | custom-call | tf_op jit(solution)/shard_map/pallas_call | solution.py:34
  3.3 2.6 %collective-permute-start = (bf16[1,2,72,896]{3,2,1,0:T(8,128)(2,1)S(1)}, bf16[1,2,72,896]{3,2,1,0:T(8,128)(2,1)S(1)}, u32[]{:S(2)}, u32[]{:S(2)}) collective-permute-start(bf16[1,2,72,896]{3,2,1,0:T(8,128)(2,1)S(1)} %get-tuple-element.41.refs_0_.refs_1_), channel_id=1, source_target_pairs={{0,4},{4,0},{1,5},{5,1},{2,6},{6,2},{3,7},{7,3},{8,12},{12,8},{9,1... | collective-permute-start | bytes 774152 | tf_op jit(solution)/shard_map/ppermute | solution.py:184
  5.9 1.5 %collective-permute-start.13 = (bf16[1,2,72,896]{3,2,1,0:T(8,128)(2,1)S(1)}, bf16[1,2,72,896]{3,2,1,0:T(8,128)(2,1)S(1)}, u32[]{:S(2)}, u32[]{:S(2)}) collective-permute-start(bf16[1,2,72,896]{3,2,1,0:T(8,128)(2,1)S(1)} %get-tuple-element.52), channel_id=1, source_target_pairs={{0,16},{8,24},{16,0},{24,8},{1,17},{9,25},{17,1},{25,9},{2,18},{10... | collective-permute-start | bytes 774152 | tf_op jit(solution)/shard_map/ppermute | solution.py:184
  7.4 2.5 %shard_map.108 = (bf16[72,1536]{1,0:T(8,128)(2,1)S(1)}, bf16[72,1536]{1,0:T(8,128)(2,1)S(1)}) custom-call(bf16[1,2,72,896]{3,2,1,0:T(8,128)(2,1)S(1)} %get-tuple-element.41.refs_0_.refs_1_, bf16[1,2,72,896]{3,2,1,0:T(8,128)(2,1)S(1)} %collective-permute-done.7.refs_1_.refs_0_, bf16[896,512]{1,0:T(8,128)(2,1)} %bitcast.5, bf16[896,512]{1,0:T(8,128)(2,1)} %bitcast.18, ...), custom_call_target="tpu_custom_call" | custom-call | tf_op jit(solution)/shard_map/pallas_call | solution.py:34
  9.9 3.5 %collective-permute-start.11 = (bf16[72,1536]{1,0:T(8,128)(2,1)S(1)}, bf16[72,1536]{1,0:T(8,128)(2,1)S(1)}, u32[]{:S(2)}, u32[]{:S(2)}) collective-permute-start(bf16[72,1536]{1,0:T(8,128)(2,1)S(1)} %get-tuple-element.51.refs_1_), channel_id=1, source_target_pairs={{0,1},{3,2},{4,5},{7,6},{8,9},{11,10},{12,13},{15,14},{16,17},{19,... | collective-permute-start | bytes 663560 | tf_op jit(solution)/shard_map/ppermute | solution.py:220
  13.5 0.7 shard_map.103.refs_1_
  14.3 2.9 %collective-permute-start.1 = (bf16[72,1536]{1,0:T(8,128)(2,1)S(1)}, bf16[72,1536]{1,0:T(8,128)(2,1)S(1)}, u32[]{:S(2)}, u32[]{:S(2)}) collective-permute-start(bf16[72,1536]{1,0:T(8,128)(2,1)S(1)} %shard_map.103.refs_1_), channel_id=1, source_target_pairs={{0,1},{3,2},{4,5},{7,6},{8,9},{11,10},{12,13},{15,14},{16,17},{19,... | collective-permute-start | bytes 663560 | tf_op jit(solution)/shard_map/ppermute | solution.py:220
  17.2 1.6 %collective-permute-start.17 = (bf16[1,2,72,896]{3,2,1,0:T(8,128)(2,1)S(1)}, bf16[1,2,72,896]{3,2,1,0:T(8,128)(2,1)S(1)}, u32[]{:S(2)}, u32[]{:S(2)}) collective-permute-start(bf16[1,2,72,896]{3,2,1,0:T(8,128)(2,1)S(1)} %collective-permute-done.7.refs_1_.refs_0_), channel_id=1, source_target_pairs={{0,4},{4,0},{1,5},{5,1},{2,6},{6,2},{3,7},{7,3},{8,12},{12,8},{9,1... | collective-permute-start | bytes 774152 | tf_op jit(solution)/shard_map/ppermute | solution.py:184
  19.3 0.7 collective-permute-start.12
  20.0 1.7 %collective-permute-done.3.refs_1_.refs_0_ = bf16[1,2,72,896]{3,2,1,0:T(8,128)(2,1)S(1)} collective-permute-done((bf16[1,2,72,896]{3,2,1,0:T(8,128)(2,1)S(1)}, bf16[1,2,72,896]{3,2,1,0:T(8,128)(2,1)S(1)}, u32[]{:S(2)}, u32[]{:S(2)}) %collective-permute-start.3) | collective-permute-done | bytes 258080 | tf_op jit(solution)/shard_map/ppermute | solution.py:184
  22.9 0.7 collective-permute-start.2
  23.6 2.8 %collective-permute-done.17.refs_0_.refs_2_ = bf16[1,2,72,896]{3,2,1,0:T(8,128)(2,1)S(1)} collective-permute-done((bf16[1,2,72,896]{3,2,1,0:T(8,128)(2,1)S(1)}, bf16[1,2,72,896]{3,2,1,0:T(8,128)(2,1)S(1)}, u32[]{:S(2)}, u32[]{:S(2)}) %collective-permute-start.17) | collective-permute-done | bytes 258080 | tf_op jit(solution)/shard_map/ppermute | solution.py:184
  26.3 0.7 shard_map.120.refs_1_
  27.1 4.5 %collective-permute-start.18 = (bf16[72,1536]{1,0:T(8,128)(2,1)S(1)}, bf16[72,1536]{1,0:T(8,128)(2,1)S(1)}, u32[]{:S(2)}, u32[]{:S(2)}) collective-permute-start(bf16[72,1536]{1,0:T(8,128)(2,1)S(1)} %shard_map.120.refs_1_), channel_id=1, source_target_pairs={{0,1},{3,2},{4,5},{7,6},{8,9},{11,10},{12,13},{15,14},{16,17},{19,... | collective-permute-start | bytes 663560 | tf_op jit(solution)/shard_map/ppermute | solution.py:220
  31.9 0.7 shard_map.115.refs_0_.refs_1_
  32.8 2.9 %collective-permute-done.4.refs_0_.refs_4_ = bf16[1,2,72,896]{3,2,1,0:T(8,128)(2,1)S(1)} collective-permute-done((bf16[1,2,72,896]{3,2,1,0:T(8,128)(2,1)S(1)}, bf16[1,2,72,896]{3,2,1,0:T(8,128)(2,1)S(1)}, u32[]{:S(2)}, u32[]{:S(2)}) %collective-permute-start.4) | collective-permute-done | bytes 258080 | tf_op jit(solution)/shard_map/ppermute | solution.py:184
  35.7 0.7 shard_map.105.refs_0_.refs_1_
  37.4 0.7 collective-permute-start.19
  38.1 4.0 %collective-permute-done.15.refs_0_ = bf16[72,1536]{1,0:T(8,128)(2,1)S(1)} collective-permute-done((bf16[72,1536]{1,0:T(8,128)(2,1)S(1)}, bf16[72,1536]{1,0:T(8,128)(2,1)S(1)}, u32[]{:S(2)}, u32[]{:S(2)}) %collective-permute-start.15) | collective-permute-done | bytes 221216 | tf_op jit(solution)/shard_map/ppermute | solution.py:220
  42.1 0.7 collective-permute-start.25
  42.8 1.7 %collective-permute-done.5.refs_0_ = bf16[72,1536]{1,0:T(8,128)(2,1)S(1)} collective-permute-done((bf16[72,1536]{1,0:T(8,128)(2,1)S(1)}, bf16[72,1536]{1,0:T(8,128)(2,1)S(1)}, u32[]{:S(2)}, u32[]{:S(2)}) %collective-permute-start.5) | collective-permute-done | bytes 221216 | tf_op jit(solution)/shard_map/ppermute | solution.py:220
  44.6 0.7 collective-permute-start.6
  45.3 0.8 shard_map.122
  46.3 5.3 %collective-permute-start.20 = (bf16[72,1536]{1,0:T(8,128)(2,1)S(1)}, bf16[72,1536]{1,0:T(8,128)(2,1)S(1)}, u32[]{:S(2)}, u32[]{:S(2)}) collective-permute-start(bf16[72,1536]{1,0:T(8,128)(2,1)S(1)} %get-tuple-element.60), channel_id=1, source_target_pairs={{0,1},{3,2},{1,0},{2,3},{4,5},{7,6},{5,4},{6,7},{8,9},{11,10},{9,8... | collective-permute-start | bytes 663560 | tf_op jit(solution)/shard_map/ppermute | solution.py:220
  51.7 2.7 %collective-permute-start.26 = (bf16[72,1536]{1,0:T(8,128)(2,1)S(1)}, bf16[72,1536]{1,0:T(8,128)(2,1)S(1)}, u32[]{:S(2)}, u32[]{:S(2)}) collective-permute-start(bf16[72,1536]{1,0:T(8,128)(2,1)S(1)} %get-tuple-element.66), channel_id=1, source_target_pairs={{0,1},{3,2},{1,0},{2,3},{4,5},{7,6},{5,4},{6,7},{8,9},{11,10},{9,8... | collective-permute-start | bytes 663560 | tf_op jit(solution)/shard_map/ppermute | solution.py:220
  54.6 2.2 %collective-permute-start.8 = (bf16[72,1536]{1,0:T(8,128)(2,1)S(1)}, bf16[72,1536]{1,0:T(8,128)(2,1)S(1)}, u32[]{:S(2)}, u32[]{:S(2)}) collective-permute-start(bf16[72,1536]{1,0:T(8,128)(2,1)S(1)} %get-tuple-element.48), channel_id=1, source_target_pairs={{0,1},{3,2},{1,0},{2,3},{4,5},{7,6},{5,4},{6,7},{8,9},{11,10},{9,8... | collective-permute-start | bytes 663560 | tf_op jit(solution)/shard_map/ppermute | solution.py:220
  57.3 0.7 collective-permute-start.23
  58.0 2.8 %collective-permute-done.26.refs_0_ = bf16[72,1536]{1,0:T(8,128)(2,1)S(1)} collective-permute-done((bf16[72,1536]{1,0:T(8,128)(2,1)S(1)}, bf16[72,1536]{1,0:T(8,128)(2,1)S(1)}, u32[]{:S(2)}, u32[]{:S(2)}) %collective-permute-start.26) | collective-permute-done | bytes 221216 | tf_op jit(solution)/shard_map/ppermute | solution.py:220
  60.8 0.7 collective-permute-start.29
  61.5 1.6 %collective-permute-done.8.refs_0_ = bf16[72,1536]{1,0:T(8,128)(2,1)S(1)} collective-permute-done((bf16[72,1536]{1,0:T(8,128)(2,1)S(1)}, bf16[72,1536]{1,0:T(8,128)(2,1)S(1)}, u32[]{:S(2)}, u32[]{:S(2)}) %collective-permute-start.8) | collective-permute-done | bytes 221216 | tf_op jit(solution)/shard_map/ppermute | solution.py:220
  63.2 0.7 collective-permute-start.9
  64.0 1.3 %collective-permute-start.24 = (bf16[72,1536]{1,0:T(8,128)(2,1)S(1)}, bf16[72,1536]{1,0:T(8,128)(2,1)S(1)}, u32[]{:S(2)}, u32[]{:S(2)}) collective-permute-start(bf16[72,1536]{1,0:T(8,128)(2,1)S(1)} %shard_map.127.refs_1_), channel_id=1, source_target_pairs={{1,0},{2,3},{5,4},{6,7},{9,8},{10,11},{13,12},{14,15},{17,16},{18,... | collective-permute-start | bytes 663560 | tf_op jit(solution)/shard_map/ppermute | solution.py:220
  65.3 0.7 shard_map.125
  66.0 0.9 collective-permute-start.21
  67.0 1.3 %collective-permute-start.30 = (bf16[72,1536]{1,0:T(8,128)(2,1)S(1)}, bf16[72,1536]{1,0:T(8,128)(2,1)S(1)}, u32[]{:S(2)}, u32[]{:S(2)}) collective-permute-start(bf16[72,1536]{1,0:T(8,128)(2,1)S(1)} %shard_map.134.refs_1_), channel_id=1, source_target_pairs={{1,0},{2,3},{5,4},{6,7},{9,8},{10,11},{13,12},{14,15},{17,16},{18,... | collective-permute-start | bytes 663560 | tf_op jit(solution)/shard_map/ppermute | solution.py:220
  68.3 0.7 shard_map.132
  69.0 1.3 %collective-permute-start.27 = (bf16[72,896]{1,0:T(8,128)(2,1)S(1)}, bf16[72,896]{1,0:T(8,128)(2,1)S(1)}, u32[]{:S(2)}, u32[]{:S(2)}) collective-permute-start(bf16[72,896]{1,0:T(8,128)(2,1)S(1)} %shard_map.132), channel_id=1, source_target_pairs={{0,4},{4,0},{1,5},{5,1},{2,6},{6,2},{3,7},{7,3},{8,12},{12,8},{9,1... | collective-permute-start | bytes 387080 | tf_op jit(solution)/shard_map/ppermute | solution.py:184
  70.9 0.9 collective-permute-start.31
  72.4 1.3 %collective-permute-start.10 = (bf16[72,1536]{1,0:T(8,128)(2,1)S(1)}, bf16[72,1536]{1,0:T(8,128)(2,1)S(1)}, u32[]{:S(2)}, u32[]{:S(2)}) collective-permute-start(bf16[72,1536]{1,0:T(8,128)(2,1)S(1)} %shard_map.111.refs_1_), channel_id=1, source_target_pairs={{1,0},{2,3},{5,4},{6,7},{9,8},{10,11},{13,12},{14,15},{17,16},{18,... | collective-permute-start | bytes 663560 | tf_op jit(solution)/shard_map/ppermute | solution.py:220
  73.7 0.7 shard_map.118
  74.7 1.5 %collective-permute-start.16 = (bf16[72,896]{1,0:T(8,128)(2,1)S(1)}, bf16[72,896]{1,0:T(8,128)(2,1)S(1)}, u32[]{:S(2)}, u32[]{:S(2)}) collective-permute-start(bf16[72,896]{1,0:T(8,128)(2,1)S(1)} %get-tuple-element.57), channel_id=1, source_target_pairs={{0,4},{4,0},{1,5},{5,1},{2,6},{6,2},{3,7},{7,3},{8,12},{12,8},{9,1... | collective-permute-start | bytes 387080 | tf_op jit(solution)/shard_map/ppermute | solution.py:184
  76.2 0.7 shard_map.129.refs_0_
  77.0 2.0 %collective-permute-done.30.refs_0_ = bf16[72,1536]{1,0:T(8,128)(2,1)S(1)} collective-permute-done((bf16[72,1536]{1,0:T(8,128)(2,1)S(1)}, bf16[72,1536]{1,0:T(8,128)(2,1)S(1)}, u32[]{:S(2)}, u32[]{:S(2)}) %collective-permute-start.30) | collective-permute-done | bytes 221216 | tf_op jit(solution)/shard_map/ppermute | solution.py:220
  79.0 1.1 %collective-permute-start.28 = (bf16[72,896]{1,0:T(8,128)(2,1)S(1)}, bf16[72,896]{1,0:T(8,128)(2,1)S(1)}, u32[]{:S(2)}, u32[]{:S(2)}) collective-permute-start(bf16[72,896]{1,0:T(8,128)(2,1)S(1)} %shard_map.133), channel_id=1, source_target_pairs={{0,16},{8,24},{16,0},{24,8},{1,17},{9,25},{17,1},{25,9},{2,18},{10... | collective-permute-start | bytes 387080 | tf_op jit(solution)/shard_map/ppermute | solution.py:184
  81.0 1.7 %shard_map.140 = (f32[896,1024]{1,0:T(8,128)S(1)}, f32[512,896]{1,0:T(8,128)S(1)}) custom-call(bf16[1,2,72,896]{3,2,1,0:T(8,128)(2,1)S(1)} %collective-permute-done.7.refs_1_.refs_0_, bf16[1,2,72,896]{3,2,1,0:T(8,128)(2,1)S(1)} %collective-permute-done.refs_0_.refs_1_, bf16[1,2,72,896]{3,2,1,0:T(8,128)(2,1)S(1)} %collective-permute-done.17.refs_0_.refs_2_, ...), custom_call_target="tpu_custom_call" | custom-call | tf_op jit(solution)/shard_map/pallas_call | solution.py:34
  83.5 2.0 %shard_map.141 = (bf16[1,896,512]{2,1,0:T(8,128)(2,1)}, bf16[1,896,512]{2,1,0:T(8,128)(2,1)}, bf16[1,512,896]{2,1,0:T(8,128)(2,1)}) custom-call(bf16[1,2,72,896]{3,2,1,0:T(8,128)(2,1)S(1)} %collective-permute-done.3.refs_1_.refs_0_, bf16[1,2,72,896]{3,2,1,0:T(8,128)(2,1)S(1)} %get-tuple-element.41.refs_0_.refs_1_, ...), custom_call_target="tpu_custom_call" | custom-call | tf_op jit(solution)/shard_map/pallas_call | solution.py:34
  85.5 1.2 %collective-permute-done.32.refs_3_ = bf16[72,896]{1,0:T(8,128)(2,1)S(1)} collective-permute-done((bf16[72,896]{1,0:T(8,128)(2,1)S(1)}, bf16[72,896]{1,0:T(8,128)(2,1)S(1)}, u32[]{:S(2)}, u32[]{:S(2)}) %collective-permute-start.32) | collective-permute-done | bytes 129056 | tf_op jit(solution)/shard_map/ppermute | solution.py:184
  86.7 1.3 %shard_map.139 = bf16[192,896]{1,0:T(8,128)(2,1)} custom-call(f32[1,192]{1,0:T(1,128)S(1)} %bitcast.38, bf16[4,72,192]{2,1,0:T(8,128)(2,1)S(1)} %get-tuple-element.40.pick_ref, bf16[72,896]{1,0:T(8,128)(2,1)S(1)} %shard_map.119.refs_0_, bf16[72,896]{1,0:T(8,128)(2,1)S(1)} %collective-permute-done.22.refs_1_, ...), custom_call_target="tpu_custom_call" | custom-call | tf_op jit(solution)/shard_map/pallas_call | solution.py:34
  (66 shorter events, 8.3 us)
Async XLA Ops:
  0.6 12.9 %copy-start.2 = (bf16[1,512,896]{2,1,0:T(8,128)(2,1)S(1)}, bf16[1,512,896]{2,1,0:T(8,128)(2,1)}, u32[]{:S(2)}) copy-start(bf16[1,512,896]{2,1,0:T(8,128)(2,1)} %param.13) | copy-start | bytes 2752516
  0.6 12.9 %copy-start.1 = (bf16[1,896,512]{2,1,0:T(8,128)(2,1)S(1)}, bf16[1,896,512]{2,1,0:T(8,128)(2,1)}, u32[]{:S(2)}) copy-start(bf16[1,896,512]{2,1,0:T(8,128)(2,1)} %param.12) | copy-start | bytes 2752516
  0.7 12.9 %copy-start = (bf16[1,896,512]{2,1,0:T(8,128)(2,1)S(1)}, bf16[1,896,512]{2,1,0:T(8,128)(2,1)}, u32[]{:S(2)}) copy-start(bf16[1,896,512]{2,1,0:T(8,128)(2,1)} %param.11) | copy-start | bytes 2752516
  2.8 4.6 %collective-permute-start.7 = (bf16[1,2,72,896]{3,2,1,0:T(8,128)(2,1)S(1)}, bf16[1,2,72,896]{3,2,1,0:T(8,128)(2,1)S(1)}, u32[]{:S(2)}, u32[]{:S(2)}) collective-permute-start(bf16[1,2,72,896]{3,2,1,0:T(8,128)(2,1)S(1)} %get-tuple-element.46), channel_id=1, source_target_pairs={{0,8},{8,0},{16,24},{24,16},{1,9},{9,1},{17,25},{25,17},{2,10},{10... | collective-permute-start | bytes 774152 | tf_op jit(solution)/shard_map/ppermute | solution.py:184
  3.3 10.2 %collective-permute-start = (bf16[1,2,72,896]{3,2,1,0:T(8,128)(2,1)S(1)}, bf16[1,2,72,896]{3,2,1,0:T(8,128)(2,1)S(1)}, u32[]{:S(2)}, u32[]{:S(2)}) collective-permute-start(bf16[1,2,72,896]{3,2,1,0:T(8,128)(2,1)S(1)} %get-tuple-element.41.refs_0_.refs_1_), channel_id=1, source_target_pairs={{0,4},{4,0},{1,5},{5,1},{2,6},{6,2},{3,7},{7,3},{8,12},{12,8},{9,1... | collective-permute-start | bytes 774152 | tf_op jit(solution)/shard_map/ppermute | solution.py:184
  5.9 12.9 %collective-permute-start.13 = (bf16[1,2,72,896]{3,2,1,0:T(8,128)(2,1)S(1)}, bf16[1,2,72,896]{3,2,1,0:T(8,128)(2,1)S(1)}, u32[]{:S(2)}, u32[]{:S(2)}) collective-permute-start(bf16[1,2,72,896]{3,2,1,0:T(8,128)(2,1)S(1)} %get-tuple-element.52), channel_id=1, source_target_pairs={{0,16},{8,24},{16,0},{24,8},{1,17},{9,25},{17,1},{25,9},{2,18},{10... | collective-permute-start | bytes 774152 | tf_op jit(solution)/shard_map/ppermute | solution.py:184
  9.9 9.4 %collective-permute-start.11 = (bf16[72,1536]{1,0:T(8,128)(2,1)S(1)}, bf16[72,1536]{1,0:T(8,128)(2,1)S(1)}, u32[]{:S(2)}, u32[]{:S(2)}) collective-permute-start(bf16[72,1536]{1,0:T(8,128)(2,1)S(1)} %get-tuple-element.51.refs_1_), channel_id=1, source_target_pairs={{0,1},{3,2},{4,5},{7,6},{8,9},{11,10},{12,13},{15,14},{16,17},{19,... | collective-permute-start | bytes 663560 | tf_op jit(solution)/shard_map/ppermute | solution.py:220
  13.4 8.4 %collective-permute-start.3 = (bf16[1,2,72,896]{3,2,1,0:T(8,128)(2,1)S(1)}, bf16[1,2,72,896]{3,2,1,0:T(8,128)(2,1)S(1)}, u32[]{:S(2)}, u32[]{:S(2)}) collective-permute-start(bf16[1,2,72,896]{3,2,1,0:T(8,128)(2,1)S(1)} %get-tuple-element.42), channel_id=1, source_target_pairs={{0,24},{8,16},{16,8},{24,0},{1,25},{9,17},{17,9},{25,1},{2,26},{10... | collective-permute-start | bytes 774152 | tf_op jit(solution)/shard_map/ppermute | solution.py:184
  14.3 8.6 %collective-permute-start.1 = (bf16[72,1536]{1,0:T(8,128)(2,1)S(1)}, bf16[72,1536]{1,0:T(8,128)(2,1)S(1)}, u32[]{:S(2)}, u32[]{:S(2)}) collective-permute-start(bf16[72,1536]{1,0:T(8,128)(2,1)S(1)} %shard_map.103.refs_1_), channel_id=1, source_target_pairs={{0,1},{3,2},{4,5},{7,6},{8,9},{11,10},{12,13},{15,14},{16,17},{19,... | collective-permute-start | bytes 663560 | tf_op jit(solution)/shard_map/ppermute | solution.py:220
  17.2 9.2 %collective-permute-start.17 = (bf16[1,2,72,896]{3,2,1,0:T(8,128)(2,1)S(1)}, bf16[1,2,72,896]{3,2,1,0:T(8,128)(2,1)S(1)}, u32[]{:S(2)}, u32[]{:S(2)}) collective-permute-start(bf16[1,2,72,896]{3,2,1,0:T(8,128)(2,1)S(1)} %collective-permute-done.7.refs_1_.refs_0_), channel_id=1, source_target_pairs={{0,4},{4,0},{1,5},{5,1},{2,6},{6,2},{3,7},{7,3},{8,12},{12,8},{9,1... | collective-permute-start | bytes 774152 | tf_op jit(solution)/shard_map/ppermute | solution.py:184
  18.7 13.1 %collective-permute-start.14 = (bf16[1,2,72,896]{3,2,1,0:T(8,128)(2,1)S(1)}, bf16[1,2,72,896]{3,2,1,0:T(8,128)(2,1)S(1)}, u32[]{:S(2)}, u32[]{:S(2)}) collective-permute-start(bf16[1,2,72,896]{3,2,1,0:T(8,128)(2,1)S(1)} %collective-permute-done.13.refs_0_.refs_5_), channel_id=1, source_target_pairs={{0,4},{4,0},{1,5},{5,1},{2,6},{6,2},{3,7},{7,3},{8,12},{12,8},{9,1... | collective-permute-start | bytes 774152 | tf_op jit(solution)/shard_map/ppermute | solution.py:184
  19.3 13.3 %collective-permute-start.12 = (bf16[72,1536]{1,0:T(8,128)(2,1)S(1)}, bf16[72,1536]{1,0:T(8,128)(2,1)S(1)}, u32[]{:S(2)}, u32[]{:S(2)}) collective-permute-start(bf16[72,1536]{1,0:T(8,128)(2,1)S(1)} %shard_map.114.s_ref), channel_id=1, source_target_pairs={{1,2},{2,1},{5,6},{6,5},{9,10},{10,9},{13,14},{14,13},{17,18},{18,... | collective-permute-start | bytes 663560 | tf_op jit(solution)/shard_map/ppermute | solution.py:232
  21.8 14.0 %collective-permute-start.4 = (bf16[1,2,72,896]{3,2,1,0:T(8,128)(2,1)S(1)}, bf16[1,2,72,896]{3,2,1,0:T(8,128)(2,1)S(1)}, u32[]{:S(2)}, u32[]{:S(2)}) collective-permute-start(bf16[1,2,72,896]{3,2,1,0:T(8,128)(2,1)S(1)} %collective-permute-done.3.refs_1_.refs_0_), channel_id=1, source_target_pairs={{0,4},{4,0},{1,5},{5,1},{2,6},{6,2},{3,7},{7,3},{8,12},{12,8},{9,1... | collective-permute-start | bytes 774152 | tf_op jit(solution)/shard_map/ppermute | solution.py:184
  22.9 13.6 %collective-permute-start.2 = (bf16[72,1536]{1,0:T(8,128)(2,1)S(1)}, bf16[72,1536]{1,0:T(8,128)(2,1)S(1)}, u32[]{:S(2)}, u32[]{:S(2)}) collective-permute-start(bf16[72,1536]{1,0:T(8,128)(2,1)S(1)} %shard_map.104.s_ref), channel_id=1, source_target_pairs={{1,2},{2,1},{5,6},{6,5},{9,10},{10,9},{13,14},{14,13},{17,18},{18,... | collective-permute-start | bytes 663560 | tf_op jit(solution)/shard_map/ppermute | solution.py:232
  27.1 10.3 %collective-permute-start.18 = (bf16[72,1536]{1,0:T(8,128)(2,1)S(1)}, bf16[72,1536]{1,0:T(8,128)(2,1)S(1)}, u32[]{:S(2)}, u32[]{:S(2)}) collective-permute-start(bf16[72,1536]{1,0:T(8,128)(2,1)S(1)} %shard_map.120.refs_1_), channel_id=1, source_target_pairs={{0,1},{3,2},{4,5},{7,6},{8,9},{11,10},{12,13},{15,14},{16,17},{19,... | collective-permute-start | bytes 663560 | tf_op jit(solution)/shard_map/ppermute | solution.py:220
  32.7 9.3 %collective-permute-start.15 = (bf16[72,1536]{1,0:T(8,128)(2,1)S(1)}, bf16[72,1536]{1,0:T(8,128)(2,1)S(1)}, u32[]{:S(2)}, u32[]{:S(2)}) collective-permute-start(bf16[72,1536]{1,0:T(8,128)(2,1)S(1)} %get-tuple-element.53), channel_id=1, source_target_pairs={{0,1},{3,2},{1,0},{2,3},{4,5},{7,6},{5,4},{6,7},{8,9},{11,10},{9,8... | collective-permute-start | bytes 663560 | tf_op jit(solution)/shard_map/ppermute | solution.py:220
  36.6 8.0 %collective-permute-start.5 = (bf16[72,1536]{1,0:T(8,128)(2,1)S(1)}, bf16[72,1536]{1,0:T(8,128)(2,1)S(1)}, u32[]{:S(2)}, u32[]{:S(2)}) collective-permute-start(bf16[72,1536]{1,0:T(8,128)(2,1)S(1)} %get-tuple-element.43), channel_id=1, source_target_pairs={{0,1},{3,2},{1,0},{2,3},{4,5},{7,6},{5,4},{6,7},{8,9},{11,10},{9,8... | collective-permute-start | bytes 663560 | tf_op jit(solution)/shard_map/ppermute | solution.py:220
  37.4 8.7 %collective-permute-start.19 = (bf16[72,1536]{1,0:T(8,128)(2,1)S(1)}, bf16[72,1536]{1,0:T(8,128)(2,1)S(1)}, u32[]{:S(2)}, u32[]{:S(2)}) collective-permute-start(bf16[72,1536]{1,0:T(8,128)(2,1)S(1)} %shard_map.121.s_ref), channel_id=1, source_target_pairs={{1,2},{2,1},{5,6},{6,5},{9,10},{10,9},{13,14},{14,13},{17,18},{18,... | collective-permute-start | bytes 663560 | tf_op jit(solution)/shard_map/ppermute | solution.py:232
  42.1 9.4 %collective-permute-start.25 = (bf16[72,1536]{1,0:T(8,128)(2,1)S(1)}, bf16[72,1536]{1,0:T(8,128)(2,1)S(1)}, u32[]{:S(2)}, u32[]{:S(2)}) collective-permute-start(bf16[72,1536]{1,0:T(8,128)(2,1)S(1)} %get-tuple-element.64.s_ref), channel_id=1, source_target_pairs={{1,2},{2,1},{5,6},{6,5},{9,10},{10,9},{13,14},{14,13},{17,18},{18,... | collective-permute-start | bytes 663560 | tf_op jit(solution)/shard_map/ppermute | solution.py:232
  44.6 9.8 %collective-permute-start.6 = (bf16[72,1536]{1,0:T(8,128)(2,1)S(1)}, bf16[72,1536]{1,0:T(8,128)(2,1)S(1)}, u32[]{:S(2)}, u32[]{:S(2)}) collective-permute-start(bf16[72,1536]{1,0:T(8,128)(2,1)S(1)} %get-tuple-element.45.s_ref), channel_id=1, source_target_pairs={{1,2},{2,1},{5,6},{6,5},{9,10},{10,9},{13,14},{14,13},{17,18},{18,... | collective-permute-start | bytes 663560 | tf_op jit(solution)/shard_map/ppermute | solution.py:232
  46.3 11.0 %collective-permute-start.20 = (bf16[72,1536]{1,0:T(8,128)(2,1)S(1)}, bf16[72,1536]{1,0:T(8,128)(2,1)S(1)}, u32[]{:S(2)}, u32[]{:S(2)}) collective-permute-start(bf16[72,1536]{1,0:T(8,128)(2,1)S(1)} %get-tuple-element.60), channel_id=1, source_target_pairs={{0,1},{3,2},{1,0},{2,3},{4,5},{7,6},{5,4},{6,7},{8,9},{11,10},{9,8... | collective-permute-start | bytes 663560 | tf_op jit(solution)/shard_map/ppermute | solution.py:220
  51.7 9.1 %collective-permute-start.26 = (bf16[72,1536]{1,0:T(8,128)(2,1)S(1)}, bf16[72,1536]{1,0:T(8,128)(2,1)S(1)}, u32[]{:S(2)}, u32[]{:S(2)}) collective-permute-start(bf16[72,1536]{1,0:T(8,128)(2,1)S(1)} %get-tuple-element.66), channel_id=1, source_target_pairs={{0,1},{3,2},{1,0},{2,3},{4,5},{7,6},{5,4},{6,7},{8,9},{11,10},{9,8... | collective-permute-start | bytes 663560 | tf_op jit(solution)/shard_map/ppermute | solution.py:220
  54.6 8.6 %collective-permute-start.8 = (bf16[72,1536]{1,0:T(8,128)(2,1)S(1)}, bf16[72,1536]{1,0:T(8,128)(2,1)S(1)}, u32[]{:S(2)}, u32[]{:S(2)}) collective-permute-start(bf16[72,1536]{1,0:T(8,128)(2,1)S(1)} %get-tuple-element.48), channel_id=1, source_target_pairs={{0,1},{3,2},{1,0},{2,3},{4,5},{7,6},{5,4},{6,7},{8,9},{11,10},{9,8... | collective-permute-start | bytes 663560 | tf_op jit(solution)/shard_map/ppermute | solution.py:220
  57.3 6.6 %collective-permute-start.23 = (bf16[72,1536]{1,0:T(8,128)(2,1)S(1)}, bf16[72,1536]{1,0:T(8,128)(2,1)S(1)}, u32[]{:S(2)}, u32[]{:S(2)}) collective-permute-start(bf16[72,1536]{1,0:T(8,128)(2,1)S(1)} %get-tuple-element.63.s_ref), channel_id=1, source_target_pairs={{1,2},{2,1},{5,6},{6,5},{9,10},{10,9},{13,14},{14,13},{17,18},{18,... | collective-permute-start | bytes 663560 | tf_op jit(solution)/shard_map/ppermute | solution.py:232
  60.8 6.0 %collective-permute-start.29 = (bf16[72,1536]{1,0:T(8,128)(2,1)S(1)}, bf16[72,1536]{1,0:T(8,128)(2,1)S(1)}, u32[]{:S(2)}, u32[]{:S(2)}) collective-permute-start(bf16[72,1536]{1,0:T(8,128)(2,1)S(1)} %get-tuple-element.69.s_ref), channel_id=1, source_target_pairs={{1,2},{2,1},{5,6},{6,5},{9,10},{10,9},{13,14},{14,13},{17,18},{18,... | collective-permute-start | bytes 663560 | tf_op jit(solution)/shard_map/ppermute | solution.py:232
  63.2 7.7 %collective-permute-start.9 = (bf16[72,1536]{1,0:T(8,128)(2,1)S(1)}, bf16[72,1536]{1,0:T(8,128)(2,1)S(1)}, u32[]{:S(2)}, u32[]{:S(2)}) collective-permute-start(bf16[72,1536]{1,0:T(8,128)(2,1)S(1)} %get-tuple-element.50.s_ref), channel_id=1, source_target_pairs={{1,2},{2,1},{5,6},{6,5},{9,10},{10,9},{13,14},{14,13},{17,18},{18,... | collective-permute-start | bytes 663560 | tf_op jit(solution)/shard_map/ppermute | solution.py:232
  64.0 10.6 %collective-permute-start.24 = (bf16[72,1536]{1,0:T(8,128)(2,1)S(1)}, bf16[72,1536]{1,0:T(8,128)(2,1)S(1)}, u32[]{:S(2)}, u32[]{:S(2)}) collective-permute-start(bf16[72,1536]{1,0:T(8,128)(2,1)S(1)} %shard_map.127.refs_1_), channel_id=1, source_target_pairs={{1,0},{2,3},{5,4},{6,7},{9,8},{10,11},{13,12},{14,15},{17,16},{18,... | collective-permute-start | bytes 663560 | tf_op jit(solution)/shard_map/ppermute | solution.py:220
  66.0 6.4 %collective-permute-start.21 = (bf16[72,896]{1,0:T(8,128)(2,1)S(1)}, bf16[72,896]{1,0:T(8,128)(2,1)S(1)}, u32[]{:S(2)}, u32[]{:S(2)}) collective-permute-start(bf16[72,896]{1,0:T(8,128)(2,1)S(1)} %shard_map.125), channel_id=1, source_target_pairs={{0,4},{4,0},{1,5},{5,1},{2,6},{6,2},{3,7},{7,3},{8,12},{12,8},{9,1... | collective-permute-start | bytes 387080 | tf_op jit(solution)/shard_map/ppermute | solution.py:184
  67.0 12.0 %collective-permute-start.30 = (bf16[72,1536]{1,0:T(8,128)(2,1)S(1)}, bf16[72,1536]{1,0:T(8,128)(2,1)S(1)}, u32[]{:S(2)}, u32[]{:S(2)}) collective-permute-start(bf16[72,1536]{1,0:T(8,128)(2,1)S(1)} %shard_map.134.refs_1_), channel_id=1, source_target_pairs={{1,0},{2,3},{5,4},{6,7},{9,8},{10,11},{13,12},{14,15},{17,16},{18,... | collective-permute-start | bytes 663560 | tf_op jit(solution)/shard_map/ppermute | solution.py:220
  69.0 7.9 %collective-permute-start.27 = (bf16[72,896]{1,0:T(8,128)(2,1)S(1)}, bf16[72,896]{1,0:T(8,128)(2,1)S(1)}, u32[]{:S(2)}, u32[]{:S(2)}) collective-permute-start(bf16[72,896]{1,0:T(8,128)(2,1)S(1)} %shard_map.132), channel_id=1, source_target_pairs={{0,4},{4,0},{1,5},{5,1},{2,6},{6,2},{3,7},{7,3},{8,12},{12,8},{9,1... | collective-permute-start | bytes 387080 | tf_op jit(solution)/shard_map/ppermute | solution.py:184
  70.9 9.9 %collective-permute-start.31 = (bf16[72,896]{1,0:T(8,128)(2,1)S(1)}, bf16[72,896]{1,0:T(8,128)(2,1)S(1)}, u32[]{:S(2)}, u32[]{:S(2)}) collective-permute-start(bf16[72,896]{1,0:T(8,128)(2,1)S(1)} %shard_map.137), channel_id=1, source_target_pairs={{0,4},{4,0},{1,5},{5,1},{2,6},{6,2},{3,7},{7,3},{8,12},{12,8},{9,1... | collective-permute-start | bytes 387080 | tf_op jit(solution)/shard_map/ppermute | solution.py:184
  72.4 10.3 %collective-permute-start.10 = (bf16[72,1536]{1,0:T(8,128)(2,1)S(1)}, bf16[72,1536]{1,0:T(8,128)(2,1)S(1)}, u32[]{:S(2)}, u32[]{:S(2)}) collective-permute-start(bf16[72,1536]{1,0:T(8,128)(2,1)S(1)} %shard_map.111.refs_1_), channel_id=1, source_target_pairs={{1,0},{2,3},{5,4},{6,7},{9,8},{10,11},{13,12},{14,15},{17,16},{18,... | collective-permute-start | bytes 663560 | tf_op jit(solution)/shard_map/ppermute | solution.py:220
  74.7 8.8 %collective-permute-start.16 = (bf16[72,896]{1,0:T(8,128)(2,1)S(1)}, bf16[72,896]{1,0:T(8,128)(2,1)S(1)}, u32[]{:S(2)}, u32[]{:S(2)}) collective-permute-start(bf16[72,896]{1,0:T(8,128)(2,1)S(1)} %get-tuple-element.57), channel_id=1, source_target_pairs={{0,4},{4,0},{1,5},{5,1},{2,6},{6,2},{3,7},{7,3},{8,12},{12,8},{9,1... | collective-permute-start | bytes 387080 | tf_op jit(solution)/shard_map/ppermute | solution.py:184
  76.9 8.6 %collective-permute-start.22 = (bf16[72,896]{1,0:T(8,128)(2,1)S(1)}, bf16[72,896]{1,0:T(8,128)(2,1)S(1)}, u32[]{:S(2)}, u32[]{:S(2)}) collective-permute-start(bf16[72,896]{1,0:T(8,128)(2,1)S(1)} %shard_map.126), channel_id=1, source_target_pairs={{0,8},{8,0},{16,24},{24,16},{1,9},{9,1},{17,25},{25,17},{2,10},{10... | collective-permute-start | bytes 387080 | tf_op jit(solution)/shard_map/ppermute | solution.py:184
  79.0 6.4 %collective-permute-start.28 = (bf16[72,896]{1,0:T(8,128)(2,1)S(1)}, bf16[72,896]{1,0:T(8,128)(2,1)S(1)}, u32[]{:S(2)}, u32[]{:S(2)}) collective-permute-start(bf16[72,896]{1,0:T(8,128)(2,1)S(1)} %shard_map.133), channel_id=1, source_target_pairs={{0,16},{8,24},{16,0},{24,8},{1,17},{9,25},{17,1},{25,9},{2,18},{10... | collective-permute-start | bytes 387080 | tf_op jit(solution)/shard_map/ppermute | solution.py:184
  80.9 5.8 %collective-permute-start.32 = (bf16[72,896]{1,0:T(8,128)(2,1)S(1)}, bf16[72,896]{1,0:T(8,128)(2,1)S(1)}, u32[]{:S(2)}, u32[]{:S(2)}) collective-permute-start(bf16[72,896]{1,0:T(8,128)(2,1)S(1)} %shard_map.138), channel_id=1, source_target_pairs={{0,24},{8,16},{16,8},{24,0},{1,25},{9,17},{17,9},{25,1},{2,26},{10... | collective-permute-start | bytes 387080 | tf_op jit(solution)/shard_map/ppermute | solution.py:184
  83.4 3.3 %copy-start.3 = (f32[192]{0:T(256)S(1)}, f32[192]{0:T(256)}, u32[]{:S(2)}) copy-start(f32[192]{0:T(256)} %param.9) | copy-start | bytes 2308

commit v6 on v5

--- a/solution.py
+++ b/solution.py
@@ -131,15 +131,16 @@
     acts, (wg_ref, wu_ref), outs = refs[:n], refs[n:n + 2], refs[n + 2:]
     a = jnp.concatenate([r[:, :2 * half] for r in acts], axis=0)
     o = (mm(a[:, :half], wg_ref[...], NT) + mm(a[:, half:], wu_ref[...], NT)).astype(BF16)
-    size = o.shape[0] // n
-    for i in range(n):
+    size = outs[0].shape[0]
+    for i in range(len(outs)):
         outs[i][...] = o[i * size:(i + 1) * size]
 
 
-def total_body(*refs):
+def total_body(n, *refs):
     value = refs[0][...].astype(F32)
+    size = value.shape[0]
     for r in refs[1:-1]:
-        value = value + r[...].astype(F32)
+        value = value + r[n * size:(n + 1) * size].astype(F32)
     refs[-1][...] = value.astype(BF16)
 
 
@@ -233,19 +234,20 @@
             )
             acts[now], leaving[i + lag] = both[0], both[-1]
 
-    groups = [[(0, 1)] + [(q, 0) for q in range(1, n_rep)]]
-    groups += [[(q, j)] for j in range(1, 4) for q in range(1, n_rep)] + [[(0, 2)], [(0, 3)], [(0, 0)]]
-    outs = {}
-    for group in groups:
-        done = call(
-            functools.partial(out_body, half, len(group)), [keep(size, quarter)] * len(group),
-            (*[full[w] for w in group], w_gate, w_up),
-        )
-        outs.update(zip(group, done))
+    def out(group, whole=False):
+        shape = [keep(len(group) * size, quarter)] if whole else [keep(size, quarter)] * len(group)
+        return call(functools.partial(out_body, half, len(group)), shape, (*[full[w] for w in group], w_gate, w_up))
+
+    back = {0: [], 2: []}
+    for j in (0, 2):
+        for q in range(1, n_rep):
+            both = out([(q, j), (q, j + 1)], True)[0]
+            back[j].append(swap(both, "replica", q))
+    mine = dict(zip((1, 2, 3), out([(0, 1), (0, 2), (0, 3)])))
+    mine[0] = out([(0, 0)])[0]
     total = {}
     for j in range(4):
-        back = [swap(outs[q, j], "replica", q) for q in range(1, n_rep)]
-        total[j] = call(total_body, keep(size, quarter), (outs[0, j], *back))
+        total[j] = call(functools.partial(total_body, j % 2), keep(size, quarter), (mine[j], *back[j - j % 2]))
     ret = [total[k // each][k % each * cap:(k % each + 1) * cap] for k in range(n_expert)]
     ret = [ret[0]] + [swap(ret[k], "expert", k) for k in range(1, n_expert)]
     sds = jax.ShapeDtypeStruct

time: 88.4 us -> 91.5 us (1.035)
  waiting for transfers between devices: 23.4 us -> 29.8 us
  Pallas kernels: 19.7 us -> 17.8 us
  starting transfers between devices: 43.7 us -> 42.1 us
    ppermute x11, waiting for transfers between devices: 14 us -> 22 us  [steps(): came = lax.ppermute(leaving[i], 'seq', pairs)]
    pallas_call x40 -> x37, Pallas kernels: 19.7 us -> 17.8 us  [call(): pl.pallas_call(body, out_shape=outs, in_specs=[pl.BlockSpec(memory_space=...]
    ppermute x14 -> x12, waiting for transfers between devices: 9.42 us -> 7.78 us  [swap(): lax.ppermute(x, axis, [(i, i ^ k) for i in range(lax.axis_size(axis))])]
    ppermute x14 -> x12, starting transfers between devices: 13.1 us -> 11.5 us  [swap(): lax.ppermute(x, axis, [(i, i ^ k) for i in range(lax.axis_size(axis))])]
  transfers between devices with their start and end apart: 33 -> 31, of which waited for: 15 -> 13; matrix products, arithmetic and copies ran while one was open for 0% -> 0% of each run, Pallas kernels for 19% -> 16%
where the time goes in v6:
time: 91.5 us; the launch traced here: 90.8 us
  starting transfers between devices  42.1 us (46%)
  waiting for transfers between devices  29.8 us (33%)
  Pallas kernels  17.8 us (19%)
  between operations  1.12 us (1%)
    ppermute x11, starting transfers between devices, steps(): came = lax.ppermute(leaving[i], 'seq', pairs)  25.1 us
    ppermute x11, waiting for transfers between devices, steps(): came = lax.ppermute(leaving[i], 'seq', pairs)  22 us
    pallas_call x37, Pallas kernels, call(): pl.pallas_call(body, out_shape=outs, in_specs=[pl.BlockSpec(memory_space=...  17.8 us
    ppermute x12, starting transfers between devices, swap(): lax.ppermute(x, axis, [(i, i ^ k) for i in range(lax.axis_size(axis))])  11.5 us
    ppermute x12, waiting for transfers between devices, swap(): lax.ppermute(x, axis, [(i, i ^ k) for i in range(lax.axis_size(axis))])  7.78 us
    ppermute x8, starting transfers between devices, steps(): lax.ppermute(done[0], 'seq', middle)  5.4 us
  transfers between devices with their start and end apart: 31, of which 13 were waited for; matrix products, arithmetic and copies ran while one was open for 0% of the time, Pallas kernels for 16%

profile of v6, /device:TPU:0, one launch (start us, length us, event | category | flops | bytes accessed | tf_op | source)
XLA Modules:
  0.0 90.8 jit_solution(15759598211529489044)
XLA Ops:
  0.7 2.1 %shard_map.102 = (bf16[1,2,72,896]{3,2,1,0:T(8,128)(2,1)S(1)}, bf16[1,2,72,896]{3,2,1,0:T(8,128)(2,1)S(1)}, bf16[1,2,72,896]{3,2,1,0:T(8,128)(2,1)S(1)}, bf16[1,...) custom-call(s32[1,192]{1,0:T(1,128)} %bitcast.33, f32[1,192]{1,0:T(1,128)} %bitcast.31, bf16[192,896]{1,0:T(8,128)(2,1)} %tokens_ref.1, ...), custom_call_target="tpu_custom_call" | custom-call | tf_op jit(solution)/shard_map/pallas_call | solution.py:34
  2.8 0.6 collective-permute-start.7
  3.3 2.6 %collective-permute-start = (bf16[1,2,72,896]{3,2,1,0:T(8,128)(2,1)S(1)}, bf16[1,2,72,896]{3,2,1,0:T(8,128)(2,1)S(1)}, u32[]{:S(2)}, u32[]{:S(2)}) collective-permute-start(bf16[1,2,72,896]{3,2,1,0:T(8,128)(2,1)S(1)} %get-tuple-element.42.refs_0_.refs_1_), channel_id=1, source_target_pairs={{0,4},{4,0},{1,5},{5,1},{2,6},{6,2},{3,7},{7,3},{8,12},{12,8},{9,1... | collective-permute-start | bytes 774152 | tf_op jit(solution)/shard_map/ppermute | solution.py:185
  5.9 1.5 %collective-permute-start.14 = (bf16[1,2,72,896]{3,2,1,0:T(8,128)(2,1)S(1)}, bf16[1,2,72,896]{3,2,1,0:T(8,128)(2,1)S(1)}, u32[]{:S(2)}, u32[]{:S(2)}) collective-permute-start(bf16[1,2,72,896]{3,2,1,0:T(8,128)(2,1)S(1)} %get-tuple-element.53), channel_id=1, source_target_pairs={{0,16},{8,24},{16,0},{24,8},{1,17},{9,25},{17,1},{25,9},{2,18},{10... | collective-permute-start | bytes 774152 | tf_op jit(solution)/shard_map/ppermute | solution.py:185
  7.4 2.5 %shard_map.108 = (bf16[72,1536]{1,0:T(8,128)(2,1)S(1)}, bf16[72,1536]{1,0:T(8,128)(2,1)S(1)}) custom-call(bf16[1,2,72,896]{3,2,1,0:T(8,128)(2,1)S(1)} %get-tuple-element.42.refs_0_.refs_1_, bf16[1,2,72,896]{3,2,1,0:T(8,128)(2,1)S(1)} %collective-permute-done.7.refs_1_.refs_0_, bf16[896,512]{1,0:T(8,128)(2,1)} %bitcast.5, bf16[896,512]{1,0:T(8,128)(2,1)} %bitcast.15, ...), custom_call_target="tpu_custom_call" | custom-call | tf_op jit(solution)/shard_map/pallas_call | solution.py:34
  9.9 3.5 %collective-permute-start.17 = (bf16[72,1536]{1,0:T(8,128)(2,1)S(1)}, bf16[72,1536]{1,0:T(8,128)(2,1)S(1)}, u32[]{:S(2)}, u32[]{:S(2)}) collective-permute-start(bf16[72,1536]{1,0:T(8,128)(2,1)S(1)} %get-tuple-element.58.refs_1_), channel_id=1, source_target_pairs={{0,1},{3,2},{4,5},{7,6},{8,9},{11,10},{12,13},{15,14},{16,17},{19,... | collective-permute-start | bytes 663560 | tf_op jit(solution)/shard_map/ppermute | solution.py:221
  13.5 0.7 shard_map.103.refs_1_
  14.2 2.9 %collective-permute-start.1 = (bf16[72,1536]{1,0:T(8,128)(2,1)S(1)}, bf16[72,1536]{1,0:T(8,128)(2,1)S(1)}, u32[]{:S(2)}, u32[]{:S(2)}) collective-permute-start(bf16[72,1536]{1,0:T(8,128)(2,1)S(1)} %shard_map.103.refs_1_), channel_id=1, source_target_pairs={{0,1},{3,2},{4,5},{7,6},{8,9},{11,10},{12,13},{15,14},{16,17},{19,... | collective-permute-start | bytes 663560 | tf_op jit(solution)/shard_map/ppermute | solution.py:221
  17.2 1.6 %collective-permute-start.11 = (bf16[1,2,72,896]{3,2,1,0:T(8,128)(2,1)S(1)}, bf16[1,2,72,896]{3,2,1,0:T(8,128)(2,1)S(1)}, u32[]{:S(2)}, u32[]{:S(2)}) collective-permute-start(bf16[1,2,72,896]{3,2,1,0:T(8,128)(2,1)S(1)} %collective-permute-done.7.refs_1_.refs_0_), channel_id=1, source_target_pairs={{0,4},{4,0},{1,5},{5,1},{2,6},{6,2},{3,7},{7,3},{8,12},{12,8},{9,1... | collective-permute-start | bytes 774152 | tf_op jit(solution)/shard_map/ppermute | solution.py:185
  19.3 0.7 collective-permute-start.18
  20.0 1.7 %collective-permute-done.3.refs_1_.refs_0_ = bf16[1,2,72,896]{3,2,1,0:T(8,128)(2,1)S(1)} collective-permute-done((bf16[1,2,72,896]{3,2,1,0:T(8,128)(2,1)S(1)}, bf16[1,2,72,896]{3,2,1,0:T(8,128)(2,1)S(1)}, u32[]{:S(2)}, u32[]{:S(2)}) %collective-permute-start.3) | collective-permute-done | bytes 258080 | tf_op jit(solution)/shard_map/ppermute | solution.py:185
  22.9 0.7 collective-permute-start.2
  23.6 2.8 %collective-permute-done.11.refs_0_.refs_2_ = bf16[1,2,72,896]{3,2,1,0:T(8,128)(2,1)S(1)} collective-permute-done((bf16[1,2,72,896]{3,2,1,0:T(8,128)(2,1)S(1)}, bf16[1,2,72,896]{3,2,1,0:T(8,128)(2,1)S(1)}, u32[]{:S(2)}, u32[]{:S(2)}) %collective-permute-start.11) | collective-permute-done | bytes 258080 | tf_op jit(solution)/shard_map/ppermute | solution.py:185
  26.3 0.7 shard_map.114.refs_1_
  27.1 4.5 %collective-permute-start.12 = (bf16[72,1536]{1,0:T(8,128)(2,1)S(1)}, bf16[72,1536]{1,0:T(8,128)(2,1)S(1)}, u32[]{:S(2)}, u32[]{:S(2)}) collective-permute-start(bf16[72,1536]{1,0:T(8,128)(2,1)S(1)} %shard_map.114.refs_1_), channel_id=1, source_target_pairs={{0,1},{3,2},{4,5},{7,6},{8,9},{11,10},{12,13},{15,14},{16,17},{19,... | collective-permute-start | bytes 663560 | tf_op jit(solution)/shard_map/ppermute | solution.py:221
  31.9 0.7 shard_map.122.refs_0_.refs_1_
  32.8 2.9 %collective-permute-done.4.refs_0_.refs_4_ = bf16[1,2,72,896]{3,2,1,0:T(8,128)(2,1)S(1)} collective-permute-done((bf16[1,2,72,896]{3,2,1,0:T(8,128)(2,1)S(1)}, bf16[1,2,72,896]{3,2,1,0:T(8,128)(2,1)S(1)}, u32[]{:S(2)}, u32[]{:S(2)}) %collective-permute-start.4) | collective-permute-done | bytes 258080 | tf_op jit(solution)/shard_map/ppermute | solution.py:185
  35.7 0.7 shard_map.105.refs_0_.refs_1_
  36.7 0.6 collective-permute-done.12.refs_0_
  37.4 0.7 collective-permute-start.13
  38.1 4.0 %collective-permute-done.20.refs_0_ = bf16[72,1536]{1,0:T(8,128)(2,1)S(1)} collective-permute-done((bf16[72,1536]{1,0:T(8,128)(2,1)S(1)}, bf16[72,1536]{1,0:T(8,128)(2,1)S(1)}, u32[]{:S(2)}, u32[]{:S(2)}) %collective-permute-start.20) | collective-permute-done | bytes 221216 | tf_op jit(solution)/shard_map/ppermute | solution.py:221
  42.1 0.7 collective-permute-start.23
  42.8 1.7 %collective-permute-done.5.refs_0_ = bf16[72,1536]{1,0:T(8,128)(2,1)S(1)} collective-permute-done((bf16[72,1536]{1,0:T(8,128)(2,1)S(1)}, bf16[72,1536]{1,0:T(8,128)(2,1)S(1)}, u32[]{:S(2)}, u32[]{:S(2)}) %collective-permute-start.5) | collective-permute-done | bytes 221216 | tf_op jit(solution)/shard_map/ppermute | solution.py:221
  44.6 0.7 collective-permute-start.6
  45.3 0.8 shard_map.116
  46.2 5.3 %collective-permute-start.15 = (bf16[72,1536]{1,0:T(8,128)(2,1)S(1)}, bf16[72,1536]{1,0:T(8,128)(2,1)S(1)}, u32[]{:S(2)}, u32[]{:S(2)}) collective-permute-start(bf16[72,1536]{1,0:T(8,128)(2,1)S(1)} %get-tuple-element.55), channel_id=1, source_target_pairs={{0,1},{3,2},{1,0},{2,3},{4,5},{7,6},{5,4},{6,7},{8,9},{11,10},{9,8... | collective-permute-start | bytes 663560 | tf_op jit(solution)/shard_map/ppermute | solution.py:221
  51.7 2.7 %collective-permute-start.24 = (bf16[72,1536]{1,0:T(8,128)(2,1)S(1)}, bf16[72,1536]{1,0:T(8,128)(2,1)S(1)}, u32[]{:S(2)}, u32[]{:S(2)}) collective-permute-start(bf16[72,1536]{1,0:T(8,128)(2,1)S(1)} %get-tuple-element.65), channel_id=1, source_target_pairs={{0,1},{3,2},{1,0},{2,3},{4,5},{7,6},{5,4},{6,7},{8,9},{11,10},{9,8... | collective-permute-start | bytes 663560 | tf_op jit(solution)/shard_map/ppermute | solution.py:221
  54.5 2.2 %collective-permute-start.8 = (bf16[72,1536]{1,0:T(8,128)(2,1)S(1)}, bf16[72,1536]{1,0:T(8,128)(2,1)S(1)}, u32[]{:S(2)}, u32[]{:S(2)}) collective-permute-start(bf16[72,1536]{1,0:T(8,128)(2,1)S(1)} %get-tuple-element.49), channel_id=1, source_target_pairs={{0,1},{3,2},{1,0},{2,3},{4,5},{7,6},{5,4},{6,7},{8,9},{11,10},{9,8... | collective-permute-start | bytes 663560 | tf_op jit(solution)/shard_map/ppermute | solution.py:221
  57.3 0.7 collective-permute-start.21
  58.0 2.8 %collective-permute-done.24.refs_0_ = bf16[72,1536]{1,0:T(8,128)(2,1)S(1)} collective-permute-done((bf16[72,1536]{1,0:T(8,128)(2,1)S(1)}, bf16[72,1536]{1,0:T(8,128)(2,1)S(1)}, u32[]{:S(2)}, u32[]{:S(2)}) %collective-permute-start.24) | collective-permute-done | bytes 221216 | tf_op jit(solution)/shard_map/ppermute | solution.py:221
  60.8 0.7 collective-permute-start.25
  61.5 1.6 %collective-permute-done.8.refs_0_ = bf16[72,1536]{1,0:T(8,128)(2,1)S(1)} collective-permute-done((bf16[72,1536]{1,0:T(8,128)(2,1)S(1)}, bf16[72,1536]{1,0:T(8,128)(2,1)S(1)}, u32[]{:S(2)}, u32[]{:S(2)}) %collective-permute-start.8) | collective-permute-done | bytes 221216 | tf_op jit(solution)/shard_map/ppermute | solution.py:221
  63.2 0.7 collective-permute-start.9
  63.8 0.7 shard_map.133
  64.6 0.9 collective-permute-start.28
  65.5 0.7 shard_map.119
  66.2 1.3 %collective-permute-start.16 = (bf16[144,896]{1,0:T(8,128)(2,1)S(1)}, bf16[144,896]{1,0:T(8,128)(2,1)S(1)}, u32[]{:S(2)}, u32[]{:S(2)}) collective-permute-start(bf16[144,896]{1,0:T(8,128)(2,1)S(1)} %shard_map.119), channel_id=1, source_target_pairs={{0,4},{4,0},{1,5},{5,1},{2,6},{6,2},{3,7},{7,3},{8,12},{12,8},{9,1... | collective-permute-start | bytes 774152 | tf_op jit(solution)/shard_map/ppermute | solution.py:185
  67.6 1.3 %collective-permute-start.22 = (bf16[72,1536]{1,0:T(8,128)(2,1)S(1)}, bf16[72,1536]{1,0:T(8,128)(2,1)S(1)}, u32[]{:S(2)}, u32[]{:S(2)}) collective-permute-start(bf16[72,1536]{1,0:T(8,128)(2,1)S(1)} %shard_map.125.refs_1_), channel_id=1, source_target_pairs={{1,0},{2,3},{5,4},{6,7},{9,8},{10,11},{13,12},{14,15},{17,16},{18,... | collective-permute-start | bytes 663560 | tf_op jit(solution)/shard_map/ppermute | solution.py:221
  69.0 1.3 %collective-permute-start.26 = (bf16[72,1536]{1,0:T(8,128)(2,1)S(1)}, bf16[72,1536]{1,0:T(8,128)(2,1)S(1)}, u32[]{:S(2)}, u32[]{:S(2)}) collective-permute-start(bf16[72,1536]{1,0:T(8,128)(2,1)S(1)} %shard_map.129.refs_1_), channel_id=1, source_target_pairs={{1,0},{2,3},{5,4},{6,7},{9,8},{10,11},{13,12},{14,15},{17,16},{18,... | collective-permute-start | bytes 663560 | tf_op jit(solution)/shard_map/ppermute | solution.py:221
  70.4 1.3 %collective-permute-start.10 = (bf16[72,1536]{1,0:T(8,128)(2,1)S(1)}, bf16[72,1536]{1,0:T(8,128)(2,1)S(1)}, u32[]{:S(2)}, u32[]{:S(2)}) collective-permute-start(bf16[72,1536]{1,0:T(8,128)(2,1)S(1)} %shard_map.111.refs_1_), channel_id=1, source_target_pairs={{1,0},{2,3},{5,4},{6,7},{9,8},{10,11},{13,12},{14,15},{17,16},{18,... | collective-permute-start | bytes 663560 | tf_op jit(solution)/shard_map/ppermute | solution.py:221
  71.7 7.9 %collective-permute-done.22.refs_0_ = bf16[72,1536]{1,0:T(8,128)(2,1)S(1)} collective-permute-done((bf16[72,1536]{1,0:T(8,128)(2,1)S(1)}, bf16[72,1536]{1,0:T(8,128)(2,1)S(1)}, u32[]{:S(2)}, u32[]{:S(2)}) %collective-permute-start.22) | collective-permute-done | bytes 221216 | tf_op jit(solution)/shard_map/ppermute | solution.py:221
  79.7 2.3 %collective-permute-done.26.refs_0_ = bf16[72,1536]{1,0:T(8,128)(2,1)S(1)} collective-permute-done((bf16[72,1536]{1,0:T(8,128)(2,1)S(1)}, bf16[72,1536]{1,0:T(8,128)(2,1)S(1)}, u32[]{:S(2)}, u32[]{:S(2)}) %collective-permute-start.26) | collective-permute-done | bytes 221216 | tf_op jit(solution)/shard_map/ppermute | solution.py:221
  82.0 0.7 shard_map.131
  83.6 1.4 %collective-permute-start.27 = (bf16[72,896]{1,0:T(8,128)(2,1)S(1)}, bf16[72,896]{1,0:T(8,128)(2,1)S(1)}, u32[]{:S(2)}, u32[]{:S(2)}) collective-permute-start(bf16[72,896]{1,0:T(8,128)(2,1)S(1)} %shard_map.132), channel_id=1, source_target_pairs={{0,8},{8,0},{16,24},{24,16},{1,9},{9,1},{17,25},{25,17},{2,10},{10... | collective-permute-start | bytes 387080 | tf_op jit(solution)/shard_map/ppermute | solution.py:185
  85.0 1.7 %shard_map.137 = (f32[896,1024]{1,0:T(8,128)S(1)}, f32[512,896]{1,0:T(8,128)S(1)}) custom-call(bf16[1,2,72,896]{3,2,1,0:T(8,128)(2,1)S(1)} %collective-permute-done.7.refs_1_.refs_0_, bf16[1,2,72,896]{3,2,1,0:T(8,128)(2,1)S(1)} %collective-permute-done.refs_0_.refs_1_, bf16[1,2,72,896]{3,2,1,0:T(8,128)(2,1)S(1)} %collective-permute-done.11.refs_0_.refs_2_, ...), custom_call_target="tpu_custom_call" | custom-call | tf_op jit(solution)/shard_map/pallas_call | solution.py:34
  86.7 0.7 shard_map.113.refs_0_
  87.5 2.0 %shard_map.138 = (bf16[1,896,512]{2,1,0:T(8,128)(2,1)}, bf16[1,896,512]{2,1,0:T(8,128)(2,1)}, bf16[1,512,896]{2,1,0:T(8,128)(2,1)}) custom-call(bf16[1,2,72,896]{3,2,1,0:T(8,128)(2,1)S(1)} %collective-permute-done.3.refs_1_.refs_0_, bf16[1,2,72,896]{3,2,1,0:T(8,128)(2,1)S(1)} %get-tuple-element.42.refs_0_.refs_1_, bf16[72,1536]{1,0:T(8,128)(2,1)S(1)} %shard_map.130.refs_2_, ...), custom_call_target="tpu_custom_call" | custom-call | tf_op jit(solution)/shard_map/pallas_call | solution.py:34
  89.5 1.3 %shard_map.136 = bf16[192,896]{1,0:T(8,128)(2,1)} custom-call(f32[1,192]{1,0:T(1,128)S(1)} %bitcast.32, bf16[4,72,192]{2,1,0:T(8,128)(2,1)S(1)} %get-tuple-element.41.pick_ref, bf16[72,896]{1,0:T(8,128)(2,1)S(1)} %shard_map.120.refs_0_, bf16[72,896]{1,0:T(8,128)(2,1)S(1)} %collective-permute-done.27.refs_1_, ...), custom_call_target="tpu_custom_call" | custom-call | tf_op jit(solution)/shard_map/pallas_call | solution.py:34
  (59 shorter events, 5.0 us)
Async XLA Ops:
  0.6 12.9 %copy-start.2 = (bf16[1,512,896]{2,1,0:T(8,128)(2,1)S(1)}, bf16[1,512,896]{2,1,0:T(8,128)(2,1)}, u32[]{:S(2)}) copy-start(bf16[1,512,896]{2,1,0:T(8,128)(2,1)} %param.13) | copy-start | bytes 2752516
  0.6 12.9 %copy-start.1 = (bf16[1,896,512]{2,1,0:T(8,128)(2,1)S(1)}, bf16[1,896,512]{2,1,0:T(8,128)(2,1)}, u32[]{:S(2)}) copy-start(bf16[1,896,512]{2,1,0:T(8,128)(2,1)} %param.12) | copy-start | bytes 2752516
  0.7 12.9 %copy-start = (bf16[1,896,512]{2,1,0:T(8,128)(2,1)S(1)}, bf16[1,896,512]{2,1,0:T(8,128)(2,1)}, u32[]{:S(2)}) copy-start(bf16[1,896,512]{2,1,0:T(8,128)(2,1)} %param.11) | copy-start | bytes 2752516
  2.8 4.6 %collective-permute-start.7 = (bf16[1,2,72,896]{3,2,1,0:T(8,128)(2,1)S(1)}, bf16[1,2,72,896]{3,2,1,0:T(8,128)(2,1)S(1)}, u32[]{:S(2)}, u32[]{:S(2)}) collective-permute-start(bf16[1,2,72,896]{3,2,1,0:T(8,128)(2,1)S(1)} %get-tuple-element.47), channel_id=1, source_target_pairs={{0,8},{8,0},{16,24},{24,16},{1,9},{9,1},{17,25},{25,17},{2,10},{10... | collective-permute-start | bytes 774152 | tf_op jit(solution)/shard_map/ppermute | solution.py:185
  3.3 10.2 %collective-permute-start = (bf16[1,2,72,896]{3,2,1,0:T(8,128)(2,1)S(1)}, bf16[1,2,72,896]{3,2,1,0:T(8,128)(2,1)S(1)}, u32[]{:S(2)}, u32[]{:S(2)}) collective-permute-start(bf16[1,2,72,896]{3,2,1,0:T(8,128)(2,1)S(1)} %get-tuple-element.42.refs_0_.refs_1_), channel_id=1, source_target_pairs={{0,4},{4,0},{1,5},{5,1},{2,6},{6,2},{3,7},{7,3},{8,12},{12,8},{9,1... | collective-permute-start | bytes 774152 | tf_op jit(solution)/shard_map/ppermute | solution.py:185
  5.9 12.9 %collective-permute-start.14 = (bf16[1,2,72,896]{3,2,1,0:T(8,128)(2,1)S(1)}, bf16[1,2,72,896]{3,2,1,0:T(8,128)(2,1)S(1)}, u32[]{:S(2)}, u32[]{:S(2)}) collective-permute-start(bf16[1,2,72,896]{3,2,1,0:T(8,128)(2,1)S(1)} %get-tuple-element.53), channel_id=1, source_target_pairs={{0,16},{8,24},{16,0},{24,8},{1,17},{9,25},{17,1},{25,9},{2,18},{10... | collective-permute-start | bytes 774152 | tf_op jit(solution)/shard_map/ppermute | solution.py:185
  9.9 9.4 %collective-permute-start.17 = (bf16[72,1536]{1,0:T(8,128)(2,1)S(1)}, bf16[72,1536]{1,0:T(8,128)(2,1)S(1)}, u32[]{:S(2)}, u32[]{:S(2)}) collective-permute-start(bf16[72,1536]{1,0:T(8,128)(2,1)S(1)} %get-tuple-element.58.refs_1_), channel_id=1, source_target_pairs={{0,1},{3,2},{4,5},{7,6},{8,9},{11,10},{12,13},{15,14},{16,17},{19,... | collective-permute-start | bytes 663560 | tf_op jit(solution)/shard_map/ppermute | solution.py:221
  13.4 8.3 %collective-permute-start.3 = (bf16[1,2,72,896]{3,2,1,0:T(8,128)(2,1)S(1)}, bf16[1,2,72,896]{3,2,1,0:T(8,128)(2,1)S(1)}, u32[]{:S(2)}, u32[]{:S(2)}) collective-permute-start(bf16[1,2,72,896]{3,2,1,0:T(8,128)(2,1)S(1)} %get-tuple-element.43), channel_id=1, source_target_pairs={{0,24},{8,16},{16,8},{24,0},{1,25},{9,17},{17,9},{25,1},{2,26},{10... | collective-permute-start | bytes 774152 | tf_op jit(solution)/shard_map/ppermute | solution.py:185
  14.2 8.6 %collective-permute-start.1 = (bf16[72,1536]{1,0:T(8,128)(2,1)S(1)}, bf16[72,1536]{1,0:T(8,128)(2,1)S(1)}, u32[]{:S(2)}, u32[]{:S(2)}) collective-permute-start(bf16[72,1536]{1,0:T(8,128)(2,1)S(1)} %shard_map.103.refs_1_), channel_id=1, source_target_pairs={{0,1},{3,2},{4,5},{7,6},{8,9},{11,10},{12,13},{15,14},{16,17},{19,... | collective-permute-start | bytes 663560 | tf_op jit(solution)/shard_map/ppermute | solution.py:221
  17.2 9.2 %collective-permute-start.11 = (bf16[1,2,72,896]{3,2,1,0:T(8,128)(2,1)S(1)}, bf16[1,2,72,896]{3,2,1,0:T(8,128)(2,1)S(1)}, u32[]{:S(2)}, u32[]{:S(2)}) collective-permute-start(bf16[1,2,72,896]{3,2,1,0:T(8,128)(2,1)S(1)} %collective-permute-done.7.refs_1_.refs_0_), channel_id=1, source_target_pairs={{0,4},{4,0},{1,5},{5,1},{2,6},{6,2},{3,7},{7,3},{8,12},{12,8},{9,1... | collective-permute-start | bytes 774152 | tf_op jit(solution)/shard_map/ppermute | solution.py:185
  18.7 13.1 %collective-permute-start.19 = (bf16[1,2,72,896]{3,2,1,0:T(8,128)(2,1)S(1)}, bf16[1,2,72,896]{3,2,1,0:T(8,128)(2,1)S(1)}, u32[]{:S(2)}, u32[]{:S(2)}) collective-permute-start(bf16[1,2,72,896]{3,2,1,0:T(8,128)(2,1)S(1)} %collective-permute-done.14.refs_0_.refs_5_), channel_id=1, source_target_pairs={{0,4},{4,0},{1,5},{5,1},{2,6},{6,2},{3,7},{7,3},{8,12},{12,8},{9,1... | collective-permute-start | bytes 774152 | tf_op jit(solution)/shard_map/ppermute | solution.py:185
  19.3 13.3 %collective-permute-start.18 = (bf16[72,1536]{1,0:T(8,128)(2,1)S(1)}, bf16[72,1536]{1,0:T(8,128)(2,1)S(1)}, u32[]{:S(2)}, u32[]{:S(2)}) collective-permute-start(bf16[72,1536]{1,0:T(8,128)(2,1)S(1)} %shard_map.121.s_ref), channel_id=1, source_target_pairs={{1,2},{2,1},{5,6},{6,5},{9,10},{10,9},{13,14},{14,13},{17,18},{18,... | collective-permute-start | bytes 663560 | tf_op jit(solution)/shard_map/ppermute | solution.py:233
  21.7 14.0 %collective-permute-start.4 = (bf16[1,2,72,896]{3,2,1,0:T(8,128)(2,1)S(1)}, bf16[1,2,72,896]{3,2,1,0:T(8,128)(2,1)S(1)}, u32[]{:S(2)}, u32[]{:S(2)}) collective-permute-start(bf16[1,2,72,896]{3,2,1,0:T(8,128)(2,1)S(1)} %collective-permute-done.3.refs_1_.refs_0_), channel_id=1, source_target_pairs={{0,4},{4,0},{1,5},{5,1},{2,6},{6,2},{3,7},{7,3},{8,12},{12,8},{9,1... | collective-permute-start | bytes 774152 | tf_op jit(solution)/shard_map/ppermute | solution.py:185
  22.9 13.6 %collective-permute-start.2 = (bf16[72,1536]{1,0:T(8,128)(2,1)S(1)}, bf16[72,1536]{1,0:T(8,128)(2,1)S(1)}, u32[]{:S(2)}, u32[]{:S(2)}) collective-permute-start(bf16[72,1536]{1,0:T(8,128)(2,1)S(1)} %shard_map.104.s_ref), channel_id=1, source_target_pairs={{1,2},{2,1},{5,6},{6,5},{9,10},{10,9},{13,14},{14,13},{17,18},{18,... | collective-permute-start | bytes 663560 | tf_op jit(solution)/shard_map/ppermute | solution.py:233
  27.1 10.3 %collective-permute-start.12 = (bf16[72,1536]{1,0:T(8,128)(2,1)S(1)}, bf16[72,1536]{1,0:T(8,128)(2,1)S(1)}, u32[]{:S(2)}, u32[]{:S(2)}) collective-permute-start(bf16[72,1536]{1,0:T(8,128)(2,1)S(1)} %shard_map.114.refs_1_), channel_id=1, source_target_pairs={{0,1},{3,2},{4,5},{7,6},{8,9},{11,10},{12,13},{15,14},{16,17},{19,... | collective-permute-start | bytes 663560 | tf_op jit(solution)/shard_map/ppermute | solution.py:221
  32.7 9.3 %collective-permute-start.20 = (bf16[72,1536]{1,0:T(8,128)(2,1)S(1)}, bf16[72,1536]{1,0:T(8,128)(2,1)S(1)}, u32[]{:S(2)}, u32[]{:S(2)}) collective-permute-start(bf16[72,1536]{1,0:T(8,128)(2,1)S(1)} %get-tuple-element.59), channel_id=1, source_target_pairs={{0,1},{3,2},{1,0},{2,3},{4,5},{7,6},{5,4},{6,7},{8,9},{11,10},{9,8... | collective-permute-start | bytes 663560 | tf_op jit(solution)/shard_map/ppermute | solution.py:221
  36.6 8.0 %collective-permute-start.5 = (bf16[72,1536]{1,0:T(8,128)(2,1)S(1)}, bf16[72,1536]{1,0:T(8,128)(2,1)S(1)}, u32[]{:S(2)}, u32[]{:S(2)}) collective-permute-start(bf16[72,1536]{1,0:T(8,128)(2,1)S(1)} %get-tuple-element.44), channel_id=1, source_target_pairs={{0,1},{3,2},{1,0},{2,3},{4,5},{7,6},{5,4},{6,7},{8,9},{11,10},{9,8... | collective-permute-start | bytes 663560 | tf_op jit(solution)/shard_map/ppermute | solution.py:221
  37.4 8.7 %collective-permute-start.13 = (bf16[72,1536]{1,0:T(8,128)(2,1)S(1)}, bf16[72,1536]{1,0:T(8,128)(2,1)S(1)}, u32[]{:S(2)}, u32[]{:S(2)}) collective-permute-start(bf16[72,1536]{1,0:T(8,128)(2,1)S(1)} %shard_map.115.s_ref), channel_id=1, source_target_pairs={{1,2},{2,1},{5,6},{6,5},{9,10},{10,9},{13,14},{14,13},{17,18},{18,... | collective-permute-start | bytes 663560 | tf_op jit(solution)/shard_map/ppermute | solution.py:233
  42.1 9.4 %collective-permute-start.23 = (bf16[72,1536]{1,0:T(8,128)(2,1)S(1)}, bf16[72,1536]{1,0:T(8,128)(2,1)S(1)}, u32[]{:S(2)}, u32[]{:S(2)}) collective-permute-start(bf16[72,1536]{1,0:T(8,128)(2,1)S(1)} %get-tuple-element.63.s_ref), channel_id=1, source_target_pairs={{1,2},{2,1},{5,6},{6,5},{9,10},{10,9},{13,14},{14,13},{17,18},{18,... | collective-permute-start | bytes 663560 | tf_op jit(solution)/shard_map/ppermute | solution.py:233
  44.6 9.8 %collective-permute-start.6 = (bf16[72,1536]{1,0:T(8,128)(2,1)S(1)}, bf16[72,1536]{1,0:T(8,128)(2,1)S(1)}, u32[]{:S(2)}, u32[]{:S(2)}) collective-permute-start(bf16[72,1536]{1,0:T(8,128)(2,1)S(1)} %get-tuple-element.46.s_ref), channel_id=1, source_target_pairs={{1,2},{2,1},{5,6},{6,5},{9,10},{10,9},{13,14},{14,13},{17,18},{18,... | collective-permute-start | bytes 663560 | tf_op jit(solution)/shard_map/ppermute | solution.py:233
  46.2 11.0 %collective-permute-start.15 = (bf16[72,1536]{1,0:T(8,128)(2,1)S(1)}, bf16[72,1536]{1,0:T(8,128)(2,1)S(1)}, u32[]{:S(2)}, u32[]{:S(2)}) collective-permute-start(bf16[72,1536]{1,0:T(8,128)(2,1)S(1)} %get-tuple-element.55), channel_id=1, source_target_pairs={{0,1},{3,2},{1,0},{2,3},{4,5},{7,6},{5,4},{6,7},{8,9},{11,10},{9,8... | collective-permute-start | bytes 663560 | tf_op jit(solution)/shard_map/ppermute | solution.py:221
  51.7 9.0 %collective-permute-start.24 = (bf16[72,1536]{1,0:T(8,128)(2,1)S(1)}, bf16[72,1536]{1,0:T(8,128)(2,1)S(1)}, u32[]{:S(2)}, u32[]{:S(2)}) collective-permute-start(bf16[72,1536]{1,0:T(8,128)(2,1)S(1)} %get-tuple-element.65), channel_id=1, source_target_pairs={{0,1},{3,2},{1,0},{2,3},{4,5},{7,6},{5,4},{6,7},{8,9},{11,10},{9,8... | collective-permute-start | bytes 663560 | tf_op jit(solution)/shard_map/ppermute | solution.py:221
  54.5 8.6 %collective-permute-start.8 = (bf16[72,1536]{1,0:T(8,128)(2,1)S(1)}, bf16[72,1536]{1,0:T(8,128)(2,1)S(1)}, u32[]{:S(2)}, u32[]{:S(2)}) collective-permute-start(bf16[72,1536]{1,0:T(8,128)(2,1)S(1)} %get-tuple-element.49), channel_id=1, source_target_pairs={{0,1},{3,2},{1,0},{2,3},{4,5},{7,6},{5,4},{6,7},{8,9},{11,10},{9,8... | collective-permute-start | bytes 663560 | tf_op jit(solution)/shard_map/ppermute | solution.py:221
  57.3 10.2 %collective-permute-start.21 = (bf16[72,1536]{1,0:T(8,128)(2,1)S(1)}, bf16[72,1536]{1,0:T(8,128)(2,1)S(1)}, u32[]{:S(2)}, u32[]{:S(2)}) collective-permute-start(bf16[72,1536]{1,0:T(8,128)(2,1)S(1)} %get-tuple-element.62.s_ref), channel_id=1, source_target_pairs={{1,2},{2,1},{5,6},{6,5},{9,10},{10,9},{13,14},{14,13},{17,18},{18,... | collective-permute-start | bytes 663560 | tf_op jit(solution)/shard_map/ppermute | solution.py:233
  60.8 8.1 %collective-permute-start.25 = (bf16[72,1536]{1,0:T(8,128)(2,1)S(1)}, bf16[72,1536]{1,0:T(8,128)(2,1)S(1)}, u32[]{:S(2)}, u32[]{:S(2)}) collective-permute-start(bf16[72,1536]{1,0:T(8,128)(2,1)S(1)} %get-tuple-element.67.s_ref), channel_id=1, source_target_pairs={{1,2},{2,1},{5,6},{6,5},{9,10},{10,9},{13,14},{14,13},{17,18},{18,... | collective-permute-start | bytes 663560 | tf_op jit(solution)/shard_map/ppermute | solution.py:233
  63.2 7.1 %collective-permute-start.9 = (bf16[72,1536]{1,0:T(8,128)(2,1)S(1)}, bf16[72,1536]{1,0:T(8,128)(2,1)S(1)}, u32[]{:S(2)}, u32[]{:S(2)}) collective-permute-start(bf16[72,1536]{1,0:T(8,128)(2,1)S(1)} %get-tuple-element.51.s_ref), channel_id=1, source_target_pairs={{1,2},{2,1},{5,6},{6,5},{9,10},{10,9},{13,14},{14,13},{17,18},{18,... | collective-permute-start | bytes 663560 | tf_op jit(solution)/shard_map/ppermute | solution.py:233
  64.6 18.2 %collective-permute-start.28 = (bf16[144,896]{1,0:T(8,128)(2,1)S(1)}, bf16[144,896]{1,0:T(8,128)(2,1)S(1)}, u32[]{:S(2)}, u32[]{:S(2)}) collective-permute-start(bf16[144,896]{1,0:T(8,128)(2,1)S(1)} %shard_map.133), channel_id=1, source_target_pairs={{0,4},{4,0},{1,5},{5,1},{2,6},{6,2},{3,7},{7,3},{8,12},{12,8},{9,1... | collective-permute-start | bytes 774152 | tf_op jit(solution)/shard_map/ppermute | solution.py:185
  66.2 17.3 %collective-permute-start.16 = (bf16[144,896]{1,0:T(8,128)(2,1)S(1)}, bf16[144,896]{1,0:T(8,128)(2,1)S(1)}, u32[]{:S(2)}, u32[]{:S(2)}) collective-permute-start(bf16[144,896]{1,0:T(8,128)(2,1)S(1)} %shard_map.119), channel_id=1, source_target_pairs={{0,4},{4,0},{1,5},{5,1},{2,6},{6,2},{3,7},{7,3},{8,12},{12,8},{9,1... | collective-permute-start | bytes 774152 | tf_op jit(solution)/shard_map/ppermute | solution.py:185
  67.6 12.1 %collective-permute-start.22 = (bf16[72,1536]{1,0:T(8,128)(2,1)S(1)}, bf16[72,1536]{1,0:T(8,128)(2,1)S(1)}, u32[]{:S(2)}, u32[]{:S(2)}) collective-permute-start(bf16[72,1536]{1,0:T(8,128)(2,1)S(1)} %shard_map.125.refs_1_), channel_id=1, source_target_pairs={{1,0},{2,3},{5,4},{6,7},{9,8},{10,11},{13,12},{14,15},{17,16},{18,... | collective-permute-start | bytes 663560 | tf_op jit(solution)/shard_map/ppermute | solution.py:221
  69.0 13.0 %collective-permute-start.26 = (bf16[72,1536]{1,0:T(8,128)(2,1)S(1)}, bf16[72,1536]{1,0:T(8,128)(2,1)S(1)}, u32[]{:S(2)}, u32[]{:S(2)}) collective-permute-start(bf16[72,1536]{1,0:T(8,128)(2,1)S(1)} %shard_map.129.refs_1_), channel_id=1, source_target_pairs={{1,0},{2,3},{5,4},{6,7},{9,8},{10,11},{13,12},{14,15},{17,16},{18,... | collective-permute-start | bytes 663560 | tf_op jit(solution)/shard_map/ppermute | solution.py:221
  70.4 16.3 %collective-permute-start.10 = (bf16[72,1536]{1,0:T(8,128)(2,1)S(1)}, bf16[72,1536]{1,0:T(8,128)(2,1)S(1)}, u32[]{:S(2)}, u32[]{:S(2)}) collective-permute-start(bf16[72,1536]{1,0:T(8,128)(2,1)S(1)} %shard_map.111.refs_1_), channel_id=1, source_target_pairs={{1,0},{2,3},{5,4},{6,7},{9,8},{10,11},{13,12},{14,15},{17,16},{18,... | collective-permute-start | bytes 663560 | tf_op jit(solution)/shard_map/ppermute | solution.py:221
  82.8 6.6 %collective-permute-start.30 = (bf16[72,896]{1,0:T(8,128)(2,1)S(1)}, bf16[72,896]{1,0:T(8,128)(2,1)S(1)}, u32[]{:S(2)}, u32[]{:S(2)}) collective-permute-start(bf16[72,896]{1,0:T(8,128)(2,1)S(1)} %shard_map.135), channel_id=1, source_target_pairs={{0,24},{8,16},{16,8},{24,0},{1,25},{9,17},{17,9},{25,1},{2,26},{10... | collective-permute-start | bytes 387080 | tf_op jit(solution)/shard_map/ppermute | solution.py:185
  83.0 6.5 %collective-permute-start.29 = (bf16[72,896]{1,0:T(8,128)(2,1)S(1)}, bf16[72,896]{1,0:T(8,128)(2,1)S(1)}, u32[]{:S(2)}, u32[]{:S(2)}) collective-permute-start(bf16[72,896]{1,0:T(8,128)(2,1)S(1)} %shard_map.134), channel_id=1, source_target_pairs={{0,16},{8,24},{16,0},{24,8},{1,17},{9,25},{17,1},{25,9},{2,18},{10... | collective-permute-start | bytes 387080 | tf_op jit(solution)/shard_map/ppermute | solution.py:185
  83.6 5.9 %collective-permute-start.27 = (bf16[72,896]{1,0:T(8,128)(2,1)S(1)}, bf16[72,896]{1,0:T(8,128)(2,1)S(1)}, u32[]{:S(2)}, u32[]{:S(2)}) collective-permute-start(bf16[72,896]{1,0:T(8,128)(2,1)S(1)} %shard_map.132), channel_id=1, source_target_pairs={{0,8},{8,0},{16,24},{24,16},{1,9},{9,1},{17,25},{25,17},{2,10},{10... | collective-permute-start | bytes 387080 | tf_op jit(solution)/shard_map/ppermute | solution.py:185
  87.4 2.1 %copy-start.3 = (f32[192]{0:T(256)S(1)}, f32[192]{0:T(256)}, u32[]{:S(2)}) copy-start(f32[192]{0:T(256)} %param.9) | copy-start | bytes 2308
